TPU v7x, 32 devices: a whole 2x2x4 slice. The times are simulated.
32 devices in a mesh: tm: 8 (over y, x, core), row: 4 (over z).
Axes of the slice: x: 2, y: 2, z: 4, core: 2. Of those that a mesh axis runs over, the one named last changes fastest.
Arguments:
- observations: float32 [64, 128], P('tm'), may hold values from -6 to 6
- sites: int32 [64, 128], P('tm'), may hold values from 0 to 255
- pattern: int32 [64, 8, 3], P('tm'), may hold values from 0 to 7, as said below
- block_values: float32 [64, 8, 3, 128, 128], P('tm', 'row')
- gains: float32 [64, 1024, 128], P('tm', 'row'), may hold values from -0.03 to 0.73
- variances: float32 [64, 128], P('tm'), may hold values from 0.5 to 2
- monotone_bend_strength: float32 [1], replicated, may hold values from 0.2 to 0.9
- initial_mean: float32 [1024], P('row'), may hold values from -6 to 6
Outputs:
- filtered: float32 [64, 1024], P('tm', 'row')
- evidence: float32 [1], replicated
Inputs may be any that keep to these rules, and one draw needn't show every extreme that they name: `pattern`: block row r lists r itself first, then two other distinct blocks.
All inputs are finite; a program needn't handle non-finite values.
Results may differ from a plain program's by a relative error of at most 0.0003.
Values sent between devices are 32-bit elements; how exact they have to be, the bound alone decides.
No kernel may reach another device: no remote copies, remote signals or barrier semaphores. Data moves between devices by JAX's collectives and lax.ppermute only.
A program may use at most 128 MiB of HBM per device.

v0:
```python
import math

import jax
import jax.numpy as jnp
from jax import lax
from jax.sharding import PartitionSpec as P

ORDER = 4
OBS = 128
STEPS_DEV = 8


def shifted(shard, axis, by):
    count = lax.axis_size(axis)
    pairs = [(i, i + by) for i in range(count) if 0 <= i + by < count]
    return lax.ppermute(shard, axis, pairs)


def forward_sweep(start, values_all, pattern, gains_all, warped_targets, sites, variances):

    def advance(current, inputs):
        entry_values, columns, gain_cols, targets, places, spreads = inputs
        blocks = current.reshape(columns.shape[0], -1)
        predicted = jnp.einsum(
            "rjab,rjb->ra", entry_values, blocks[columns], precision=lax.Precision.HIGHEST
        ).reshape(-1)
        innovation = targets - predicted[ORDER * places]
        current = predicted + jnp.dot(gain_cols, innovation, precision=lax.Precision.HIGHEST)
        step_term = jnp.sum(-0.5 * innovation * innovation / spreads - 0.5 * jnp.log(spreads))
        return (current, (current, step_term))

    return lax.scan(
        advance, start, (values_all, pattern, gains_all, warped_targets, sites, variances)
    )


def compose_rows(own_rows, values_all, pattern, gains_all, sites):
    width = gains_all.shape[1]
    nblocks = pattern.shape[1]

    def back_step(rows_map, inputs):
        entry_values, columns, gain_cols, places = inputs
        selector = (ORDER * places[:, None] == jnp.arange(width, dtype=jnp.int32)[None, :]).astype(
            jnp.float32
        )
        through_gain = jnp.dot(rows_map, gain_cols, precision=lax.Precision.HIGHEST)
        reduced = rows_map - jnp.dot(through_gain, selector, precision=lax.Precision.HIGHEST)
        shaped = reduced.reshape(reduced.shape[0], nblocks, -1)
        products = jnp.einsum(
            "xra,rjab->xrjb", shaped, entry_values, precision=lax.Precision.HIGHEST
        )
        placement = (
            columns[:, :, None] == jnp.arange(nblocks, dtype=jnp.int32)[None, None, :]
        ).astype(jnp.float32)
        moved = jnp.einsum("xrjb,rjc->xcb", products, placement, precision=lax.Precision.HIGHEST)
        return (moved.reshape(reduced.shape[0], width), None)

    rows_map, unused = lax.scan(
        back_step, own_rows, (values_all, pattern, gains_all, sites), reverse=True
    )
    return rows_map


def on_device(
    observations,
    sites,
    pattern,
    block_values,
    gains,
    variances,
    monotone_bend_strength,
    initial_mean,
):
    scale_value = monotone_bend_strength[0]
    bent = jnp.tanh(observations)
    warped_targets = observations + scale_value * bent
    log_jacobian = jnp.log(1.0 + scale_value * (1.0 - bent * bent))
    values_all, gains_all = (
        lax.all_gather(block_values, "row", axis=1, tiled=True),
        lax.all_gather(gains, "row", axis=1, tiled=True),
    )
    start_whole = lax.all_gather(initial_mean, "row", axis=0, tiled=True)
    width = gains_all.shape[1]
    slab = initial_mean.shape[0]
    row_start = lax.axis_index("row") * slab
    is_first = lax.axis_index("tm") == 0
    segment_end = None
    row_ids = row_start + jnp.arange(slab, dtype=jnp.int32)
    own_rows = (row_ids[:, None] == jnp.arange(width, dtype=jnp.int32)[None, :]).astype(jnp.float32)
    rows_map = compose_rows(own_rows, values_all, pattern, gains_all, sites)
    zero_end, unused_zero = forward_sweep(
        jnp.zeros((width,), jnp.float32),
        values_all,
        pattern,
        gains_all,
        warped_targets,
        sites,
        variances,
    )
    true_end, spare_flag = forward_sweep(
        start_whole, values_all, pattern, gains_all, warped_targets, sites, variances
    )
    offset = jnp.where(
        is_first,
        lax.dynamic_slice_in_dim(true_end, row_start, slab, 0),
        lax.dynamic_slice_in_dim(zero_end, row_start, slab, 0),
    )
    rows_map = jnp.where(is_first, jnp.zeros_like(rows_map), rows_map)
    distance = 1
    while distance < lax.axis_size("tm"):
        arrived_map, arrived_offset = shifted((rows_map, offset), "tm", distance)
        whole_map, whole_offset = (
            lax.all_gather(arrived_map, "row", axis=0, tiled=True),
            lax.all_gather(arrived_offset, "row", axis=0, tiled=True),
        )
        joined_map = jnp.dot(rows_map, whole_map, precision=lax.Precision.HIGHEST)
        joined_offset = jnp.dot(rows_map, whole_offset, precision=lax.Precision.HIGHEST) + offset
        combine_here = lax.axis_index("tm") >= distance
        rows_map = jnp.where(combine_here, joined_map, rows_map)
        offset = jnp.where(combine_here, joined_offset, offset)
        distance = distance * 2
    segment_end = offset
    arrived_end = shifted(offset, "tm", 1)
    start_slab = jnp.where(is_first, initial_mean, arrived_end)
    start_mean = lax.all_gather(start_slab, "row", axis=0, tiled=True)
    final_mean, outputs = forward_sweep(
        start_mean, values_all, pattern, gains_all, warped_targets, sites, variances
    )
    means_all, step_terms = outputs
    filtered = lax.dynamic_slice_in_dim(means_all, row_start, slab, 1)
    filtered = jnp.concatenate([filtered[:-1], segment_end[None, :]], axis=0)
    count = STEPS_DEV * OBS
    segment_total = (
        jnp.sum(step_terms) + jnp.sum(log_jacobian) - 0.5 * math.log(2.0 * math.pi) * count
    )
    total = lax.psum(segment_total, "tm")
    evidence = (total / (count * lax.axis_size("tm"))).reshape(1)
    return (filtered, evidence)


def solution(mesh):
    in_specs = (
        P("tm", None),
        P("tm", None),
        P("tm", None, None),
        P("tm", "row", None, None, None),
        P("tm", "row", None),
        P("tm", None),
        P(),
        P("row"),
    )
    out_specs = (P("tm", "row"), P())
    return jax.shard_map(
        on_device, mesh=mesh, in_specs=in_specs, out_specs=out_specs, check_vma=False
    )
```

profile of v0, /device:TPU:0, one launch (start us, length us, event | category | flops | bytes accessed | tf_op | source)
XLA Modules:
  0.0 781.9 jit_solution(16835293867382728782)
XLA Ops:
  8.9 84.2 %all-gather.12.cloned.1.call-done = f32[8,1024,128]{2,1,0:T(8,128)} async-done(((f32[8,256,128]{2,1,0:T(8,128)}), f32[8,1024,128]{2,1,0:T(8,128)}) %all-gather.12.cloned.1.call-update) | async-done | bytes 4194320 | tf_op jit(solution)/shard_map/all_gather | solution.py:80
  93.1 218.3 %all-gather.10.cloned.1.call-done = f32[8,8,3,128,128]{4,3,2,1,0:T(8,128)} async-done(((f32[8,2,3,128,128]{4,3,2,1,0:T(8,128)}), f32[8,8,3,128,128]{4,3,2,1,0:T(8,128)}) %all-gather.10.cloned.1.call-update) | async-done | bytes 12582928 | tf_op jit(solution)/shard_map/all_gather | solution.py:79
  311.4 102.1 %while.49 = (s32[]{:T(128)}, f32[256,1024]{1,0:T(8,128)S(1)}, s32[8,8,3]{1,0,2:T(8,128)S(1)}, f32[8,8,3,128,128]{4,3,2,1,0:T(8,128)}, f32[8,1024,128]{2,1,0:T(8,...) while((s32[]{:T(128)}, f32[256,1024]{1,0:T(8,128)S(1)}, s32[8,8,3]{1,0,2:T(8,128)S(1)}, ...), condition=%wide.region_1.2_spmd, body=%wide.region_0.1_spmd.sunk | while | flops 2089156864 | bytes 24381528 | solution.py:58
  314.4 4.1 convolution_bitcast_fusion.2
  327.2 4.1 convolution_bitcast_fusion.2
  340.0 4.1 convolution_bitcast_fusion.2
  352.7 4.1 convolution_bitcast_fusion.2
  365.5 4.1 convolution_bitcast_fusion.2
  378.3 4.1 convolution_bitcast_fusion.2
  391.0 4.1 convolution_bitcast_fusion.2
  403.8 4.1 convolution_bitcast_fusion.2
  419.7 7.8 %all-gather = f32[4,1,256]{2,1,0:T(1,128)S(1)} all-gather(f32[1,1,256]{2,1,0:T(1,128)S(1)} %bitcast.322), channel_id=1, replica_groups=mesh['tm'=8,'row'=4] {'row'}, dimensions={0}, use_global_device_ids=true | all-gather | bytes 5120 | tf_op jit(solution)/shard_map/all_gather | solution.py:82
  428.1 81.8 %all-gather.14.cloned.1.call-done = f32[1024,1024]{1,0:T(8,128)} async-done(((f32[256,1024]{1,0:T(8,128)}), f32[1024,1024]{1,0:T(8,128)}) %all-gather.14.cloned.1.call-update) | async-done | bytes 4194320 | tf_op jit(solution)/shard_map/all_gather | solution.py:113
  509.9 5.8 convolution_select_fusion.1
  515.7 3.7 collective-permute-start.1
  519.4 52.6 %while.52 = (s32[]{:T(128)}, f32[1024]{0:T(1024)S(1)}, f32[8,8,3,128,128]{4,3,2,1,0:T(8,128)}, s32[8,8,3]{1,0,2:T(8,128)S(1)}, f32[8,1024,128]{2,1,0:T(8,128)}, ...) while((s32[]{:T(128)}, f32[1024]{0:T(1024)S(1)}, ...), condition=%wide.region_5.6_spmd.clone, body=%wide.region_4.5_spmd.clone.sunk | while | flops 6296267 | bytes 2176891 | solution.py:32
  573.0 52.7 %while.50 = (s32[]{:T(128)}, f32[1024]{0:T(1024)S(1)}, f32[8,8,3,128,128]{4,3,2,1,0:T(8,128)}, s32[8,8,3]{1,0,2:T(8,128)S(1)}, f32[8,1024,128]{2,1,0:T(8,128)}, ...) while((s32[]{:T(128)}, f32[1024]{0:T(1024)S(1)}, f32[8,8,3,128,128]{4,3,2,1,0:T(8,128)}, ...), condition=%wide.region_3.4_spmd, body=%wide.region_2.3_spmd.sunk | while | flops 6295242 | bytes 2168681 | solution.py:32
  573.8 3.2 fusion.130
  580.4 3.3 fusion.130
  587.1 3.2 fusion.130
  606.8 3.2 fusion.130
  613.4 3.2 fusion.130
  619.9 3.2 fusion.130
  628.1 8.7 %all-gather.1 = f32[4,1,256]{2,1,0:T(1,128)S(1)} all-gather(f32[1,1,256]{2,1,0:T(1,128)S(1)} %bitcast.327), channel_id=1, replica_groups=mesh['tm'=8,'row'=4] {'row'}, dimensions={0}, use_global_device_ids=true | all-gather | bytes 5120 | tf_op jit(solution)/shard_map/all_gather | solution.py:114
  637.7 5.7 collective-permute-start.3
  644.7 9.0 %all-gather.2 = f32[4,1,256]{2,1,0:T(1,128)S(1)} all-gather(f32[1,1,256]{2,1,0:T(1,128)S(1)} %bitcast.326), channel_id=1, replica_groups=mesh['tm'=8,'row'=4] {'row'}, dimensions={0}, use_global_device_ids=true | all-gather | bytes 5120 | tf_op jit(solution)/shard_map/all_gather | solution.py:114
  654.7 5.8 collective-permute-start.4
  661.7 8.5 %all-gather.3 = f32[4,1,256]{2,1,0:T(1,128)S(1)} all-gather(f32[1,1,256]{2,1,0:T(1,128)S(1)} %bitcast.325), channel_id=1, replica_groups=mesh['tm'=8,'row'=4] {'row'}, dimensions={0}, use_global_device_ids=true | all-gather | bytes 5120 | tf_op jit(solution)/shard_map/all_gather | solution.py:114
  670.2 5.8 convolution_select_fusion
  679.0 8.6 %all-gather.4 = f32[4,1,256]{2,1,0:T(1,128)S(1)} all-gather(f32[1,1,256]{2,1,0:T(1,128)S(1)} %bitcast.324), channel_id=1, replica_groups=mesh['tm'=8,'row'=4] {'row'}, dimensions={0}, use_global_device_ids=true | all-gather | bytes 5120 | tf_op jit(solution)/shard_map/all_gather | solution.py:125
  687.7 69.8 %while.51 = (s32[]{:T(128)}, f32[1024]{0:T(1024)S(1)}, f32[8,1024]{1,0:T(8,128)S(1)}, f32[8]{0:T(128)S(1)}, f32[8,8,3,128,128]{4,3,2,1,0:T(8,128)}, /*index=5*/s...) while((s32[]{:T(128)}, f32[1024]{0:T(1024)S(1)}, ...), condition=%wide.region_8.9_spmd, body=%wide.region_6.8_spmd.sunk | while | flops 6296137 | bytes 2178465 | solution.py:32
  759.4 13.6 %psum.7 = f32[]{:T(128)} all-reduce(f32[]{:T(128)S(6)} %sub.46), channel_id=1, replica_groups=mesh['tm'=8,'row'=4] {'tm'}, use_global_device_ids=true, to_apply=%region_11.12 | all-reduce | flops 1 | bytes 8 | tf_op jit(solution)/shard_map/psum | solution.py:136
  (410 shorter events, 243.4 us)
Async XLA Ops:
  7.2 304.3 %copy-start.2 = (s32[8,8,3]{1,0,2:T(8,128)S(1)}, s32[8,8,3]{1,0,2:T(8,128)}, u32[]{:S(2)}) copy-start(s32[8,8,3]{1,0,2:T(8,128)} %param.18) | copy-start | bytes 2308
  7.2 304.3 %copy-start.5 = (s32[8,128]{1,0:T(8,128)S(1)}, s32[8,128]{1,0:T(8,128)}, u32[]{:S(2)}) copy-start(s32[8,128]{1,0:T(8,128)} %param.17) | copy-start | bytes 12292
  7.2 85.9 %all-gather.12.cloned.1.call-start = ((), (), s32[]{:S(2)}) async-start(), calls=%async_computation.1 | async-start | bytes 5242880 | tf_op jit(solution)/shard_map/all_gather | solution.py:80
  7.9 303.5 %all-gather.10.cloned.1.call-start = ((), (), s32[]{:S(2)}) async-start(), calls=%async_computation | async-start | bytes 15728640 | tf_op jit(solution)/shard_map/all_gather | solution.py:79
  8.7 501.3 %all-gather.14.cloned.1.call-start = ((), (), s32[]{:S(2)}) async-start(), calls=%async_computation.2 | async-start | bytes 5242880 | tf_op jit(solution)/shard_map/all_gather | solution.py:113
  311.4 108.2 %copy-start.3 = (f32[256]{0:T(256)S(1)}, f32[256]{0:T(256)}, u32[]{:S(2)}) copy-start(f32[256]{0:T(256)} %param.23) | copy-start | bytes 3076
  311.4 116.1 %copy-start.4 = (f32[8,128]{1,0:T(8,128)S(1)}, f32[8,128]{1,0:T(8,128)}, u32[]{:S(2)}) copy-start(f32[8,128]{1,0:T(8,128)} %param.16) | copy-start | bytes 12292
  413.7 4.2 collective-permute-start
  417.9 1.0 copy-start.1
  418.9 251.3 %all-gather.16.cloned.1.call-start = ((), (), s32[]{:S(2)}) async-start(), calls=%async_computation.3 | async-start | bytes 5242880 | tf_op jit(solution)/shard_map/all_gather | solution.py:113
  515.7 56.3 %collective-permute-start.1 = (f32[256,1024]{1,0:T(8,128)S(1)}, f32[256,1024]{1,0:T(8,128)S(1)}, u32[]{:S(2)}, u32[]{:S(2)}) collective-permute-start(f32[256,1024]{1,0:T(8,128)S(1)} %convolution_select_fusion.1), channel_id=1, source_target_pairs={{0,8},{4,12},{8,16},{12,20},{16,24},{20,28},{1,9},{5,13},{9,17},{1... | collective-permute-start | bytes 3145736 | tf_op jit(solution)/shard_map/ppermute | solution.py:16
  572.0 1.0 copy-start
  625.8 2.3 collective-permute-start.2
  637.7 7.0 collective-permute-start.3
  654.7 7.1 collective-permute-start.4
  676.9 2.1 collective-permute-start.5
Sparse Core Ops, SparseCore 0:
  9.6 83.4 all-gather.11
  94.7 216.7 all-gather.9
  419.1 90.8 all-gather.13
  573.1 78.3 all-gather.15
where the time goes:
time: 787 us; the launch traced here: 782 us
  waiting for transfers between devices  392 us (50%)
  matrix products  208 us (26%)
  local copies, waits for them, and re-layouts  71.9 us (9%)
  blocking collectives  56.2 us (7%)
  starting transfers between devices  20.1 us (3%)
  between operations  17.7 us (2%)
  other arithmetic  14 us (2%)
    all_gather x1, waiting for transfers between devices, on_device(): lax.all_gather(block_values, 'row', axis=1, tiled=True)  218 us
    all_gather x1, waiting for transfers between devices, on_device(): lax.all_gather(gains, 'row', axis=1, tiled=True)  84.2 us
    all_gather x2, waiting for transfers between devices, on_device(): lax.all_gather(arrived_map, 'row', axis=0, tiled=True)  81.8 us
    dot_general x24, matrix products, advance(): jnp.einsum('rjab,rjb->ra', entry_values, blocks[columns], precision=lax.P...  76.3 us
    dot_general x24, matrix products, advance(): jnp.dot(gain_cols, innovation, precision=lax.Precision.HIGHEST)  38.2 us
    dot_general x8, matrix products, back_step(): jnp.einsum('xra,rjab->xrjb', shaped, entry_values, precision=lax.Precisio...  32.7 us
    all_gather x3, blocking collectives, on_device(): lax.all_gather(arrived_offset, 'row', axis=0, tiled=True)  26.2 us
    dot_general x8, matrix products, back_step(): jnp.einsum('xrjb,rjc->xcb', products, placement, precision=lax.Precision....  24.9 us
  transfers between devices with their start and end apart: 10, of which 8 were waited for; matrix products, arithmetic and copies ran while one was open for 14% of the time, Pallas kernels for 0%

commit v1 on v0

v1 whole, which is shorter than its diff:
```python
import math

import jax
import jax.numpy as jnp
from jax import lax
from jax.experimental import pallas as pl
from jax.experimental.pallas import tpu as pltpu
from jax.sharding import PartitionSpec as P

ORDER = 4
LANES = 128


def lane_sums(block):
    return jnp.sum(block.T, axis=0, keepdims=True)


def segment_kernel(slots, pattern, places, *refs):
    values, gains = refs[:slots], refs[slots : 2 * slots]
    targets, sites, start, filtered, innovations, mean, predicted = refs[2 * slots :]
    steps, held, nonzero = values[0].shape[:3]
    blocks = start.shape[0]
    mean[...] = start[...]

    def step(t, carry):
        for s in range(slots):
            for h in range(held):
                row = held * places[s] + h
                total = None
                for j in range(nonzero):
                    column = pattern[t, row * nonzero + j]
                    part = values[s][t, h, j] * mean[pl.ds(column, 1), :]
                    total = part if total is None else total + part
                predicted[pl.ds(row, 1), :] = lane_sums(total)
        flat = ORDER * sites[pl.ds(t, 1), :]
        lane = jnp.broadcast_to(flat % LANES, (blocks, LANES))
        picked = jnp.take_along_axis(predicted[...], lane, axis=1)
        block = lax.broadcasted_iota(jnp.int32, (blocks, LANES), 0)
        seen = jnp.sum(jnp.where(block == flat // LANES, picked, 0.0), axis=0, keepdims=True)
        innovation = targets[pl.ds(t, 1), :] - seen
        innovations[pl.ds(t, 1), :] = innovation
        for s in range(slots):
            for h in range(held):
                row = held * places[s] + h
                moved = gains[s][t, pl.ds(h * LANES, LANES), :] * innovation
                updated = predicted[pl.ds(row, 1), :] + lane_sums(moved)
                mean[pl.ds(row, 1), :] = updated
                filtered[t, pl.ds(row, 1), :] = updated
        return carry

    lax.fori_loop(0, steps, step, 0)


def run_segment(pattern, places, values, gains, targets, sites, start):
    slots = len(values)
    steps = values[0].shape[0]
    blocks, lanes = start.shape
    vmem = pl.BlockSpec(memory_space=pltpu.VMEM)
    smem = pl.BlockSpec(memory_space=pltpu.SMEM)

    def body(*refs):
        segment_kernel(slots, *refs)

    return pl.pallas_call(
        body,
        in_specs=[smem, smem] + [vmem] * (2 * slots + 3),
        out_specs=[vmem, vmem],
        out_shape=[
            jax.ShapeDtypeStruct((steps, blocks, lanes), jnp.float32),
            jax.ShapeDtypeStruct((steps, lanes), jnp.float32),
        ],
        scratch_shapes=[
            pltpu.VMEM((blocks, lanes), jnp.float32),
            pltpu.VMEM((blocks, lanes), jnp.float32),
        ],
        compiler_params=pltpu.CompilerParams(vmem_limit_bytes=32 << 20),
        name="segment",
    )(pattern, places, *values, *gains, targets, sites, start)


def on_device(
    observations,
    sites,
    pattern,
    block_values,
    gains,
    variances,
    monotone_bend_strength,
    initial_mean,
):
    segments, rows = lax.axis_size("tm"), lax.axis_size("row")
    tm, row = lax.axis_index("tm"), lax.axis_index("row")
    steps, held = block_values.shape[:2]
    blocks = pattern.shape[1]
    even = tm % 2 == 0

    low = (rows - 1) // 2
    order_even = sorted(range(rows), key=lambda z: (abs(z - low), z))
    order_odd = [rows - 1 - z for z in order_even]

    def order(t):
        return order_even if t % 2 == 0 else order_odd

    def flat(t, z):
        return t * rows + z

    both = ("tm", "row")

    def meet(shard):
        moved = [shard]
        for k in range(1, rows):
            pairs = [(flat(t, order(t)[k]), flat(t, order(t)[0])) for t in range(segments)]
            moved.append(lax.ppermute(shard, both, pairs))
        return moved

    starts = meet(initial_mean.reshape(held, LANES))
    all_values = meet(block_values)
    all_gains = meet(gains)
    places = jnp.where(
        even, jnp.array(order_even, jnp.int32), jnp.array(order_odd, jnp.int32)
    )
    by_even = [starts[order_even.index(z)] for z in range(rows)]
    by_odd = [starts[order_odd.index(z)] for z in range(rows)]
    start = jnp.where(even, jnp.concatenate(by_even), jnp.concatenate(by_odd))

    scale = monotone_bend_strength[0]
    bent = jnp.tanh(observations)
    targets = observations + scale * bent
    log_jacobian = jnp.log(1.0 + scale * (1.0 - bent * bent))
    flat_pattern = pattern.reshape(steps, -1)

    for t in range(segments):
        filtered, innovations = run_segment(
            flat_pattern, places, all_values, all_gains, targets, sites, start
        )
        if t + 1 < segments:
            pair = [(flat(t, order(t)[0]), flat(t + 1, order(t + 1)[0]))]
            arrived = lax.ppermute(filtered[steps - 1], both, pair)
            start = jnp.where(tm == t + 1, arrived, start)

    misfit = jnp.sum(innovations * innovations / variances, axis=0, keepdims=True)

    def parcel(z):
        own_rows = lax.dynamic_slice_in_dim(filtered, held * z, held, 1)
        return jnp.concatenate([own_rows.reshape(steps * held, LANES), misfit])

    is_owner = row == places[0]
    received = jnp.where(is_owner, parcel(places[0]), 0.0)
    for k in range(1, rows):
        pairs = [(flat(t, order(t)[0]), flat(t, order(t)[k])) for t in range(segments)]
        received = received + lax.ppermute(parcel(places[k]), both, pairs)
    own_filtered = received[: steps * held].reshape(steps, held * LANES)
    term = (
        -0.5 * jnp.sum(received[steps * held :])
        + jnp.sum(log_jacobian - 0.5 * jnp.log(variances))
        - 0.5 * math.log(2.0 * math.pi) * observations.size
    )
    total = lax.psum(term, "tm")
    evidence = (total / (observations.size * segments)).reshape(1)
    return own_filtered, evidence


def solution(mesh):
    in_specs = (
        P("tm", None),
        P("tm", None),
        P("tm", None, None),
        P("tm", "row", None, None, None),
        P("tm", "row", None),
        P("tm", None),
        P(),
        P("row"),
    )
    out_specs = (P("tm", "row"), P())
    return jax.shard_map(
        on_device, mesh=mesh, in_specs=in_specs, out_specs=out_specs, check_vma=False
    )
```

time: 787 us -> 284 us (0.36)
  waiting for transfers between devices: 392 us -> 108 us
  matrix products: 208 us -> 0 us
  Pallas kernels: 0 us -> 65.5 us
  local copies, waits for them, and re-layouts: 71.9 us -> 42.1 us
  blocking collectives: 56.2 us -> 31.6 us
  other arithmetic: 14 us -> 3.4 us
  between operations: 17.7 us -> 8.05 us
    all_gather x4 -> x0, waiting for transfers between devices: 384 us -> none  [the longest x1 218 us: on_device(): lax.all_gather(block_values, 'row', axis=1, tiled=True)]
    dot_general x85 -> x0, matrix products: 208 us -> none  [the longest x24 76.3 us: advance(): jnp.einsum('rjab,rjb->ra', entry_values, blocks[columns], precision=lax.P...]
    ppermute x6 -> x19, waiting for transfers between devices: 6.34 us -> 108 us  [the longest x9 72.6 us: meet(): moved.append(lax.ppermute(shard, both, pairs))]
    pallas_call x0 -> x8, Pallas kernels: none -> 65.5 us  [run_segment(): pl.pallas_call(body, in_specs=[smem, smem] + [vmem] * (2 * slots + 3), ou...]
    all_gather x5 -> x0, blocking collectives: 42.6 us -> none  [the longest x3 26.2 us: on_device(): lax.all_gather(arrived_offset, 'row', axis=0, tiled=True)]
    unnamed x12 -> x65, local copies, waits for them, and re-layouts: 1.97 us -> 40.8 us
    gather x48 -> x0, local copies, waits for them, and re-layouts: 37 us -> none  [the longest x24 23.3 us: advance(): innovation = targets - predicted[ORDER * places]]
    transpose x8 -> x0, local copies, waits for them, and re-layouts: 18.8 us -> none  [back_step(): jnp.einsum('xra,rjab->xrjb', shaped, entry_values, precision=lax.Precisio...]
  transfers between devices with their start and end apart: 10 -> 19, of which waited for: 8 -> 2; matrix products, arithmetic and copies ran while one was open for 14% -> 1% of each run, Pallas kernels for 0% -> 0%
where the time goes in v1:
time: 284 us; the launch traced here: 283 us
  waiting for transfers between devices  108 us (38%)
  Pallas kernels  65.5 us (23%)
  local copies, waits for them, and re-layouts  42.1 us (15%)
  blocking collectives  31.6 us (11%)
  starting transfers between devices  24.1 us (8%)
  between operations  8.05 us (3%)
  other arithmetic  3.4 us (1%)
    ppermute x9, waiting for transfers between devices, meet(): moved.append(lax.ppermute(shard, both, pairs))  72.6 us
    pallas_call x8, Pallas kernels, run_segment(): pl.pallas_call(body, in_specs=[smem, smem] + [vmem] * (2 * slots + 3), ou...  65.5 us
    unnamed x65, local copies, waits for them, and re-layouts  40.8 us
    ppermute x3, waiting for transfers between devices, on_device(): received = received + lax.ppermute(parcel(places[k]), both, pairs)  35.2 us
    psum x1, blocking collectives, on_device(): total = lax.psum(term, 'tm')  31.6 us
    ppermute x9, starting transfers between devices, meet(): moved.append(lax.ppermute(shard, both, pairs))  17 us
  transfers between devices with their start and end apart: 19, of which 2 were waited for; matrix products, arithmetic and copies ran while one was open for 1% of the time, Pallas kernels for 0%

profile of v1, /device:TPU:0, one launch (start us, length us, event | category | flops | bytes accessed | tf_op | source)
XLA Modules:
  0.0 282.6 jit_solution(1069953198409258024)
XLA Ops:
  0.6 5.1 %collective-permute-start = (f32[8,2,3,128,128]{4,3,2,1,0:T(8,128)}, f32[8,2,3,128,128]{4,3,2,1,0:T(8,128)S(1)}, u32[]{:S(2)}, u32[]{:S(2)}) collective-permute-start(f32[8,2,3,128,128]{4,3,2,1,0:T(8,128)} %refs_2_.15), channel_id=1, source_target_pairs={{0,1},{7,6},{8,9},{15,14},{16,17},{23,22},{24,25},{31,30}} | collective-permute-start | bytes 9437192 | tf_op jit(solution)/shard_map/ppermute | solution.py:113
  5.8 2.3 collective-permute-start.1
  8.1 2.3 collective-permute-start.2
  10.4 1.3 collective-permute-start.3
  11.8 1.3 collective-permute-start.6
  13.1 72.5 %collective-permute-done.6 = f32[2,128]{1,0:T(2,128)S(1)} collective-permute-done((f32[2,128]{1,0:T(2,128)}, f32[2,128]{1,0:T(2,128)S(1)}, u32[]{:S(2)}, u32[]{:S(2)}) %collective-permute-start.6) | collective-permute-done | bytes 1056 | tf_op jit(solution)/shard_map/ppermute | solution.py:113
  86.9 1.6 collective-permute-start.4
  89.6 1.6 collective-permute-start.5
  94.9 1.7 copy-done.2
  96.6 1.9 copy-done
  98.5 1.9 copy-done.3
  100.4 1.2 copy-done.11
  103.6 8.4 %segment.8 = (f32[8,8,128]{2,1,0:T(8,128)S(1)}, f32[8,128]{1,0:T(8,128)}) custom-call(s32[8,24]{1,0:T(8,128)S(1)} %copy.21.refs_0_, s32[4]{0:T(128)S(1)} %broadcast_select_fusion.7.refs_1_, f32[8,2,3,128,128]{4,3,2,1,0:T(8,128)S(1)} %copy-done, f32[8,2,3,128,128]{4,3,2,1,0:T(8,128)S(1)} %copy-done.3, f32[8,2,3,128,128]{4,3,2,1,0:T(8,128)} %collective-permute-done.1.refs_4_, ...), custom_call_target="tpu_custom_call" | custom-call | tf_op jit(solution)/shard_map/segment/pallas_call | solution.py:64
  112.6 1.9 copy-done.4
  114.5 1.2 copy-done.12
  117.0 8.2 %segment.9 = (f32[8,8,128]{2,1,0:T(8,128)S(1)}, f32[8,128]{1,0:T(8,128)}) custom-call(s32[8,24]{1,0:T(8,128)S(1)} %copy.21.refs_0_, s32[4]{0:T(128)S(1)} %broadcast_select_fusion.7.refs_1_, f32[8,2,3,128,128]{4,3,2,1,0:T(8,128)S(1)} %copy-done.1, f32[8,2,3,128,128]{4,3,2,1,0:T(8,128)S(1)} %copy-done.4, ...), custom_call_target="tpu_custom_call" | custom-call | tf_op jit(solution)/shard_map/segment/pallas_call | solution.py:64
  125.9 1.9 copy-done.5
  130.2 8.2 %segment.10 = (f32[8,8,128]{2,1,0:T(8,128)S(1)}, f32[8,128]{1,0:T(8,128)}) custom-call(s32[8,24]{1,0:T(8,128)S(1)} %copy.21.refs_0_, s32[4]{0:T(128)S(1)} %broadcast_select_fusion.7.refs_1_, f32[8,2,3,128,128]{4,3,2,1,0:T(8,128)S(1)} %copy-done.1, f32[8,2,3,128,128]{4,3,2,1,0:T(8,128)S(1)} %copy-done.5, ...), custom_call_target="tpu_custom_call" | custom-call | tf_op jit(solution)/shard_map/segment/pallas_call | solution.py:64
  139.1 1.9 copy-done.6
  143.4 8.2 %segment.11 = (f32[8,8,128]{2,1,0:T(8,128)S(1)}, f32[8,128]{1,0:T(8,128)}) custom-call(s32[8,24]{1,0:T(8,128)S(1)} %copy.21.refs_0_, s32[4]{0:T(128)S(1)} %broadcast_select_fusion.7.refs_1_, f32[8,2,3,128,128]{4,3,2,1,0:T(8,128)S(1)} %copy-done.1, f32[8,2,3,128,128]{4,3,2,1,0:T(8,128)S(1)} %copy-done.6, ...), custom_call_target="tpu_custom_call" | custom-call | tf_op jit(solution)/shard_map/segment/pallas_call | solution.py:64
  152.3 1.9 copy-done.7
  155.5 1.2 copy-done.24
  156.7 8.2 %segment.12 = (f32[8,8,128]{2,1,0:T(8,128)S(1)}, f32[8,128]{1,0:T(8,128)}) custom-call(s32[8,24]{1,0:T(8,128)S(1)} %copy.21.refs_0_, s32[4]{0:T(128)S(1)} %broadcast_select_fusion.7.refs_1_, f32[8,2,3,128,128]{4,3,2,1,0:T(8,128)S(1)} %copy-done.1, f32[8,2,3,128,128]{4,3,2,1,0:T(8,128)S(1)} %copy-done.7, ...), custom_call_target="tpu_custom_call" | custom-call | tf_op jit(solution)/shard_map/segment/pallas_call | solution.py:64
  165.6 1.9 copy-done.8
  169.9 8.2 %segment.13 = (f32[8,8,128]{2,1,0:T(8,128)S(1)}, f32[8,128]{1,0:T(8,128)}) custom-call(s32[8,24]{1,0:T(8,128)S(1)} %copy.21.refs_0_, s32[4]{0:T(128)S(1)} %broadcast_select_fusion.7.refs_1_, f32[8,2,3,128,128]{4,3,2,1,0:T(8,128)S(1)} %copy-done.1, f32[8,2,3,128,128]{4,3,2,1,0:T(8,128)S(1)} %copy-done.8, ...), custom_call_target="tpu_custom_call" | custom-call | tf_op jit(solution)/shard_map/segment/pallas_call | solution.py:64
  178.8 1.9 copy-done.9
  183.2 8.2 %segment.14 = (f32[8,8,128]{2,1,0:T(8,128)S(1)}, f32[8,128]{1,0:T(8,128)}) custom-call(s32[8,24]{1,0:T(8,128)S(1)} %copy.21.refs_0_, s32[4]{0:T(128)S(1)} %broadcast_select_fusion.7.refs_1_, f32[8,2,3,128,128]{4,3,2,1,0:T(8,128)S(1)} %copy-done.1, f32[8,2,3,128,128]{4,3,2,1,0:T(8,128)S(1)} %copy-done.9, ...), custom_call_target="tpu_custom_call" | custom-call | tf_op jit(solution)/shard_map/segment/pallas_call | solution.py:64
  195.3 1.9 copy-done.10
  199.6 7.9 %segment.15 = (f32[8,8,128]{2,1,0:T(8,128)S(1)}, f32[8,128]{1,0:T(8,128)S(1)}) custom-call(s32[8,24]{1,0:T(8,128)S(1)} %copy.21.refs_0_, s32[4]{0:T(128)S(1)} %broadcast_select_fusion.7.refs_1_, f32[8,2,3,128,128]{4,3,2,1,0:T(8,128)S(1)} %copy-done.1, f32[8,2,3,128,128]{4,3,2,1,0:T(8,128)S(1)} %copy-done.10, ...), custom_call_target="tpu_custom_call" | custom-call | tf_op jit(solution)/shard_map/segment/pallas_call | solution.py:64
  208.2 1.3 collective-permute-start.16
  211.5 35.2 %collective-permute-done.16 = f32[17,128]{1,0:T(8,128)S(1)} collective-permute-done((f32[17,128]{1,0:T(8,128)S(1)}, f32[17,128]{1,0:T(8,128)S(1)}, u32[]{:S(2)}, u32[]{:S(2)}) %collective-permute-start.16) | collective-permute-done | bytes 8736 | tf_op jit(solution)/shard_map/ppermute | solution.py:151
  248.6 31.6 %psum.7 = f32[]{:T(128)} all-reduce(f32[]{:T(128)S(6)} %sub.11), channel_id=1, replica_groups=mesh['tm'=8,'row'=4] {'tm'}, use_global_device_ids=true, to_apply=%region_3.4 | all-reduce | flops 1 | bytes 8 | tf_op jit(solution)/shard_map/psum | solution.py:158
  (107 shorter events, 30.5 us)
Async XLA Ops:
  0.6 94.3 %collective-permute-start = (f32[8,2,3,128,128]{4,3,2,1,0:T(8,128)}, f32[8,2,3,128,128]{4,3,2,1,0:T(8,128)S(1)}, u32[]{:S(2)}, u32[]{:S(2)}) collective-permute-start(f32[8,2,3,128,128]{4,3,2,1,0:T(8,128)} %refs_2_.15), channel_id=1, source_target_pairs={{0,1},{7,6},{8,9},{15,14},{16,17},{23,22},{24,25},{31,30}} | collective-permute-start | bytes 9437192 | tf_op jit(solution)/shard_map/ppermute | solution.py:113
  5.8 90.9 %collective-permute-start.1 = (f32[8,2,3,128,128]{4,3,2,1,0:T(8,128)}, f32[8,2,3,128,128]{4,3,2,1,0:T(8,128)}, u32[]{:S(2)}, u32[]{:S(2)}) collective-permute-start(f32[8,2,3,128,128]{4,3,2,1,0:T(8,128)} %refs_2_.15), channel_id=1, source_target_pairs={{2,1},{5,6},{10,9},{13,14},{18,17},{21,22},{26,25},{29,30}} | collective-permute-start | bytes 9437192 | tf_op jit(solution)/shard_map/ppermute | solution.py:113
  8.1 88.6 %collective-permute-start.2 = (f32[8,2,3,128,128]{4,3,2,1,0:T(8,128)}, f32[8,2,3,128,128]{4,3,2,1,0:T(8,128)}, u32[]{:S(2)}, u32[]{:S(2)}) collective-permute-start(f32[8,2,3,128,128]{4,3,2,1,0:T(8,128)} %refs_2_.15), channel_id=1, source_target_pairs={{3,1},{4,6},{11,9},{12,14},{19,17},{20,22},{27,25},{28,30}} | collective-permute-start | bytes 9437192 | tf_op jit(solution)/shard_map/ppermute | solution.py:113
  10.4 78.2 %collective-permute-start.3 = (f32[8,256,128]{2,1,0:T(8,128)}, f32[8,256,128]{2,1,0:T(8,128)S(1)}, u32[]{:S(2)}, u32[]{:S(2)}) collective-permute-start(f32[8,256,128]{2,1,0:T(8,128)} %refs_6_.15), channel_id=1, source_target_pairs={{0,1},{7,6},{8,9},{15,14},{16,17},{23,22},{24,25},{31,30}} | collective-permute-start | bytes 3145736 | tf_op jit(solution)/shard_map/ppermute | solution.py:113
  11.8 73.8 %collective-permute-start.6 = (f32[2,128]{1,0:T(2,128)}, f32[2,128]{1,0:T(2,128)S(1)}, u32[]{:S(2)}, u32[]{:S(2)}) collective-permute-start(f32[2,128]{1,0:T(2,128)} %bitcast.36), channel_id=1, source_target_pairs={{0,1},{7,6},{8,9},{15,14},{16,17},{23,22},{24,25},{31,30}} | collective-permute-start | bytes 3080 | tf_op jit(solution)/shard_map/ppermute | solution.py:113
  85.6 0.7 collective-permute-start.7
  86.3 0.7 collective-permute-start.8
  86.9 7.9 %collective-permute-start.4 = (f32[8,256,128]{2,1,0:T(8,128)}, f32[8,256,128]{2,1,0:T(8,128)}, u32[]{:S(2)}, u32[]{:S(2)}) collective-permute-start(f32[8,256,128]{2,1,0:T(8,128)} %refs_6_.15), channel_id=1, source_target_pairs={{2,1},{5,6},{10,9},{13,14},{18,17},{21,22},{26,25},{29,30}} | collective-permute-start | bytes 3145736 | tf_op jit(solution)/shard_map/ppermute | solution.py:113
  89.6 5.3 %collective-permute-start.5 = (f32[8,256,128]{2,1,0:T(8,128)}, f32[8,256,128]{2,1,0:T(8,128)}, u32[]{:S(2)}, u32[]{:S(2)}) collective-permute-start(f32[8,256,128]{2,1,0:T(8,128)} %refs_6_.15), channel_id=1, source_target_pairs={{3,1},{4,6},{11,9},{12,14},{19,17},{20,22},{27,25},{28,30}} | collective-permute-start | bytes 3145736 | tf_op jit(solution)/shard_map/ppermute | solution.py:113
  94.1 18.5 %copy-start.29 = (s32[8,128]{1,0:T(8,128)S(1)}, s32[8,128]{1,0:T(8,128)}, u32[]{:S(2)}) copy-start(s32[8,128]{1,0:T(8,128)} %refs_11_.15) | copy-start | bytes 12292
  96.6 1.9 copy-start
  98.5 1.9 copy-start.3
  103.6 9.1 %copy-start.1 = (f32[8,2,3,128,128]{4,3,2,1,0:T(8,128)S(1)}, f32[8,2,3,128,128]{4,3,2,1,0:T(8,128)}, u32[]{:S(2)}) copy-start(f32[8,2,3,128,128]{4,3,2,1,0:T(8,128)} %refs_2_.15) | copy-start | bytes 9437188
  111.9 0.7 collective-permute-start.9
  112.6 1.9 copy-start.4
  125.2 0.7 collective-permute-start.10
  125.9 1.9 copy-start.5
  138.4 0.7 collective-permute-start.11
  139.1 1.9 copy-start.6
  151.7 0.7 collective-permute-start.12
  152.3 1.9 copy-start.7
  164.9 0.7 collective-permute-start.13
  165.6 1.9 copy-start.8
  178.1 0.7 collective-permute-start.14
  178.8 1.9 copy-start.9
  191.4 3.9 %collective-permute-start.15 = (f32[8,128]{1,0:T(8,128)S(1)}, f32[8,128]{1,0:T(8,128)S(1)}, u32[]{:S(2)}, u32[]{:S(2)}) collective-permute-start(f32[8,128]{1,0:T(8,128)S(1)} %slice_bitcast_fusion), channel_id=1, source_target_pairs={{25,30}} | collective-permute-start | bytes 12296 | tf_op jit(solution)/shard_map/ppermute | solution.py:138
  195.3 1.9 copy-start.10
  199.6 7.9 %copy-start.30 = (f32[8,128]{1,0:T(8,128)S(1)}, f32[8,128]{1,0:T(8,128)}, u32[]{:S(2)}) copy-start(f32[8,128]{1,0:T(8,128)} %param.10) | copy-start | bytes 12292
  199.6 7.9 %copy-start.31 = (f32[8,128]{1,0:T(8,128)S(1)}, f32[8,128]{1,0:T(8,128)}, u32[]{:S(2)}) copy-start(f32[8,128]{1,0:T(8,128)} %param.15) | copy-start | bytes 12292
  208.2 38.4 %collective-permute-start.16 = (f32[17,128]{1,0:T(8,128)S(1)}, f32[17,128]{1,0:T(8,128)S(1)}, u32[]{:S(2)}, u32[]{:S(2)}) collective-permute-start(f32[17,128]{1,0:T(8,128)S(1)} %get-tuple-element.30), channel_id=1, source_target_pairs={{1,0},{6,7},{9,8},{14,15},{17,16},{22,23},{25,24},{30,31}} | collective-permute-start | bytes 26120 | tf_op jit(solution)/shard_map/ppermute | solution.py:151
  209.5 37.1 %collective-permute-start.17 = (f32[17,128]{1,0:T(8,128)S(1)}, f32[17,128]{1,0:T(8,128)S(1)}, u32[]{:S(2)}, u32[]{:S(2)}) collective-permute-start(f32[17,128]{1,0:T(8,128)S(1)} %get-tuple-element.31), channel_id=1, source_target_pairs={{1,2},{6,5},{9,10},{14,13},{17,18},{22,21},{25,26},{30,29}} | collective-permute-start | bytes 26120 | tf_op jit(solution)/shard_map/ppermute | solution.py:151
  210.2 36.5 %collective-permute-start.18 = (f32[17,128]{1,0:T(8,128)S(1)}, f32[17,128]{1,0:T(8,128)S(1)}, u32[]{:S(2)}, u32[]{:S(2)}) collective-permute-start(f32[17,128]{1,0:T(8,128)S(1)} %get-tuple-element.32), channel_id=1, source_target_pairs={{1,3},{6,4},{9,11},{14,12},{17,19},{22,20},{25,27},{30,28}} | collective-permute-start | bytes 26120 | tf_op jit(solution)/shard_map/ppermute | solution.py:151
  (19 other events, 23.0 us)

commit v2 on v1

--- a/solution.py
+++ b/solution.py
@@ -9,40 +9,205 @@
 
 ORDER = 4
 LANES = 128
+CHUNKS = (4, 2, 1, 1)
+VMEM = pl.BlockSpec(memory_space=pltpu.VMEM)
+HBM = pl.BlockSpec(memory_space=pltpu.HBM)
+SMEM = pl.BlockSpec(memory_space=pltpu.SMEM)
+
+
+def split(x):
+    high = x.astype(jnp.bfloat16)
+    return high, (x - high.astype(jnp.float32)).astype(jnp.bfloat16)
+
+
+def matmul(a, b):
+    return jnp.dot(a, b, preferred_element_type=jnp.float32)
 
 
 def lane_sums(block):
     return jnp.sum(block.T, axis=0, keepdims=True)
 
 
-def segment_kernel(slots, pattern, places, *refs):
-    values, gains = refs[:slots], refs[slots : 2 * slots]
-    targets, sites, start, filtered, innovations, mean, predicted = refs[2 * slots :]
-    steps, held, nonzero = values[0].shape[:3]
+def aligned(row):
+    return pl.ds(pl.multiple_of(row * LANES, LANES), LANES)
+
+
+def compose_kernel(first, last, base, held, nonzero, slots, places, pattern, sites, *refs):
+    packs, refs = refs[:slots], refs[slots:]
+    targets, refs = refs[0], refs[1:]
+    if not first:
+        refs = refs[2:]
+    high, low, refs = refs[0], refs[1], refs[2:]
+    if last:
+        whole, refs = refs[0], refs[1:]
+    through, seen, store, sems = refs
+    width, columns = high.shape
+    steps = packs[0].shape[0]
+    gain_row = held * nonzero * LANES
+
+    def fetch(s, t):
+        return pltpu.make_async_copy(packs[s].at[t], store.at[s, t], sems.at[s, t])
+
+    for t in range(steps):
+        for s in range(slots):
+            fetch(s, t).start()
+    if first:
+        rows = lax.broadcasted_iota(jnp.int32, (width, columns), 0)
+        cols = lax.broadcasted_iota(jnp.int32, (width, columns), 1)
+        high[...] = (rows == cols).astype(jnp.float32).astype(jnp.bfloat16)
+        low[...] = jnp.zeros_like(low)
+
+    def step(t, carry):
+        for s in range(slots):
+            fetch(s, t).wait()
+        for s in range(slots):
+            for h in range(held):
+                row = held * places[s] + h
+                picks = [aligned(pattern[base + t, row * nonzero + j]) for j in range(nonzero)]
+                parts = [
+                    split(store[s, t, pl.ds((h * nonzero + j) * LANES, LANES), :])
+                    for j in range(nonzero)
+                ]
+                up = [p[0] for p in parts]
+                down = [p[1] for p in parts]
+                tops = [high[pick, :] for pick in picks]
+                bottoms = [low[pick, :] for pick in picks]
+                through[aligned(row), :] = matmul(
+                    jnp.concatenate(up + down + up, axis=1),
+                    jnp.concatenate(tops + tops + bottoms),
+                )
+
+        def pick_rows(i, carry):
+            for u in range(32):
+                k = i * 32 + u
+                seen[pl.ds(k, 1), :] = through[pl.ds(ORDER * sites[base + t, k], 1), :]
+            return carry
+
+        lax.fori_loop(0, LANES // 32, pick_rows, 0)
+        target = jnp.broadcast_to(targets[pl.ds(base + t, 1), :], (LANES, LANES)).T
+        lane = lax.broadcasted_iota(jnp.int32, (LANES, LANES), 1)
+        offset = pl.ds(width, LANES)
+        seen[:, offset] = seen[:, offset] - jnp.where(lane == 0, target, 0.0)
+        top, bottom = split(seen[...])
+        halves = [split(store[s, t, pl.ds(gain_row, held * LANES), :]) for s in range(slots)]
+        left = jnp.concatenate([jnp.concatenate([a, b, a], axis=1) for a, b in halves])
+        moved = matmul(left, jnp.concatenate([top, top, bottom]))
+        for s in range(slots):
+            for h in range(held):
+                here = aligned(held * places[s] + h)
+                at = (s * held + h) * LANES
+                new = through[here, :] - moved[at : at + LANES]
+                if last:
+
+                    @pl.when(t == steps - 1)
+                    def _():
+                        whole[here, :] = new
+
+                if not last or steps > 1:
+                    a, b = split(new)
+                    high[here, :] = a
+                    low[here, :] = b
+        return carry
+
+    lax.fori_loop(0, steps, step, 0)
+
+
+def compose(first, last, base, held, nonzero, places, pattern, sites, packs, targets, state):
+    slots = len(packs)
+    steps = packs[0].shape[0]
+    width = slots * held * LANES
+    columns = width + LANES
+    part = jax.ShapeDtypeStruct((width, columns), jnp.bfloat16)
+    out_shape = [part, part]
+    if last:
+        out_shape.append(jax.ShapeDtypeStruct((width, columns), jnp.float32))
+
+    def body(*refs):
+        compose_kernel(first, last, base, held, nonzero, slots, *refs)
+
+    done = pl.pallas_call(
+        body,
+        in_specs=[SMEM] * 3 + [HBM] * slots + [VMEM] * (1 + len(state)),
+        out_specs=[VMEM] * len(out_shape),
+        out_shape=out_shape,
+        scratch_shapes=[
+            pltpu.VMEM((width, columns), jnp.float32),
+            pltpu.VMEM((LANES, columns), jnp.float32),
+            pltpu.VMEM((slots,) + packs[0].shape, jnp.float32),
+            pltpu.SemaphoreType.DMA((slots, steps)),
+        ],
+        cost_estimate=pl.CostEstimate(
+            flops=steps * 2 * width * columns * 3 * (nonzero + 1) * LANES,
+            transcendentals=0,
+            bytes_accessed=4 * slots * packs[0].size,
+        ),
+        input_output_aliases={} if first else {slots + 4: 0, slots + 5: 1},
+        compiler_params=pltpu.CompilerParams(vmem_limit_bytes=36 << 20),
+        name="compose",
+    )(places, pattern, sites, *packs, targets, *state)
+    return done[2] if last else done
+
+
+def hop_kernel(whole, start, end):
     blocks = start.shape[0]
+    for r in range(blocks):
+        rows = pl.ds(r * LANES, LANES)
+        total = whole[rows, pl.ds(blocks * LANES, LANES)]
+        for c in range(blocks):
+            total = total + whole[rows, pl.ds(c * LANES, LANES)] * start[pl.ds(c, 1), :]
+        end[pl.ds(r, 1), :] = lane_sums(total)
+
+
+def hop(whole, start):
+    return pl.pallas_call(
+        hop_kernel,
+        in_specs=[VMEM, VMEM],
+        out_specs=VMEM,
+        out_shape=jax.ShapeDtypeStruct(start.shape, jnp.float32),
+        compiler_params=pltpu.CompilerParams(vmem_limit_bytes=8 << 20),
+        name="hop",
+    )(whole, start)
+
+
+def segment_kernel(held, nonzero, slots, chunks, places, pattern, *refs):
+    packs = [refs[c * slots : (c + 1) * slots] for c in range(chunks)]
+    targets, sites, start, filtered, innovations, mean, predicted = refs[chunks * slots : -2]
+    store, sems = refs[-2:]
+    steps = store.shape[1]
+    blocks = start.shape[0]
+    gain_row = held * nonzero * LANES
+    t = 0
+    for pack in packs:
+        for i in range(pack[0].shape[0]):
+            for s in range(slots):
+                pltpu.make_async_copy(pack[s].at[i], store.at[s, t], sems.at[s, t]).start()
+            t += 1
     mean[...] = start[...]
 
     def step(t, carry):
+        for s in range(slots):
+            pltpu.make_async_copy(packs[0][s].at[0], store.at[s, t], sems.at[s, t]).wait()
         for s in range(slots):
             for h in range(held):
                 row = held * places[s] + h
                 total = None
                 for j in range(nonzero):
                     column = pattern[t, row * nonzero + j]
-                    part = values[s][t, h, j] * mean[pl.ds(column, 1), :]
+                    block = store[s, t, pl.ds((h * nonzero + j) * LANES, LANES), :]
+                    part = block * mean[pl.ds(column, 1), :]
                     total = part if total is None else total + part
                 predicted[pl.ds(row, 1), :] = lane_sums(total)
         flat = ORDER * sites[pl.ds(t, 1), :]
         lane = jnp.broadcast_to(flat % LANES, (blocks, LANES))
         picked = jnp.take_along_axis(predicted[...], lane, axis=1)
         block = lax.broadcasted_iota(jnp.int32, (blocks, LANES), 0)
-        seen = jnp.sum(jnp.where(block == flat // LANES, picked, 0.0), axis=0, keepdims=True)
-        innovation = targets[pl.ds(t, 1), :] - seen
+        picked = jnp.where(block == flat // LANES, picked, 0.0)
+        innovation = targets[pl.ds(t, 1), :] - jnp.sum(picked, axis=0, keepdims=True)
         innovations[pl.ds(t, 1), :] = innovation
         for s in range(slots):
             for h in range(held):
                 row = held * places[s] + h
-                moved = gains[s][t, pl.ds(h * LANES, LANES), :] * innovation
+                moved = store[s, t, pl.ds(gain_row + h * LANES, LANES), :] * innovation
                 updated = predicted[pl.ds(row, 1), :] + lane_sums(moved)
                 mean[pl.ds(row, 1), :] = updated
                 filtered[t, pl.ds(row, 1), :] = updated
@@ -51,20 +216,18 @@
     lax.fori_loop(0, steps, step, 0)
 
 
-def run_segment(pattern, places, values, gains, targets, sites, start):
-    slots = len(values)
-    steps = values[0].shape[0]
+def run_segment(held, nonzero, places, pattern, packs, targets, sites, start):
+    chunks, slots = len(packs), len(packs[0])
+    steps = targets.shape[0]
     blocks, lanes = start.shape
-    vmem = pl.BlockSpec(memory_space=pltpu.VMEM)
-    smem = pl.BlockSpec(memory_space=pltpu.SMEM)
 
     def body(*refs):
-        segment_kernel(slots, *refs)
+        segment_kernel(held, nonzero, slots, chunks, *refs)
 
     return pl.pallas_call(
         body,
-        in_specs=[smem, smem] + [vmem] * (2 * slots + 3),
-        out_specs=[vmem, vmem],
+        in_specs=[SMEM, SMEM] + [HBM] * (chunks * slots) + [VMEM] * 3,
+        out_specs=[VMEM, VMEM],
         out_shape=[
             jax.ShapeDtypeStruct((steps, blocks, lanes), jnp.float32),
             jax.ShapeDtypeStruct((steps, lanes), jnp.float32),
@@ -72,10 +235,12 @@
         scratch_shapes=[
             pltpu.VMEM((blocks, lanes), jnp.float32),
             pltpu.VMEM((blocks, lanes), jnp.float32),
+            pltpu.VMEM((slots, steps) + packs[0][0].shape[1:], jnp.float32),
+            pltpu.SemaphoreType.DMA((slots, steps)),
         ],
-        compiler_params=pltpu.CompilerParams(vmem_limit_bytes=32 << 20),
+        compiler_params=pltpu.CompilerParams(vmem_limit_bytes=60 << 20),
         name="segment",
-    )(pattern, places, *values, *gains, targets, sites, start)
+    )(places, pattern, *[p for pack in packs for p in pack], targets, sites, start)
 
 
 def on_device(
@@ -90,8 +255,7 @@
 ):
     segments, rows = lax.axis_size("tm"), lax.axis_size("row")
     tm, row = lax.axis_index("tm"), lax.axis_index("row")
-    steps, held = block_values.shape[:2]
-    blocks = pattern.shape[1]
+    steps, held, nonzero = block_values.shape[:3]
     even = tm % 2 == 0
 
     low = (rows - 1) // 2
@@ -113,12 +277,10 @@
             moved.append(lax.ppermute(shard, both, pairs))
         return moved
 
-    starts = meet(initial_mean.reshape(held, LANES))
-    all_values = meet(block_values)
-    all_gains = meet(gains)
     places = jnp.where(
         even, jnp.array(order_even, jnp.int32), jnp.array(order_odd, jnp.int32)
     )
+    starts = meet(initial_mean.reshape(held, LANES))
     by_even = [starts[order_even.index(z)] for z in range(rows)]
     by_odd = [starts[order_odd.index(z)] for z in range(rows)]
     start = jnp.where(even, jnp.concatenate(by_even), jnp.concatenate(by_odd))
@@ -129,15 +291,38 @@
     log_jacobian = jnp.log(1.0 + scale * (1.0 - bent * bent))
     flat_pattern = pattern.reshape(steps, -1)
 
-    for t in range(segments):
-        filtered, innovations = run_segment(
-            flat_pattern, places, all_values, all_gains, targets, sites, start
+    sizes = CHUNKS if sum(CHUNKS) == steps else (1,) * steps
+    packs, base = [], 0
+    for size in sizes:
+        blocks = block_values[base : base + size].reshape(size, -1, LANES)
+        packs.append(meet(jnp.concatenate([blocks, gains[base : base + size]], axis=1)))
+        base += size
+
+    state, base = (), 0
+    for i, size in enumerate(sizes):
+        state = compose(
+            i == 0,
+            i == len(sizes) - 1,
+            base,
+            held,
+            nonzero,
+            places,
+            flat_pattern,
+            sites,
+            packs[i],
+            targets,
+            state,
         )
-        if t + 1 < segments:
-            pair = [(flat(t, order(t)[0]), flat(t + 1, order(t + 1)[0]))]
-            arrived = lax.ppermute(filtered[steps - 1], both, pair)
-            start = jnp.where(tm == t + 1, arrived, start)
-
+        base += size
+
+    mean, begin = start, jnp.where(tm == 0, start, 0.0)
+    for t in range(segments - 1):
+        pair = [(flat(t, order(t)[0]), flat(t + 1, order(t + 1)[0]))]
+        mean = lax.ppermute(hop(state, mean), both, pair)
+        begin = begin + mean
+    filtered, innovations = run_segment(
+        held, nonzero, places, flat_pattern, packs, targets, sites, begin
+    )
     misfit = jnp.sum(innovations * innovations / variances, axis=0, keepdims=True)
 
     def parcel(z):

time: 284 us -> 188 us (0.66)
  waiting for transfers between devices: 108 us -> 31.2 us
  local copies, waits for them, and re-layouts: 42.1 us -> 8.48 us
  starting transfers between devices: 24.1 us -> 38.8 us
    ppermute x9 -> x15, waiting for transfers between devices: 72.6 us -> 28.8 us  [meet(): moved.append(lax.ppermute(shard, both, pairs))]
    unnamed x65 -> x47, local copies, waits for them, and re-layouts: 40.8 us -> 0.18 us
    ppermute x3, waiting for transfers between devices: 35.2 us -> 2.41 us  [on_device(): received = received + lax.ppermute(parcel(places[k]), both, pairs)]
    ppermute x9 -> x15, starting transfers between devices: 17 us -> 31.6 us  [meet(): moved.append(lax.ppermute(shard, both, pairs))]
    slice x0 -> x9, local copies, waits for them, and re-layouts: none -> 6.05 us  [the longest x4 4.61 us: on_device(): blocks = block_values[base:base + size].reshape(size, -1, LANES)]
    concatenate x0 -> x4, other arithmetic: none -> 3.02 us  [on_device(): jnp.concatenate([blocks, gains[base:base + size]], axis=1)]
    pallas_call x8 -> x12, Pallas kernels: 65.5 us -> 63.9 us  [the longest x4 53.2 us: compose(): pl.pallas_call(body, in_specs=[SMEM] * 3 + [HBM] * slots + [VMEM] * (1 +...]
  transfers between devices with their start and end apart: 19 -> 25, of which waited for: 2 -> 2; matrix products, arithmetic and copies ran while one was open for 1% -> 4% of each run, Pallas kernels for 0% -> 25%
where the time goes in v2:
time: 188 us; the launch traced here: 187 us
  Pallas kernels  63.9 us (34%)
  starting transfers between devices  38.8 us (21%)
  waiting for transfers between devices  31.2 us (17%)
  blocking collectives  30.5 us (16%)
  local copies, waits for them, and re-layouts  8.48 us (5%)
  between operations  8.18 us (4%)
  other arithmetic  5.57 us (3%)
    pallas_call x4, Pallas kernels, compose(): pl.pallas_call(body, in_specs=[SMEM] * 3 + [HBM] * slots + [VMEM] * (1 +...  53.2 us
    ppermute x15, starting transfers between devices, meet(): moved.append(lax.ppermute(shard, both, pairs))  31.6 us
    psum x1, blocking collectives, on_device(): total = lax.psum(term, 'tm')  30.5 us
    ppermute x15, waiting for transfers between devices, meet(): moved.append(lax.ppermute(shard, both, pairs))  28.8 us
    pallas_call x1, Pallas kernels, run_segment(): pl.pallas_call(body, in_specs=[SMEM, SMEM] + [HBM] * (chunks * slots) + [...  8.07 us
    ppermute x7, starting transfers between devices, on_device(): mean = lax.ppermute(hop(state, mean), both, pair)  4.63 us
    slice x4, local copies, waits for them, and re-layouts, on_device(): blocks = block_values[base:base + size].reshape(size, -1, LANES)  4.61 us
  transfers between devices with their start and end apart: 25, of which 2 were waited for; matrix products, arithmetic and copies ran while one was open for 4% of the time, Pallas kernels for 25%

profile of v2, /device:TPU:0, one launch (start us, length us, event | category | flops | bytes accessed | tf_op | source)
XLA Modules:
  0.0 186.6 jit_solution(13757673988155405078)
XLA Ops:
  0.7 1.4 slice-done
  2.3 6.4 %collective-permute-start = (f32[4,1024,128]{2,1,0:T(8,128)S(1)}, f32[4,1024,128]{2,1,0:T(8,128)}, u32[]{:S(2)}, u32[]{:S(2)}) collective-permute-start(f32[4,1024,128]{2,1,0:T(8,128)S(1)} %pad_maximum_fusion.refs_3_.refs_2_), channel_id=1, source_target_pairs={{0,1},{7,6},{8,9},{15,14},{16,17},{23,22},{24,25},{31,30}} | collective-permute-start | bytes 6291464 | tf_op jit(solution)/shard_map/ppermute | solution.py:277
  8.8 2.0 %collective-permute-start.1 = (f32[4,1024,128]{2,1,0:T(8,128)S(1)}, f32[4,1024,128]{2,1,0:T(8,128)}, u32[]{:S(2)}, u32[]{:S(2)}) collective-permute-start(f32[4,1024,128]{2,1,0:T(8,128)S(1)} %pad_maximum_fusion.refs_3_.refs_2_), channel_id=1, source_target_pairs={{2,1},{5,6},{10,9},{13,14},{18,17},{21,22},{26,25},{29,30}} | collective-permute-start | bytes 6291464 | tf_op jit(solution)/shard_map/ppermute | solution.py:277
  10.8 2.0 %collective-permute-start.2 = (f32[4,1024,128]{2,1,0:T(8,128)S(1)}, f32[4,1024,128]{2,1,0:T(8,128)}, u32[]{:S(2)}, u32[]{:S(2)}) collective-permute-start(f32[4,1024,128]{2,1,0:T(8,128)S(1)} %pad_maximum_fusion.refs_3_.refs_2_), channel_id=1, source_target_pairs={{3,1},{4,6},{11,9},{12,14},{19,17},{20,22},{27,25},{28,30}} | collective-permute-start | bytes 6291464 | tf_op jit(solution)/shard_map/ppermute | solution.py:277
  12.8 1.3 collective-permute-start.12
  14.8 2.1 %slice.46 = f32[2,2,3,128,128]{4,3,2,1,0:T(8,128)} slice(f32[8,2,3,128,128]{4,3,2,1,0:T(8,128)} %param.13), slice={[4:6], [0:2], [0:3], [0:128], [0:128]} | slice | bytes 1572864 | tf_op jit(solution)/shard_map/slice | solution.py:297
  17.5 1.2 pad_maximum_fusion.1.refs_3_.refs_6_
  18.8 1.3 fusion.5
  20.2 1.2 fusion.4
  21.3 0.8 pad_maximum_fusion.2.refs_3_.refs_10_
  22.2 28.7 %collective-permute-done.12 = f32[2,128]{1,0:T(2,128)S(1)} collective-permute-done((f32[2,128]{1,0:T(2,128)S(1)}, f32[2,128]{1,0:T(2,128)S(1)}, u32[]{:S(2)}, u32[]{:S(2)}) %collective-permute-start.12) | collective-permute-done | bytes 1056 | tf_op jit(solution)/shard_map/ppermute | solution.py:277
  51.5 0.8 pad_maximum_fusion.3.refs_3_.refs_14_
  52.6 6.7 %collective-permute-start.3 = (f32[2,1024,128]{2,1,0:T(8,128)S(1)}, f32[2,1024,128]{2,1,0:T(8,128)S(1)}, u32[]{:S(2)}, u32[]{:S(2)}) collective-permute-start(f32[2,1024,128]{2,1,0:T(8,128)S(1)} %pad_maximum_fusion.1.refs_3_.refs_6_), channel_id=1, source_target_pairs={{0,1},{7,6},{8,9},{15,14},{16,17},{23,22},{24,25},{31,30}} | collective-permute-start | bytes 3145736 | tf_op jit(solution)/shard_map/ppermute | solution.py:277
  59.3 0.7 collective-permute-start.4
  60.1 0.9 collective-permute-start.5
  60.9 3.6 %collective-permute-start.6 = (f32[1,1024,128]{2,1,0:T(8,128)}, f32[1,1024,128]{2,1,0:T(8,128)S(1)}, u32[]{:S(2)}, u32[]{:S(2)}) collective-permute-start(f32[1,1024,128]{2,1,0:T(8,128)} %pad_maximum_fusion.2.refs_3_.refs_10_), channel_id=1, source_target_pairs={{0,1},{7,6},{8,9},{15,14},{16,17},{23,22},{24,25},{31,30}} | collective-permute-start | bytes 1572872 | tf_op jit(solution)/shard_map/ppermute | solution.py:277
  64.5 0.7 collective-permute-start.7
  65.3 26.2 %compose.4 = (bf16[1024,1152]{1,0:T(8,128)(2,1)S(1)}, bf16[1024,1152]{1,0:T(8,128)(2,1)S(1)}) custom-call(s32[4]{0:T(128)S(1)} %broadcast_select_fusion.refs_0_, s32[8,24]{1,0:T(8,128)S(1)} %copy.24.refs_1_, s32[8,128]{1,0:T(8,128)S(1)} %copy-done.16, f32[4,1024,128]{2,1,0:T(8,128)S(1)} %pad_maximum_fusion.refs_3_.refs_2_, ...), custom_call_target="tpu_custom_call" | custom-call | flops 14495514624 | bytes 8388608 | tf_op jit(solution)/shard_map/compose/pallas_call | solution.py:128
  91.5 0.7 collective-permute-start.8
  92.2 0.7 collective-permute-start.10
  92.9 0.7 collective-permute-start.11
  93.6 3.9 %collective-permute-start.9 = (f32[1,1024,128]{2,1,0:T(8,128)S(1)}, f32[1,1024,128]{2,1,0:T(8,128)S(1)}, u32[]{:S(2)}, u32[]{:S(2)}) collective-permute-start(f32[1,1024,128]{2,1,0:T(8,128)S(1)} %copy-done.3), channel_id=1, source_target_pairs={{0,1},{7,6},{8,9},{15,14},{16,17},{23,22},{24,25},{31,30}} | collective-permute-start | bytes 1572872 | tf_op jit(solution)/shard_map/ppermute | solution.py:277
  97.5 13.0 %compose.5 = (bf16[1024,1152]{1,0:T(8,128)(2,1)S(1)}, bf16[1024,1152]{1,0:T(8,128)(2,1)S(1)}) custom-call(s32[4]{0:T(128)S(1)} %broadcast_select_fusion.refs_0_, s32[8,24]{1,0:T(8,128)S(1)} %copy.24.refs_1_, s32[8,128]{1,0:T(8,128)S(1)} %copy-done.16, ...), custom_call_target="tpu_custom_call", output_to_operand_aliasing={{0}: (8, {}), {1}: (9, {})} | custom-call | flops 7247757312 | bytes 4194304 | tf_op jit(solution)/shard_map/compose/pallas_call | solution.py:128
  110.7 6.8 %compose.6 = (bf16[1024,1152]{1,0:T(8,128)(2,1)S(1)}, bf16[1024,1152]{1,0:T(8,128)(2,1)S(1)}) custom-call(s32[4]{0:T(128)S(1)} %broadcast_select_fusion.refs_0_, s32[8,24]{1,0:T(8,128)S(1)} %copy.24.refs_1_, s32[8,128]{1,0:T(8,128)S(1)} %copy-done.16, f32[1,1024,128]{2,1,0:T(8,128)S(1)} %copy-done.2, ...), custom_call_target="tpu_custom_call", output_to_operand_aliasing={{0}: (8, {}), {1}: (9, {})} | custom-call | flops 3623878656 | bytes 2097152 | tf_op jit(solution)/shard_map/compose/pallas_call | solution.py:128
  117.6 7.2 %compose.7 = (bf16[1024,1152]{1,0:T(8,128)(2,1)S(1)}, bf16[1024,1152]{1,0:T(8,128)(2,1)S(1)}, f32[1024,1152]{1,0:T(8,128)S(1)}) custom-call(s32[4]{0:T(128)S(1)} %broadcast_select_fusion.refs_0_, s32[8,24]{1,0:T(8,128)S(1)} %copy.24.refs_1_, s32[8,128]{1,0:T(8,128)S(1)} %copy-done.16, ...), custom_call_target="tpu_custom_call", output_to_operand_aliasing={{0}: (8, {}), {1}: (9, {})} | custom-call | flops 3623878656 | bytes 2097152 | tf_op jit(solution)/shard_map/compose/pallas_call | solution.py:128
  135.9 8.1 %segment.1 = (f32[8,8,128]{2,1,0:T(8,128)}, f32[8,128]{1,0:T(8,128)}) custom-call(s32[4]{0:T(128)} %copy-done.13, s32[8,24]{1,0:T(8,128)} %copy-done.15, f32[4,1024,128]{2,1,0:T(8,128)} %copy-done, f32[4,1024,128]{2,1,0:T(8,128)} %collective-permute-done.refs_4_.refs_3_, f32[4,1024,128]{2,1,0:T(8,128)} %collective-permute-done.1.refs_5_.refs_4_, ...), custom_call_target="tpu_custom_call" | custom-call | tf_op jit(solution)/shard_map/segment/pallas_call | solution.py:227
  144.0 1.3 subtract_reduce_fusion
  145.3 0.9 constant_dynamic-slice_fusion.3
  146.2 1.3 collective-permute-start.22
  147.5 0.7 collective-permute-start.23
  149.4 2.4 %collective-permute-done.22 = f32[17,128]{1,0:T(8,128)S(1)} collective-permute-done((f32[17,128]{1,0:T(8,128)S(1)}, f32[17,128]{1,0:T(8,128)S(1)}, u32[]{:S(2)}, u32[]{:S(2)}) %collective-permute-start.22) | collective-permute-done | bytes 8736 | tf_op jit(solution)/shard_map/ppermute | solution.py:336
  153.7 30.5 %psum.7 = f32[]{:T(128)} all-reduce(f32[]{:T(128)S(6)} %sub.11), channel_id=1, replica_groups=mesh['tm'=8,'row'=4] {'tm'}, use_global_device_ids=true, to_apply=%region_3.4 | all-reduce | flops 1 | bytes 8 | tf_op jit(solution)/shard_map/psum | solution.py:343
  (105 shorter events, 12.3 us)
Async XLA Ops:
  2.3 63.0 %copy-start = (f32[4,1024,128]{2,1,0:T(8,128)}, f32[4,1024,128]{2,1,0:T(8,128)S(1)}, u32[]{:S(2)}) copy-start(f32[4,1024,128]{2,1,0:T(8,128)S(1)} %pad_maximum_fusion.refs_3_.refs_2_) | copy-start | bytes 6291460
  2.3 57.7 %collective-permute-start = (f32[4,1024,128]{2,1,0:T(8,128)S(1)}, f32[4,1024,128]{2,1,0:T(8,128)}, u32[]{:S(2)}, u32[]{:S(2)}) collective-permute-start(f32[4,1024,128]{2,1,0:T(8,128)S(1)} %pad_maximum_fusion.refs_3_.refs_2_), channel_id=1, source_target_pairs={{0,1},{7,6},{8,9},{15,14},{16,17},{23,22},{24,25},{31,30}} | collective-permute-start | bytes 6291464 | tf_op jit(solution)/shard_map/ppermute | solution.py:277
  8.8 52.2 %collective-permute-start.1 = (f32[4,1024,128]{2,1,0:T(8,128)S(1)}, f32[4,1024,128]{2,1,0:T(8,128)}, u32[]{:S(2)}, u32[]{:S(2)}) collective-permute-start(f32[4,1024,128]{2,1,0:T(8,128)S(1)} %pad_maximum_fusion.refs_3_.refs_2_), channel_id=1, source_target_pairs={{2,1},{5,6},{10,9},{13,14},{18,17},{21,22},{26,25},{29,30}} | collective-permute-start | bytes 6291464 | tf_op jit(solution)/shard_map/ppermute | solution.py:277
  10.8 53.8 %collective-permute-start.2 = (f32[4,1024,128]{2,1,0:T(8,128)S(1)}, f32[4,1024,128]{2,1,0:T(8,128)}, u32[]{:S(2)}, u32[]{:S(2)}) collective-permute-start(f32[4,1024,128]{2,1,0:T(8,128)S(1)} %pad_maximum_fusion.refs_3_.refs_2_), channel_id=1, source_target_pairs={{3,1},{4,6},{11,9},{12,14},{19,17},{20,22},{27,25},{28,30}} | collective-permute-start | bytes 6291464 | tf_op jit(solution)/shard_map/ppermute | solution.py:277
  12.8 38.1 %collective-permute-start.12 = (f32[2,128]{1,0:T(2,128)S(1)}, f32[2,128]{1,0:T(2,128)S(1)}, u32[]{:S(2)}, u32[]{:S(2)}) collective-permute-start(f32[2,128]{1,0:T(2,128)S(1)} %bitcast.30), channel_id=1, source_target_pairs={{0,1},{7,6},{8,9},{15,14},{16,17},{23,22},{24,25},{31,30}} | collective-permute-start | bytes 3080 | tf_op jit(solution)/shard_map/ppermute | solution.py:277
  14.1 38.4 %collective-permute-start.13 = (f32[2,128]{1,0:T(2,128)S(1)}, f32[2,128]{1,0:T(2,128)S(1)}, u32[]{:S(2)}, u32[]{:S(2)}) collective-permute-start(f32[2,128]{1,0:T(2,128)S(1)} %bitcast.31), channel_id=1, source_target_pairs={{2,1},{5,6},{10,9},{13,14},{18,17},{21,22},{26,25},{29,30}} | collective-permute-start | bytes 3080 | tf_op jit(solution)/shard_map/ppermute | solution.py:277
  18.7 78.8 %copy-start.1 = (f32[2,1024,128]{2,1,0:T(8,128)}, f32[2,1024,128]{2,1,0:T(8,128)S(1)}, u32[]{:S(2)}) copy-start(f32[2,1024,128]{2,1,0:T(8,128)S(1)} %pad_maximum_fusion.1.refs_3_.refs_6_) | copy-start | bytes 3145732
  18.8 33.6 %copy-start.18 = (s32[8,8,3]{1,0,2:T(8,128)S(1)}, s32[8,8,3]{1,0,2:T(8,128)}, u32[]{:S(2)}) copy-start(s32[8,8,3]{1,0,2:T(8,128)} %param.12) | copy-start | bytes 2308
  18.8 46.5 %copy-start.16 = (s32[8,128]{1,0:T(8,128)S(1)}, s32[8,128]{1,0:T(8,128)}, u32[]{:S(2)}) copy-start(s32[8,128]{1,0:T(8,128)} %refs_19_.1) | copy-start | bytes 12292
  18.8 113.4 %copy-start.13 = (s32[4]{0:T(128)}, s32[4]{0:T(128)S(1)}, u32[]{:S(2)}) copy-start(s32[4]{0:T(128)S(1)} %broadcast_select_fusion.refs_0_) | copy-start | bytes 52
  18.8 98.8 %copy-start.14 = (f32[8,128]{1,0:T(8,128)}, f32[8,128]{1,0:T(8,128)S(1)}, u32[]{:S(2)}) copy-start(f32[8,128]{1,0:T(8,128)S(1)} %multiply_add_fusion.refs_7_.refs_18_) | copy-start | bytes 12292
  50.9 8.4 %collective-permute-start.14 = (f32[2,128]{1,0:T(2,128)S(1)}, f32[2,128]{1,0:T(2,128)S(1)}, u32[]{:S(2)}, u32[]{:S(2)}) collective-permute-start(f32[2,128]{1,0:T(2,128)S(1)} %bitcast.32), channel_id=1, source_target_pairs={{3,1},{4,6},{11,9},{12,14},{19,17},{20,22},{27,25},{28,30}} | collective-permute-start | bytes 3080 | tf_op jit(solution)/shard_map/ppermute | solution.py:277
  52.5 65.1 %copy-start.15 = (s32[8,24]{1,0:T(8,128)}, s32[8,24]{1,0:T(8,128)S(1)}, u32[]{:S(2)}) copy-start(s32[8,24]{1,0:T(8,128)S(1)} %copy.24.refs_1_) | copy-start | bytes 2308
  52.6 39.6 %collective-permute-start.3 = (f32[2,1024,128]{2,1,0:T(8,128)S(1)}, f32[2,1024,128]{2,1,0:T(8,128)S(1)}, u32[]{:S(2)}, u32[]{:S(2)}) collective-permute-start(f32[2,1024,128]{2,1,0:T(8,128)S(1)} %pad_maximum_fusion.1.refs_3_.refs_6_), channel_id=1, source_target_pairs={{0,1},{7,6},{8,9},{15,14},{16,17},{23,22},{24,25},{31,30}} | collective-permute-start | bytes 3145736 | tf_op jit(solution)/shard_map/ppermute | solution.py:277
  59.3 33.6 %collective-permute-start.4 = (f32[2,1024,128]{2,1,0:T(8,128)S(1)}, f32[2,1024,128]{2,1,0:T(8,128)S(1)}, u32[]{:S(2)}, u32[]{:S(2)}) collective-permute-start(f32[2,1024,128]{2,1,0:T(8,128)S(1)} %pad_maximum_fusion.1.refs_3_.refs_6_), channel_id=1, source_target_pairs={{2,1},{5,6},{10,9},{13,14},{18,17},{21,22},{26,25},{29,30}} | collective-permute-start | bytes 3145736 | tf_op jit(solution)/shard_map/ppermute | solution.py:277
  60.1 33.6 %collective-permute-start.5 = (f32[2,1024,128]{2,1,0:T(8,128)S(1)}, f32[2,1024,128]{2,1,0:T(8,128)S(1)}, u32[]{:S(2)}, u32[]{:S(2)}) collective-permute-start(f32[2,1024,128]{2,1,0:T(8,128)S(1)} %pad_maximum_fusion.1.refs_3_.refs_6_), channel_id=1, source_target_pairs={{3,1},{4,6},{11,9},{12,14},{19,17},{20,22},{27,25},{28,30}} | collective-permute-start | bytes 3145736 | tf_op jit(solution)/shard_map/ppermute | solution.py:277
  60.9 30.5 %collective-permute-start.6 = (f32[1,1024,128]{2,1,0:T(8,128)}, f32[1,1024,128]{2,1,0:T(8,128)S(1)}, u32[]{:S(2)}, u32[]{:S(2)}) collective-permute-start(f32[1,1024,128]{2,1,0:T(8,128)} %pad_maximum_fusion.2.refs_3_.refs_10_), channel_id=1, source_target_pairs={{0,1},{7,6},{8,9},{15,14},{16,17},{23,22},{24,25},{31,30}} | collective-permute-start | bytes 1572872 | tf_op jit(solution)/shard_map/ppermute | solution.py:277
  64.5 46.1 %collective-permute-start.7 = (f32[1,1024,128]{2,1,0:T(8,128)}, f32[1,1024,128]{2,1,0:T(8,128)S(1)}, u32[]{:S(2)}, u32[]{:S(2)}) collective-permute-start(f32[1,1024,128]{2,1,0:T(8,128)} %pad_maximum_fusion.2.refs_3_.refs_10_), channel_id=1, source_target_pairs={{2,1},{5,6},{10,9},{13,14},{18,17},{21,22},{26,25},{29,30}} | collective-permute-start | bytes 1572872 | tf_op jit(solution)/shard_map/ppermute | solution.py:277
  91.5 19.2 %collective-permute-start.8 = (f32[1,1024,128]{2,1,0:T(8,128)S(1)}, f32[1,1024,128]{2,1,0:T(8,128)S(1)}, u32[]{:S(2)}, u32[]{:S(2)}) collective-permute-start(f32[1,1024,128]{2,1,0:T(8,128)S(1)} %copy-done.2), channel_id=1, source_target_pairs={{3,1},{4,6},{11,9},{12,14},{19,17},{20,22},{27,25},{28,30}} | collective-permute-start | bytes 1572872 | tf_op jit(solution)/shard_map/ppermute | solution.py:277
  92.2 25.3 %collective-permute-start.10 = (f32[1,1024,128]{2,1,0:T(8,128)S(1)}, f32[1,1024,128]{2,1,0:T(8,128)S(1)}, u32[]{:S(2)}, u32[]{:S(2)}) collective-permute-start(f32[1,1024,128]{2,1,0:T(8,128)S(1)} %copy-done.3), channel_id=1, source_target_pairs={{2,1},{5,6},{10,9},{13,14},{18,17},{21,22},{26,25},{29,30}} | collective-permute-start | bytes 1572872 | tf_op jit(solution)/shard_map/ppermute | solution.py:277
  92.9 24.6 %collective-permute-start.11 = (f32[1,1024,128]{2,1,0:T(8,128)S(1)}, f32[1,1024,128]{2,1,0:T(8,128)S(1)}, u32[]{:S(2)}, u32[]{:S(2)}) collective-permute-start(f32[1,1024,128]{2,1,0:T(8,128)S(1)} %copy-done.3), channel_id=1, source_target_pairs={{3,1},{4,6},{11,9},{12,14},{19,17},{20,22},{27,25},{28,30}} | collective-permute-start | bytes 1572872 | tf_op jit(solution)/shard_map/ppermute | solution.py:277
  93.6 23.9 %collective-permute-start.9 = (f32[1,1024,128]{2,1,0:T(8,128)S(1)}, f32[1,1024,128]{2,1,0:T(8,128)S(1)}, u32[]{:S(2)}, u32[]{:S(2)}) collective-permute-start(f32[1,1024,128]{2,1,0:T(8,128)S(1)} %copy-done.3), channel_id=1, source_target_pairs={{0,1},{7,6},{8,9},{15,14},{16,17},{23,22},{24,25},{31,30}} | collective-permute-start | bytes 1572872 | tf_op jit(solution)/shard_map/ppermute | solution.py:277
  125.2 0.7 collective-permute-start.15
  126.2 0.7 collective-permute-start.16
  127.3 0.7 collective-permute-start.17
  128.3 0.7 collective-permute-start.18
  129.4 0.7 collective-permute-start.19
  130.4 0.7 collective-permute-start.20
  131.5 3.8 %collective-permute-start.21 = (f32[8,128]{1,0:T(8,128)S(1)}, f32[8,128]{1,0:T(8,128)S(1)}, u32[]{:S(2)}, u32[]{:S(2)}) collective-permute-start(f32[8,128]{1,0:T(8,128)S(1)} %hop.13), channel_id=1, source_target_pairs={{25,30}} | collective-permute-start | bytes 12296 | tf_op jit(solution)/shard_map/ppermute | solution.py:321
  146.2 5.6 %collective-permute-start.22 = (f32[17,128]{1,0:T(8,128)S(1)}, f32[17,128]{1,0:T(8,128)S(1)}, u32[]{:S(2)}, u32[]{:S(2)}) collective-permute-start(f32[17,128]{1,0:T(8,128)S(1)} %get-tuple-element.34), channel_id=1, source_target_pairs={{1,0},{6,7},{9,8},{14,15},{17,16},{22,23},{25,24},{30,31}} | collective-permute-start | bytes 26120 | tf_op jit(solution)/shard_map/ppermute | solution.py:336
  147.5 4.3 %collective-permute-start.23 = (f32[17,128]{1,0:T(8,128)S(1)}, f32[17,128]{1,0:T(8,128)S(1)}, u32[]{:S(2)}, u32[]{:S(2)}) collective-permute-start(f32[17,128]{1,0:T(8,128)S(1)} %get-tuple-element.35), channel_id=1, source_target_pairs={{1,2},{6,5},{9,10},{14,13},{17,18},{22,21},{25,26},{30,29}} | collective-permute-start | bytes 26120 | tf_op jit(solution)/shard_map/ppermute | solution.py:336
  148.2 3.6 %collective-permute-start.24 = (f32[17,128]{1,0:T(8,128)S(1)}, f32[17,128]{1,0:T(8,128)S(1)}, u32[]{:S(2)}, u32[]{:S(2)}) collective-permute-start(f32[17,128]{1,0:T(8,128)S(1)} %get-tuple-element.36), channel_id=1, source_target_pairs={{1,3},{6,4},{9,11},{14,12},{17,19},{22,20},{25,27},{30,28}} | collective-permute-start | bytes 26120 | tf_op jit(solution)/shard_map/ppermute | solution.py:336
  (19 other events, 259.1 us)

commit v3 on v2

v3 whole, which is shorter than its diff:
```python
import math

import jax
import jax.numpy as jnp
from jax import lax
from jax.experimental import pallas as pl
from jax.experimental.pallas import tpu as pltpu
from jax.sharding import PartitionSpec as P

ORDER = 4
LANES = 128
CHUNKS = (1, 2, 2, 2, 1)
VMEM = pl.BlockSpec(memory_space=pltpu.VMEM)
UNROLL = 8
HBM = pl.BlockSpec(memory_space=pltpu.HBM)
SMEM = pl.BlockSpec(memory_space=pltpu.SMEM)


def in_hbm(x):
    return pltpu.with_memory_space_constraint(x, pltpu.HBM)


def split(x):
    high = x.astype(jnp.bfloat16)
    return high, (x - high.astype(jnp.float32)).astype(jnp.bfloat16)


def matmul(a, b):
    return jnp.dot(a, b, preferred_element_type=jnp.float32)


def lane_sums(block):
    return jnp.sum(block.T, axis=0, keepdims=True)


def aligned(row):
    return pl.ds(pl.multiple_of(row * LANES, LANES), LANES)


def compose_kernel(first, last, base, steps, held, nonzero, slots, places, pattern, sites, *refs):
    packs, refs = refs[:slots], refs[slots:]
    targets, refs = refs[0], refs[1:]
    if not first:
        refs = refs[2:]
    high, low, refs = refs[0], refs[1], refs[2:]
    if last:
        whole, refs = refs[0], refs[1:]
    through, seen, store, sems = refs
    width, columns = high.shape
    pack_rows = store.shape[2]
    gain_row = held * nonzero * LANES

    def fetch(s, t):
        rows = pl.ds(t * pack_rows, pack_rows)
        return pltpu.make_async_copy(packs[s].at[rows, :], store.at[s, t], sems.at[s, t])

    for t in range(steps):
        for s in range(slots):
            fetch(s, t).start()
    if first:
        rows = lax.broadcasted_iota(jnp.int32, (width, columns), 0)
        cols = lax.broadcasted_iota(jnp.int32, (width, columns), 1)
        high[...] = (rows == cols).astype(jnp.float32).astype(jnp.bfloat16)
        low[...] = jnp.zeros_like(low)

    def step(t, carry):
        for s in range(slots):
            fetch(s, t).wait()

        def block_row(i, carry):
            s, h = i // held, i % held
            row = held * places[s] + h
            picks = [aligned(pattern[base + t, row * nonzero + j]) for j in range(nonzero)]
            parts = [split(store[s, t, aligned(h * nonzero + j), :]) for j in range(nonzero)]
            up = [p[0] for p in parts]
            down = [p[1] for p in parts]
            tops = [high[pick, :] for pick in picks]
            bottoms = [low[pick, :] for pick in picks]
            through[aligned(row), :] = matmul(
                jnp.concatenate(up + down + up, axis=1),
                jnp.concatenate(tops + tops + bottoms),
            )
            return carry

        lax.fori_loop(0, slots * held, block_row, 0, unroll=UNROLL)

        def pick_rows(i, carry):
            for u in range(32):
                k = i * 32 + u
                seen[pl.ds(k, 1), :] = through[pl.ds(ORDER * sites[base + t, k], 1), :]
            return carry

        lax.fori_loop(0, LANES // 32, pick_rows, 0)
        target = jnp.broadcast_to(targets[pl.ds(base + t, 1), :], (LANES, LANES)).T
        lane = lax.broadcasted_iota(jnp.int32, (LANES, LANES), 1)
        offset = pl.ds(width, LANES)
        seen[:, offset] = seen[:, offset] - jnp.where(lane == 0, target, 0.0)
        top, bottom = split(seen[...])
        halves = [split(store[s, t, pl.ds(gain_row, held * LANES), :]) for s in range(slots)]
        left = jnp.concatenate([jnp.concatenate([a, b, a], axis=1) for a, b in halves])
        moved = matmul(left, jnp.concatenate([top, top, bottom]))
        for s in range(slots):
            for h in range(held):
                here = aligned(held * places[s] + h)
                at = (s * held + h) * LANES
                new = through[here, :] - moved[at : at + LANES]
                if last:

                    @pl.when(t == steps - 1)
                    def _(here=here, new=new):
                        whole[here, :] = new

                if not last or steps > 1:
                    a, b = split(new)
                    high[here, :] = a
                    low[here, :] = b
        return carry

    lax.fori_loop(0, steps, step, 0)


def compose(first, last, base, steps, held, nonzero, places, pattern, sites, packs, targets, state):
    slots = len(packs)
    pack_rows = held * (nonzero + 1) * LANES
    width = slots * held * LANES
    columns = width + LANES
    part = jax.ShapeDtypeStruct((width, columns), jnp.bfloat16)
    out_shape = [part, part]
    if last:
        out_shape.append(jax.ShapeDtypeStruct((width, columns), jnp.float32))

    def body(*refs):
        compose_kernel(first, last, base, steps, held, nonzero, slots, *refs)

    done = pl.pallas_call(
        body,
        in_specs=[SMEM] * 3 + [HBM] * slots + [VMEM] * (1 + len(state)),
        out_specs=[VMEM] * len(out_shape),
        out_shape=out_shape,
        scratch_shapes=[
            pltpu.VMEM((width, columns), jnp.float32),
            pltpu.VMEM((LANES, columns), jnp.float32),
            pltpu.VMEM((slots, steps, pack_rows, LANES), jnp.float32),
            pltpu.SemaphoreType.DMA((slots, steps)),
        ],
        cost_estimate=pl.CostEstimate(
            flops=steps * 2 * width * columns * 3 * (nonzero + 1) * LANES,
            transcendentals=0,
            bytes_accessed=4 * slots * steps * pack_rows * LANES,
        ),
        input_output_aliases={} if first else {slots + 4: 0, slots + 5: 1},
        compiler_params=pltpu.CompilerParams(vmem_limit_bytes=36 << 20),
        name="compose",
    )(places, pattern, sites, *[in_hbm(p) for p in packs], targets, *state)
    return done[2] if last else done


def hop_kernel(whole, start, end):
    blocks = start.shape[0]
    for r in range(blocks):
        rows = pl.ds(r * LANES, LANES)
        total = whole[rows, pl.ds(blocks * LANES, LANES)]
        for c in range(blocks):
            total = total + whole[rows, pl.ds(c * LANES, LANES)] * start[pl.ds(c, 1), :]
        end[pl.ds(r, 1), :] = lane_sums(total)


def hop(whole, start):
    return pl.pallas_call(
        hop_kernel,
        in_specs=[VMEM, VMEM],
        out_specs=VMEM,
        out_shape=jax.ShapeDtypeStruct(start.shape, jnp.float32),
        compiler_params=pltpu.CompilerParams(vmem_limit_bytes=8 << 20),
        name="hop",
    )(whole, start)


def stage_kernel(slots, sizes, *refs):
    packs, store, sems = refs[: slots * len(sizes)], refs[-2], refs[-1]
    rows = store.shape[2]
    copies, t = [], 0
    for c, size in enumerate(sizes):
        for i in range(size):
            for s in range(slots):
                copies.append(
                    pltpu.make_async_copy(
                        packs[c * slots + s].at[pl.ds(i * rows, rows), :],
                        store.at[s, t],
                        sems.at[s, t],
                    )
                )
            t += 1
    for copy in copies:
        copy.start()
    for copy in copies:
        copy.wait()


def stage(sizes, pack_rows, packs, after):
    slots, steps = len(packs[0]), sum(sizes)

    def body(*refs):
        stage_kernel(slots, sizes, *refs)

    shape = (slots, steps, pack_rows, LANES)
    return pl.pallas_call(
        body,
        in_specs=[HBM] * (slots * len(sizes)) + [VMEM],
        out_specs=VMEM,
        out_shape=jax.ShapeDtypeStruct(shape, jnp.float32),
        scratch_shapes=[pltpu.SemaphoreType.DMA((slots, steps))],
        cost_estimate=pl.CostEstimate(
            flops=0, transcendentals=0, bytes_accessed=8 * math.prod(shape)
        ),
        compiler_params=pltpu.CompilerParams(vmem_limit_bytes=24 << 20),
        name="stage",
    )(*[in_hbm(p) for pack in packs for p in pack], after)


def segment_kernel(held, nonzero, places, pattern, owner, store, *refs):
    targets, sites, weights, start, parcels, mean, predicted = refs
    slots, steps = store.shape[:2]
    blocks = start.shape[0]
    gain_row = held * nonzero * LANES
    mean[...] = start[...]
    mine = owner[0] == 1

    def step(t, misfit):
        for s in range(slots):
            for h in range(held):
                row = held * places[s] + h
                total = None
                for j in range(nonzero):
                    column = pattern[t, row * nonzero + j]
                    block = store[s, t, pl.ds((h * nonzero + j) * LANES, LANES), :]
                    part = block * mean[pl.ds(column, 1), :]
                    total = part if total is None else total + part
                predicted[pl.ds(row, 1), :] = lane_sums(total)
        flat = ORDER * sites[pl.ds(t, 1), :]
        lane = jnp.broadcast_to(flat % LANES, (blocks, LANES))
        picked = jnp.take_along_axis(predicted[...], lane, axis=1)
        block = lax.broadcasted_iota(jnp.int32, (blocks, LANES), 0)
        picked = jnp.where(block == flat // LANES, picked, 0.0)
        innovation = targets[pl.ds(t, 1), :] - jnp.sum(picked, axis=0, keepdims=True)
        for s in range(slots):
            for h in range(held):
                row = held * places[s] + h
                moved = store[s, t, pl.ds(gain_row + h * LANES, LANES), :] * innovation
                updated = predicted[pl.ds(row, 1), :] + lane_sums(moved)
                mean[pl.ds(row, 1), :] = updated
                parcels[s, pl.ds(t * held + h, 1), :] = jnp.where(mine, updated, 0.0)
        return misfit + innovation * innovation * weights[pl.ds(t, 1), :]

    misfit = lax.fori_loop(0, steps, step, jnp.zeros((1, LANES), jnp.float32))
    for s in range(slots):
        parcels[s, pl.ds(steps * held, 1), :] = jnp.where(mine, misfit, 0.0)


def run_segment(held, nonzero, places, pattern, owner, store, targets, sites, weights, start):
    slots, steps = store.shape[:2]

    def body(*refs):
        segment_kernel(held, nonzero, *refs)

    return pl.pallas_call(
        body,
        in_specs=[SMEM] * 3 + [VMEM] * 5,
        out_specs=VMEM,
        out_shape=jax.ShapeDtypeStruct((slots, steps * held + 1, LANES), jnp.float32),
        scratch_shapes=[
            pltpu.VMEM(start.shape, jnp.float32),
            pltpu.VMEM(start.shape, jnp.float32),
        ],
        compiler_params=pltpu.CompilerParams(vmem_limit_bytes=24 << 20),
        name="segment",
    )(places, pattern, owner, store, targets, sites, weights, start)


def on_device(
    observations,
    sites,
    pattern,
    block_values,
    gains,
    variances,
    monotone_bend_strength,
    initial_mean,
):
    segments, rows = lax.axis_size("tm"), lax.axis_size("row")
    tm, row = lax.axis_index("tm"), lax.axis_index("row")
    steps, held, nonzero = block_values.shape[:3]
    even = tm % 2 == 0

    low = (rows - 1) // 2
    order_even = sorted(range(rows), key=lambda z: (abs(z - low), z))
    order_odd = [rows - 1 - z for z in order_even]

    def order(t):
        return order_even if t % 2 == 0 else order_odd

    def flat(t, z):
        return t * rows + z

    both = ("tm", "row")

    def meet(shard):
        moved = [shard]
        for k in range(1, rows):
            pairs = [(flat(t, order(t)[k]), flat(t, order(t)[0])) for t in range(segments)]
            moved.append(lax.ppermute(shard, both, pairs))
        return moved

    places = jnp.where(
        even, jnp.array(order_even, jnp.int32), jnp.array(order_odd, jnp.int32)
    )
    scale = monotone_bend_strength[0]
    bent = jnp.tanh(observations)
    targets = observations + scale * bent
    log_jacobian = jnp.log(1.0 + scale * (1.0 - bent * bent))
    flat_pattern = pattern.reshape(steps, -1)

    sizes = CHUNKS if sum(CHUNKS) == steps else (1,) * steps
    pack_rows = held * (nonzero + 1) * LANES
    packs, base = [], 0
    for i, size in enumerate(sizes):
        blocks = block_values[base : base + size].reshape(size, -1, LANES)
        pack = jnp.concatenate([blocks, gains[base : base + size]], axis=1)
        pack = pack.reshape(size * pack_rows, LANES)
        if i == 0:
            first = initial_mean.reshape(held, LANES)
            pack = jnp.concatenate([pack, jnp.pad(first, ((0, -held % 8), (0, 0)))])
        packs.append(meet(pack))
        base += size

    starts = [p[sizes[0] * pack_rows :][:held] for p in packs[0]]
    by_even = [starts[order_even.index(z)] for z in range(rows)]
    by_odd = [starts[order_odd.index(z)] for z in range(rows)]
    start = jnp.where(even, jnp.concatenate(by_even), jnp.concatenate(by_odd))

    state, base = (), 0
    for i, size in enumerate(sizes):
        state = compose(
            i == 0,
            i == len(sizes) - 1,
            base,
            size,
            held,
            nonzero,
            places,
            flat_pattern,
            sites,
            packs[i],
            targets,
            state,
        )
        base += size

    mean, begin = start, jnp.where(tm == 0, start, 0.0)
    for t in range(segments - 1):
        pair = [(flat(t, order(t)[0]), flat(t + 1, order(t + 1)[0]))]
        ended = hop(state, mean)
        mean = lax.ppermute(ended, both, pair)
        begin = begin + mean
    store = stage(sizes, pack_rows, packs, ended)
    owner = (row == places[:1]).astype(jnp.int32)
    local = run_segment(
        held,
        nonzero,
        places,
        flat_pattern,
        owner,
        store,
        targets,
        sites,
        1.0 / variances,
        begin,
    )

    while local.shape[0] > 1:
        half = local.shape[0] // 2
        pairs = [
            (flat(t, order(t)[i]), flat(t, order(t)[i + half]))
            for t in range(segments)
            for i in range(0, rows, 2 * half)
        ]
        local = local[:half] + lax.ppermute(local[half:], both, pairs)
    own_filtered = local[0, : steps * held].reshape(steps, held * LANES)

    term = jnp.sum(log_jacobian - 0.5 * jnp.log(variances), axis=0, keepdims=True)
    term = term - 0.5 * local[0, steps * held :]
    if segments & (segments - 1):
        term = lax.psum(term, "tm")
    else:
        reach = 1
        while reach < segments:
            term = term + lax.ppermute(term, "tm", [(t, t ^ reach) for t in range(segments)])
            reach *= 2
    count = observations.size * segments
    evidence = jnp.sum(term) / count - 0.5 * math.log(2.0 * math.pi)
    return own_filtered, evidence.reshape(1)


def solution(mesh):
    in_specs = (
        P("tm", None),
        P("tm", None),
        P("tm", None, None),
        P("tm", "row", None, None, None),
        P("tm", "row", None),
        P("tm", None),
        P(),
        P("row"),
    )
    out_specs = (P("tm", "row"), P())
    return jax.shard_map(
        on_device, mesh=mesh, in_specs=in_specs, out_specs=out_specs, check_vma=False
    )
```

time: 188 us -> 189 us (level)
  blocking collectives: 30.5 us -> 0 us
  starting transfers between devices: 38.8 us -> 69.2 us
  Pallas kernels: 63.9 us -> 73.4 us
  between operations: 8.18 us -> 3.91 us
  other arithmetic: 5.57 us -> 2.8 us
    psum x1 -> x0, blocking collectives: 30.5 us -> none  [on_device(): total = lax.psum(term, 'tm')]
    ppermute x10 -> x12, starting transfers between devices: 7.25 us -> 26 us  [the longest x3 19.4 us: on_device(): lax.ppermute(term, 'tm', [(t, t ^ reach) for t in range(segments)])]
    ppermute x15, starting transfers between devices: 31.6 us -> 43.2 us  [meet(): moved.append(lax.ppermute(shard, both, pairs))]
    ppermute x15, waiting for transfers between devices: 28.8 us -> 18.4 us  [meet(): moved.append(lax.ppermute(shard, both, pairs))]
    ppermute x10 -> x12, waiting for transfers between devices: 2.42 us -> 12 us  [the longest x2 8.75 us: on_device(): local = local[:half] + lax.ppermute(local[half:], both, pairs)]
    pallas_call x4 -> x5, Pallas kernels: 53.2 us -> 59.7 us  [compose(): pl.pallas_call(body, in_specs=[SMEM] * 3 + [HBM] * slots + [VMEM] * (1 +...]
    pallas_call x1 -> x2, Pallas kernels: 8.07 us -> 11.1 us  [the longest x1 6.06 us: stage(): pl.pallas_call(body, in_specs=[HBM] * (slots * len(sizes)) + [VMEM], out_...]
    unnamed x47, local copies, waits for them, and re-layouts: 0.18 us -> 2.77 us
  transfers between devices with their start and end apart: 25 -> 27, of which waited for: 2 -> 6; matrix products, arithmetic and copies ran while one was open for 4% -> 2% of each run, Pallas kernels for 25% -> 31%
where the time goes in v3:
time: 189 us; the launch traced here: 188 us
  Pallas kernels  73.4 us (39%)
  starting transfers between devices  69.2 us (37%)
  waiting for transfers between devices  30.4 us (16%)
  local copies, waits for them, and re-layouts  8.23 us (4%)
  between operations  3.91 us (2%)
  other arithmetic  2.8 us (1%)
    pallas_call x5, Pallas kernels, compose(): pl.pallas_call(body, in_specs=[SMEM] * 3 + [HBM] * slots + [VMEM] * (1 +...  59.7 us
    ppermute x15, starting transfers between devices, meet(): moved.append(lax.ppermute(shard, both, pairs))  43.2 us
    ppermute x3, starting transfers between devices, on_device(): lax.ppermute(term, 'tm', [(t, t ^ reach) for t in range(segments)])  19.4 us
    ppermute x15, waiting for transfers between devices, meet(): moved.append(lax.ppermute(shard, both, pairs))  18.4 us
    ppermute x2, waiting for transfers between devices, on_device(): local = local[:half] + lax.ppermute(local[half:], both, pairs)  8.75 us
    pallas_call x1, Pallas kernels, stage(): pl.pallas_call(body, in_specs=[HBM] * (slots * len(sizes)) + [VMEM], out_...  6.06 us
    pallas_call x1, Pallas kernels, run_segment(): pl.pallas_call(body, in_specs=[SMEM] * 3 + [VMEM] * 5, out_specs=VMEM, ou...  5.02 us
    ppermute x7, starting transfers between devices, on_device(): mean = lax.ppermute(ended, both, pair)  4.63 us
  transfers between devices with their start and end apart: 27, of which 6 were waited for; matrix products, arithmetic and copies ran while one was open for 2% of the time, Pallas kernels for 31%

profile of v3, /device:TPU:0, one launch (start us, length us, event | category | flops | bytes accessed | tf_op | source)
XLA Modules:
  0.0 187.9 jit_solution(5787865506563868065)
XLA Ops:
  0.6 2.1 %fusion.2 = (f32[1,2,3,128,128]{4,3,2,1,0:T(8,128)}, f32[1,2,3,128,128]{4,3,2,1,0:T(8,128)S(1)}) fusion(f32[8,2,3,128,128]{4,3,2,1,0:T(8,128)} %param.13), kind=kLoop, calls=%fused_computation.19 | loop fusion | bytes 1572864 | tf_op jit(solution)/shard_map/slice | solution.py:327
  2.8 1.0 fusion.4
  3.8 0.8 select_maximum_fusion.refs_3_.refs_0_
  4.6 5.1 %collective-permute-start = (f32[1032,128]{1,0:T(8,128)}, f32[1032,128]{1,0:T(8,128)S(1)}, u32[]{:S(2)}, u32[]{:S(2)}) collective-permute-start(f32[1032,128]{1,0:T(8,128)} %select_maximum_fusion.refs_3_.refs_0_), channel_id=1, source_target_pairs={{0,1},{7,6},{8,9},{15,14},{16,17},{23,22},{24,25},{31,30}} | collective-permute-start | bytes 1585160 | tf_op jit(solution)/shard_map/ppermute | solution.py:311
  9.7 1.5 collective-permute-start.1
  11.6 2.4 %collective-permute-start.3 = (f32[2048,128]{1,0:T(8,128)S(1)}, f32[2048,128]{1,0:T(8,128)}, u32[]{:S(2)}, u32[]{:S(2)}) collective-permute-start(f32[2048,128]{1,0:T(8,128)S(1)} %bitcast.27), channel_id=1, source_target_pairs={{0,1},{7,6},{8,9},{15,14},{16,17},{23,22},{24,25},{31,30}} | collective-permute-start | bytes 3145736 | tf_op jit(solution)/shard_map/ppermute | solution.py:311
  14.0 1.6 collective-permute-start.4
  15.7 1.6 collective-permute-start.5
  17.4 4.8 %collective-permute-start.6 = (f32[2048,128]{1,0:T(8,128)S(1)}, f32[2048,128]{1,0:T(8,128)}, u32[]{:S(2)}, u32[]{:S(2)}) collective-permute-start(f32[2048,128]{1,0:T(8,128)S(1)} %bitcast.32), channel_id=1, source_target_pairs={{0,1},{7,6},{8,9},{15,14},{16,17},{23,22},{24,25},{31,30}} | collective-permute-start | bytes 3145736 | tf_op jit(solution)/shard_map/ppermute | solution.py:311
  23.9 1.0 maximum_bitcast_fusion.1.refs_3_.refs_16_
  27.1 12.2 %collective-permute-done.3.refs_4_.refs_5_ = f32[2048,128]{1,0:T(8,128)} collective-permute-done((f32[2048,128]{1,0:T(8,128)S(1)}, f32[2048,128]{1,0:T(8,128)}, u32[]{:S(2)}, u32[]{:S(2)}) %collective-permute-start.3) | collective-permute-done | bytes 1048608 | tf_op jit(solution)/shard_map/ppermute | solution.py:311
  40.0 8.2 %compose.5 = (bf16[1024,1152]{1,0:T(8,128)(2,1)S(1)}, bf16[1024,1152]{1,0:T(8,128)(2,1)S(1)}) custom-call(s32[4]{0:T(128)S(1)} %broadcast_select_fusion.refs_0_, s32[8,24]{1,0:T(8,128)S(1)} %copy.27.refs_1_, s32[8,128]{1,0:T(8,128)S(1)} %copy-done, f32[1032,128]{1,0:T(8,128)} %select_maximum_fusion.refs_3_.refs_0_, f32[1032,128]{1,0:T(8,128)} %copy-done.12, ...), custom_call_target="tpu_custom_call" | custom-call | flops 3623878656 | bytes 2097152 | tf_op jit(solution)/shard_map/compose/pallas_call | solution.py:135
  49.8 6.2 %collective-permute-done.6.refs_4_.refs_9_ = f32[2048,128]{1,0:T(8,128)} collective-permute-done((f32[2048,128]{1,0:T(8,128)S(1)}, f32[2048,128]{1,0:T(8,128)}, u32[]{:S(2)}, u32[]{:S(2)}) %collective-permute-start.6) | collective-permute-done | bytes 1048608 | tf_op jit(solution)/shard_map/ppermute | solution.py:311
  56.0 13.4 %collective-permute-start.9 = (f32[2048,128]{1,0:T(8,128)S(1)}, f32[2048,128]{1,0:T(8,128)S(1)}, u32[]{:S(2)}, u32[]{:S(2)}) collective-permute-start(f32[2048,128]{1,0:T(8,128)S(1)} %bitcast.39), channel_id=1, source_target_pairs={{0,1},{7,6},{8,9},{15,14},{16,17},{23,22},{24,25},{31,30}} | collective-permute-start | bytes 3145736 | tf_op jit(solution)/shard_map/ppermute | solution.py:311
  69.4 14.4 %compose.6 = (bf16[1024,1152]{1,0:T(8,128)(2,1)S(1)}, bf16[1024,1152]{1,0:T(8,128)(2,1)S(1)}) custom-call(s32[4]{0:T(128)S(1)} %broadcast_select_fusion.refs_0_, s32[8,24]{1,0:T(8,128)S(1)} %copy.27.refs_1_, s32[8,128]{1,0:T(8,128)S(1)} %copy-done, f32[2048,128]{1,0:T(8,128)} %bitcast.30, ...), custom_call_target="tpu_custom_call", output_to_operand_aliasing={{0}: (8, {}), {1}: (9, {})} | custom-call | flops 7247757312 | bytes 4194304 | tf_op jit(solution)/shard_map/compose/pallas_call | solution.py:135
  83.8 7.6 %collective-permute-start.12 = (f32[1024,128]{1,0:T(8,128)S(1)}, f32[1024,128]{1,0:T(8,128)S(1)}, u32[]{:S(2)}, u32[]{:S(2)}) collective-permute-start(f32[1024,128]{1,0:T(8,128)S(1)} %maximum_bitcast_fusion.1.refs_3_.refs_16_), channel_id=1, source_target_pairs={{0,1},{7,6},{8,9},{15,14},{16,17},{23,22},{24,25},{31,30}} | collective-permute-start | bytes 1572872 | tf_op jit(solution)/shard_map/ppermute | solution.py:311
  92.4 14.4 %compose.7 = (bf16[1024,1152]{1,0:T(8,128)(2,1)S(1)}, bf16[1024,1152]{1,0:T(8,128)(2,1)S(1)}) custom-call(s32[4]{0:T(128)S(1)} %broadcast_select_fusion.refs_0_, s32[8,24]{1,0:T(8,128)S(1)} %copy.27.refs_1_, s32[8,128]{1,0:T(8,128)S(1)} %copy-done, f32[2048,128]{1,0:T(8,128)} %bitcast.35, ...), custom_call_target="tpu_custom_call", output_to_operand_aliasing={{0}: (8, {}), {1}: (9, {})} | custom-call | flops 7247757312 | bytes 4194304 | tf_op jit(solution)/shard_map/compose/pallas_call | solution.py:135
  106.8 0.9 collective-permute-start.14
  107.8 1.0 copy-done.9
  109.0 14.4 %compose.8 = (bf16[1024,1152]{1,0:T(8,128)(2,1)S(1)}, bf16[1024,1152]{1,0:T(8,128)(2,1)S(1)}) custom-call(s32[4]{0:T(128)S(1)} %broadcast_select_fusion.refs_0_, s32[8,24]{1,0:T(8,128)S(1)} %copy.27.refs_1_, s32[8,128]{1,0:T(8,128)S(1)} %copy-done, f32[2048,128]{1,0:T(8,128)} %bitcast.40, ...), custom_call_target="tpu_custom_call", output_to_operand_aliasing={{0}: (8, {}), {1}: (9, {})} | custom-call | flops 7247757312 | bytes 4194304 | tf_op jit(solution)/shard_map/compose/pallas_call | solution.py:135
  123.5 0.8 copy-done.14
  124.6 8.5 %compose.9 = (bf16[1024,1152]{1,0:T(8,128)(2,1)S(1)}, bf16[1024,1152]{1,0:T(8,128)(2,1)S(1)}, f32[1024,1152]{1,0:T(8,128)S(1)}) custom-call(s32[4]{0:T(128)S(1)} %broadcast_select_fusion.refs_0_, s32[8,24]{1,0:T(8,128)S(1)} %copy.27.refs_1_, s32[8,128]{1,0:T(8,128)S(1)} %copy-done, ...), custom_call_target="tpu_custom_call", output_to_operand_aliasing={{0}: (8, {}), {1}: (9, {})} | custom-call | flops 3623878656 | bytes 2097152 | tf_op jit(solution)/shard_map/compose/pallas_call | solution.py:135
  140.4 6.1 %stage.1.refs_3_ = f32[4,8,1024,128]{3,2,1,0:T(8,128)S(1)} custom-call(f32[1032,128]{1,0:T(8,128)} %select_maximum_fusion.refs_3_.refs_0_, f32[1032,128]{1,0:T(8,128)} %copy-done.12, f32[1032,128]{1,0:T(8,128)} %collective-permute-done.1.refs_5_.refs_2_, f32[1032,128]{1,0:T(8,128)} %copy-done.13, f32[2048,128]{1,0:T(8,128)} %bitcast.31, ...), custom_call_target="tpu_custom_call" | custom-call | bytes 33554432 | tf_op jit(solution)/shard_map/stage/pallas_call | solution.py:207
  146.5 5.0 %segment.1 = f32[4,17,128]{2,1,0:T(8,128)S(1)} custom-call(s32[4]{0:T(128)S(1)} %broadcast_select_fusion.refs_0_, s32[8,24]{1,0:T(8,128)S(1)} %copy.27.refs_1_, s32[1]{0:T(128)S(6)} %convert_element_type.5.refs_2_, f32[4,8,1024,128]{3,2,1,0:T(8,128)S(1)} %stage.1.refs_3_, f32[8,128]{1,0:T(8,128)S(1)} %get-tuple-element.31.refs_7_.refs_4_, ...), custom_call_target="tpu_custom_call" | custom-call | tf_op jit(solution)/shard_map/segment/pallas_call | solution.py:266
  152.3 1.3 collective-permute-start.23
  153.6 8.7 %collective-permute-done.23 = f32[1,17,128]{2,1,0:T(8,128)S(1)} collective-permute-done((f32[1,17,128]{2,1,0:T(8,128)S(1)}, f32[1,17,128]{2,1,0:T(8,128)S(1)}, u32[]{:S(2)}, u32[]{:S(2)}) %collective-permute-start.23) | collective-permute-done | bytes 8736 | tf_op jit(solution)/shard_map/ppermute | solution.py:387
  162.3 2.0 %collective-permute-start.24 = (f32[1,128]{1,0:T(1,128)S(1)}, f32[1,128]{1,0:T(1,128)S(1)}, u32[]{:S(2)}, u32[]{:S(2)}) collective-permute-start(f32[1,128]{1,0:T(1,128)S(1)} %fusion.1), channel_id=1, source_target_pairs={{0,4},{4,0},{8,12},{12,8},{16,20},{20,16},{24,28},{28,24},{1,5},{5... | collective-permute-start | bytes 1544 | tf_op jit(solution)/shard_map/ppermute | solution.py:397
  164.3 0.8 collective-permute-done.24
  165.1 7.0 %collective-permute-start.25 = (f32[1,128]{1,0:T(1,128)S(1)}, f32[1,128]{1,0:T(1,128)S(1)}, u32[]{:S(2)}, u32[]{:S(2)}) collective-permute-start(f32[1,128]{1,0:T(1,128)S(1)} %add.61), channel_id=1, source_target_pairs={{0,8},{4,12},{8,0},{12,4},{16,24},{20,28},{24,16},{28,20},{1,9},{5... | collective-permute-start | bytes 1544 | tf_op jit(solution)/shard_map/ppermute | solution.py:397
  172.1 1.5 collective-permute-done.25
  173.6 10.4 %collective-permute-start.26 = (f32[1,128]{1,0:T(1,128)S(1)}, f32[1,128]{1,0:T(1,128)S(1)}, u32[]{:S(2)}, u32[]{:S(2)}) collective-permute-start(f32[1,128]{1,0:T(1,128)S(1)} %add.62), channel_id=1, source_target_pairs={{0,16},{4,20},{8,24},{12,28},{16,0},{20,4},{24,8},{28,12},{1,17},{... | collective-permute-start | bytes 1544 | tf_op jit(solution)/shard_map/ppermute | solution.py:397
  184.6 0.9 collective-permute-done.26
  (112 shorter events, 16.5 us)
Async XLA Ops:
  4.6 12.8 %collective-permute-start = (f32[1032,128]{1,0:T(8,128)}, f32[1032,128]{1,0:T(8,128)S(1)}, u32[]{:S(2)}, u32[]{:S(2)}) collective-permute-start(f32[1032,128]{1,0:T(8,128)} %select_maximum_fusion.refs_3_.refs_0_), channel_id=1, source_target_pairs={{0,1},{7,6},{8,9},{15,14},{16,17},{23,22},{24,25},{31,30}} | collective-permute-start | bytes 1585160 | tf_op jit(solution)/shard_map/ppermute | solution.py:311
  9.7 13.4 %collective-permute-start.1 = (f32[1032,128]{1,0:T(8,128)}, f32[1032,128]{1,0:T(8,128)}, u32[]{:S(2)}, u32[]{:S(2)}) collective-permute-start(f32[1032,128]{1,0:T(8,128)} %select_maximum_fusion.refs_3_.refs_0_), channel_id=1, source_target_pairs={{2,1},{5,6},{10,9},{13,14},{18,17},{21,22},{26,25},{29,30}} | collective-permute-start | bytes 1585160 | tf_op jit(solution)/shard_map/ppermute | solution.py:311
  11.6 27.6 %collective-permute-start.3 = (f32[2048,128]{1,0:T(8,128)S(1)}, f32[2048,128]{1,0:T(8,128)}, u32[]{:S(2)}, u32[]{:S(2)}) collective-permute-start(f32[2048,128]{1,0:T(8,128)S(1)} %bitcast.27), channel_id=1, source_target_pairs={{0,1},{7,6},{8,9},{15,14},{16,17},{23,22},{24,25},{31,30}} | collective-permute-start | bytes 3145736 | tf_op jit(solution)/shard_map/ppermute | solution.py:311
  14.0 34.2 %collective-permute-start.4 = (f32[2048,128]{1,0:T(8,128)S(1)}, f32[2048,128]{1,0:T(8,128)}, u32[]{:S(2)}, u32[]{:S(2)}) collective-permute-start(f32[2048,128]{1,0:T(8,128)S(1)} %bitcast.28), channel_id=1, source_target_pairs={{2,1},{5,6},{10,9},{13,14},{18,17},{21,22},{26,25},{29,30}} | collective-permute-start | bytes 3145736 | tf_op jit(solution)/shard_map/ppermute | solution.py:311
  15.7 33.4 %collective-permute-start.5 = (f32[2048,128]{1,0:T(8,128)S(1)}, f32[2048,128]{1,0:T(8,128)}, u32[]{:S(2)}, u32[]{:S(2)}) collective-permute-start(f32[2048,128]{1,0:T(8,128)S(1)} %bitcast.29), channel_id=1, source_target_pairs={{3,1},{4,6},{11,9},{12,14},{19,17},{20,22},{27,25},{28,30}} | collective-permute-start | bytes 3145736 | tf_op jit(solution)/shard_map/ppermute | solution.py:311
  17.3 22.7 %copy-start = (s32[8,128]{1,0:T(8,128)S(1)}, s32[8,128]{1,0:T(8,128)}, u32[]{:S(2)}) copy-start(s32[8,128]{1,0:T(8,128)} %refs_5_.1) | copy-start | bytes 12292
  17.4 30.9 %copy-start.2 = (f32[2,1024,128]{2,1,0:T(8,128)}, f32[2,1024,128]{2,1,0:T(8,128)S(1)}, u32[]{:S(2)}) copy-start(f32[2,1024,128]{2,1,0:T(8,128)S(1)} %pad_maximum_fusion.1) | copy-start | bytes 3145732
  17.4 38.6 %collective-permute-start.6 = (f32[2048,128]{1,0:T(8,128)S(1)}, f32[2048,128]{1,0:T(8,128)}, u32[]{:S(2)}, u32[]{:S(2)}) collective-permute-start(f32[2048,128]{1,0:T(8,128)S(1)} %bitcast.32), channel_id=1, source_target_pairs={{0,1},{7,6},{8,9},{15,14},{16,17},{23,22},{24,25},{31,30}} | collective-permute-start | bytes 3145736 | tf_op jit(solution)/shard_map/ppermute | solution.py:311
  22.3 33.7 %copy-start.3 = (f32[2,1024,128]{2,1,0:T(8,128)}, f32[2,1024,128]{2,1,0:T(8,128)S(1)}, u32[]{:S(2)}) copy-start(f32[2,1024,128]{2,1,0:T(8,128)S(1)} %pad_maximum_fusion.2) | copy-start | bytes 3145732
  23.2 3.2 %collective-permute-start.2 = (f32[1032,128]{1,0:T(8,128)}, f32[1032,128]{1,0:T(8,128)S(1)}, u32[]{:S(2)}, u32[]{:S(2)}) collective-permute-start(f32[1032,128]{1,0:T(8,128)} %select_maximum_fusion.refs_3_.refs_0_), channel_id=1, source_target_pairs={{3,1},{4,6},{11,9},{12,14},{19,17},{20,22},{27,25},{28,30}} | collective-permute-start | bytes 1585160 | tf_op jit(solution)/shard_map/ppermute | solution.py:311
  24.9 81.9 %copy-start.5 = (f32[1024,128]{1,0:T(8,128)}, f32[1024,128]{1,0:T(8,128)S(1)}, u32[]{:S(2)}) copy-start(f32[1024,128]{1,0:T(8,128)S(1)} %maximum_bitcast_fusion.1.refs_3_.refs_16_) | copy-start | bytes 1572868
  26.4 13.6 %copy-start.13 = (f32[1032,128]{1,0:T(8,128)}, f32[1032,128]{1,0:T(8,128)S(1)}, u32[]{:S(2)}) copy-start(f32[1032,128]{1,0:T(8,128)S(1)} %collective-permute-done.2.refs_6_.refs_3_) | copy-start | bytes 1585156
  26.4 57.4 %collective-permute-start.7 = (f32[2048,128]{1,0:T(8,128)S(1)}, f32[2048,128]{1,0:T(8,128)S(1)}, u32[]{:S(2)}, u32[]{:S(2)}) collective-permute-start(f32[2048,128]{1,0:T(8,128)S(1)} %bitcast.33), channel_id=1, source_target_pairs={{2,1},{5,6},{10,9},{13,14},{18,17},{21,22},{26,25},{29,30}} | collective-permute-start | bytes 3145736 | tf_op jit(solution)/shard_map/ppermute | solution.py:311
  39.3 52.2 %collective-permute-start.8 = (f32[2048,128]{1,0:T(8,128)S(1)}, f32[2048,128]{1,0:T(8,128)S(1)}, u32[]{:S(2)}, u32[]{:S(2)}) collective-permute-start(f32[2048,128]{1,0:T(8,128)S(1)} %bitcast.34), channel_id=1, source_target_pairs={{3,1},{4,6},{11,9},{12,14},{19,17},{20,22},{27,25},{28,30}} | collective-permute-start | bytes 3145736 | tf_op jit(solution)/shard_map/ppermute | solution.py:311
  48.3 58.5 %collective-permute-start.10 = (f32[2048,128]{1,0:T(8,128)S(1)}, f32[2048,128]{1,0:T(8,128)S(1)}, u32[]{:S(2)}, u32[]{:S(2)}) collective-permute-start(f32[2048,128]{1,0:T(8,128)S(1)} %bitcast.37), channel_id=1, source_target_pairs={{2,1},{5,6},{10,9},{13,14},{18,17},{21,22},{26,25},{29,30}} | collective-permute-start | bytes 3145736 | tf_op jit(solution)/shard_map/ppermute | solution.py:311
  49.0 58.7 %collective-permute-start.11 = (f32[2048,128]{1,0:T(8,128)S(1)}, f32[2048,128]{1,0:T(8,128)S(1)}, u32[]{:S(2)}, u32[]{:S(2)}) collective-permute-start(f32[2048,128]{1,0:T(8,128)S(1)} %bitcast.38), channel_id=1, source_target_pairs={{3,1},{4,6},{11,9},{12,14},{19,17},{20,22},{27,25},{28,30}} | collective-permute-start | bytes 3145736 | tf_op jit(solution)/shard_map/ppermute | solution.py:311
  56.0 51.7 %collective-permute-start.9 = (f32[2048,128]{1,0:T(8,128)S(1)}, f32[2048,128]{1,0:T(8,128)S(1)}, u32[]{:S(2)}, u32[]{:S(2)}) collective-permute-start(f32[2048,128]{1,0:T(8,128)S(1)} %bitcast.39), channel_id=1, source_target_pairs={{0,1},{7,6},{8,9},{15,14},{16,17},{23,22},{24,25},{31,30}} | collective-permute-start | bytes 3145736 | tf_op jit(solution)/shard_map/ppermute | solution.py:311
  83.8 39.6 %collective-permute-start.12 = (f32[1024,128]{1,0:T(8,128)S(1)}, f32[1024,128]{1,0:T(8,128)S(1)}, u32[]{:S(2)}, u32[]{:S(2)}) collective-permute-start(f32[1024,128]{1,0:T(8,128)S(1)} %maximum_bitcast_fusion.1.refs_3_.refs_16_), channel_id=1, source_target_pairs={{0,1},{7,6},{8,9},{15,14},{16,17},{23,22},{24,25},{31,30}} | collective-permute-start | bytes 1572872 | tf_op jit(solution)/shard_map/ppermute | solution.py:311
  91.4 32.0 %collective-permute-start.13 = (f32[1024,128]{1,0:T(8,128)S(1)}, f32[1024,128]{1,0:T(8,128)S(1)}, u32[]{:S(2)}, u32[]{:S(2)}) collective-permute-start(f32[1024,128]{1,0:T(8,128)S(1)} %maximum_bitcast_fusion.1.refs_3_.refs_16_), channel_id=1, source_target_pairs={{2,1},{5,6},{10,9},{13,14},{18,17},{21,22},{26,25},{29,30}} | collective-permute-start | bytes 1572872 | tf_op jit(solution)/shard_map/ppermute | solution.py:311
  106.8 16.7 %collective-permute-start.14 = (f32[1024,128]{1,0:T(8,128)S(1)}, f32[1024,128]{1,0:T(8,128)S(1)}, u32[]{:S(2)}, u32[]{:S(2)}) collective-permute-start(f32[1024,128]{1,0:T(8,128)S(1)} %maximum_bitcast_fusion.1.refs_3_.refs_16_), channel_id=1, source_target_pairs={{3,1},{4,6},{11,9},{12,14},{19,17},{20,22},{27,25},{28,30}} | collective-permute-start | bytes 1572872 | tf_op jit(solution)/shard_map/ppermute | solution.py:311
  133.4 0.7 collective-permute-start.15
  134.4 0.7 collective-permute-start.16
  135.5 0.7 collective-permute-start.17
  136.5 0.7 collective-permute-start.18
  137.6 0.7 collective-permute-start.19
  138.6 0.7 collective-permute-start.20
  139.7 6.8 %collective-permute-start.21 = (f32[8,128]{1,0:T(8,128)S(1)}, f32[8,128]{1,0:T(8,128)S(1)}, u32[]{:S(2)}, u32[]{:S(2)}) collective-permute-start(f32[8,128]{1,0:T(8,128)S(1)} %hop.13.refs_20_), channel_id=1, source_target_pairs={{25,30}} | collective-permute-start | bytes 12296 | tf_op jit(solution)/shard_map/ppermute | solution.py:363
  151.5 0.7 collective-permute-start.22
  152.3 10.0 %collective-permute-start.23 = (f32[1,17,128]{2,1,0:T(8,128)S(1)}, f32[1,17,128]{2,1,0:T(8,128)S(1)}, u32[]{:S(2)}, u32[]{:S(2)}) collective-permute-start(f32[1,17,128]{2,1,0:T(8,128)S(1)} %slice.93), channel_id=1, source_target_pairs={{1,0},{2,3},{6,7},{5,4},{9,8},{10,11},{14,15},{13,12},{17,16},{18,... | collective-permute-start | bytes 26120 | tf_op jit(solution)/shard_map/ppermute | solution.py:387
  162.3 2.8 %collective-permute-start.24 = (f32[1,128]{1,0:T(1,128)S(1)}, f32[1,128]{1,0:T(1,128)S(1)}, u32[]{:S(2)}, u32[]{:S(2)}) collective-permute-start(f32[1,128]{1,0:T(1,128)S(1)} %fusion.1), channel_id=1, source_target_pairs={{0,4},{4,0},{8,12},{12,8},{16,20},{20,16},{24,28},{28,24},{1,5},{5... | collective-permute-start | bytes 1544 | tf_op jit(solution)/shard_map/ppermute | solution.py:397
  165.1 8.5 %collective-permute-start.25 = (f32[1,128]{1,0:T(1,128)S(1)}, f32[1,128]{1,0:T(1,128)S(1)}, u32[]{:S(2)}, u32[]{:S(2)}) collective-permute-start(f32[1,128]{1,0:T(1,128)S(1)} %add.61), channel_id=1, source_target_pairs={{0,8},{4,12},{8,0},{12,4},{16,24},{20,28},{24,16},{28,20},{1,9},{5... | collective-permute-start | bytes 1544 | tf_op jit(solution)/shard_map/ppermute | solution.py:397
  173.6 11.9 %collective-permute-start.26 = (f32[1,128]{1,0:T(1,128)S(1)}, f32[1,128]{1,0:T(1,128)S(1)}, u32[]{:S(2)}, u32[]{:S(2)}) collective-permute-start(f32[1,128]{1,0:T(1,128)S(1)} %add.62), channel_id=1, source_target_pairs={{0,16},{4,20},{8,24},{12,28},{16,0},{20,4},{24,8},{28,12},{1,17},{... | collective-permute-start | bytes 1544 | tf_op jit(solution)/shard_map/ppermute | solution.py:397
  (18 other events, 96.1 us)

commit v4 on v3

--- a/solution.py
+++ b/solution.py
@@ -330,14 +330,10 @@
         if i == 0:
             first = initial_mean.reshape(held, LANES)
             pack = jnp.concatenate([pack, jnp.pad(first, ((0, -held % 8), (0, 0)))])
-        packs.append(meet(pack))
+        packs.append(pack)
         base += size
 
-    starts = [p[sizes[0] * pack_rows :][:held] for p in packs[0]]
-    by_even = [starts[order_even.index(z)] for z in range(rows)]
-    by_odd = [starts[order_odd.index(z)] for z in range(rows)]
-    start = jnp.where(even, jnp.concatenate(by_even), jnp.concatenate(by_odd))
-
+    packs[:2] = [meet(pack) for pack in packs[:2]]
     state, base = (), 0
     for i, size in enumerate(sizes):
         state = compose(
@@ -355,6 +351,14 @@
             state,
         )
         base += size
+        if i + 2 < len(sizes):
+            packs[i + 2], *state = lax.optimization_barrier((packs[i + 2], *state))
+            packs[i + 2] = meet(packs[i + 2])
+
+    starts = [p[sizes[0] * pack_rows :][:held] for p in packs[0]]
+    by_even = [starts[order_even.index(z)] for z in range(rows)]
+    by_odd = [starts[order_odd.index(z)] for z in range(rows)]
+    start = jnp.where(even, jnp.concatenate(by_even), jnp.concatenate(by_odd))
 
     mean, begin = start, jnp.where(tm == 0, start, 0.0)
     for t in range(segments - 1):
@@ -362,7 +366,8 @@
         ended = hop(state, mean)
         mean = lax.ppermute(ended, both, pair)
         begin = begin + mean
-    store = stage(sizes, pack_rows, packs, ended)
+        if t == min(2, segments - 2):
+            store = stage(sizes, pack_rows, packs, ended)
     owner = (row == places[:1]).astype(jnp.int32)
     local = run_segment(
         held,

time: 189 us -> 174 us (0.921)
  waiting for transfers between devices: 30.4 us -> 21 us
  starting transfers between devices: 69.2 us -> 60.9 us
  local copies, waits for them, and re-layouts: 8.23 us -> 13.3 us
    ppermute x15, waiting for transfers between devices: 18.4 us -> 7.39 us  [meet(): moved.append(lax.ppermute(shard, both, pairs))]
    ppermute x15, starting transfers between devices: 43.2 us -> 35 us  [meet(): moved.append(lax.ppermute(shard, both, pairs))]
    unnamed x47 -> x57, local copies, waits for them, and re-layouts: 2.77 us -> 6.27 us
  transfers between devices with their start and end apart: 27 -> 27, of which waited for: 6 -> 7; matrix products, arithmetic and copies ran while one was open for 2% -> 2% of each run, Pallas kernels for 31% -> 33%
where the time goes in v4:
time: 174 us
  Pallas kernels  73.4 us (42%)
  starting transfers between devices  60.9 us (35%)
  waiting for transfers between devices  21 us (12%)
  local copies, waits for them, and re-layouts  13.3 us (8%)
  between operations  3.86 us (2%)
    pallas_call x5, Pallas kernels, compose(): pl.pallas_call(body, in_specs=[SMEM] * 3 + [HBM] * slots + [VMEM] * (1 +...  59.8 us
    ppermute x15, starting transfers between devices, meet(): moved.append(lax.ppermute(shard, both, pairs))  35 us
    ppermute x3, starting transfers between devices, on_device(): lax.ppermute(term, 'tm', [(t, t ^ reach) for t in range(segments)])  19.4 us
    ppermute x2, waiting for transfers between devices, on_device(): local = local[:half] + lax.ppermute(local[half:], both, pairs)  10.3 us
    ppermute x15, waiting for transfers between devices, meet(): moved.append(lax.ppermute(shard, both, pairs))  7.39 us
    unnamed x57, local copies, waits for them, and re-layouts  6.27 us
    pallas_call x1, Pallas kernels, stage(): pl.pallas_call(body, in_specs=[HBM] * (slots * len(sizes)) + [VMEM], out_...  6.06 us
    pallas_call x1, Pallas kernels, run_segment(): pl.pallas_call(body, in_specs=[SMEM] * 3 + [VMEM] * 5, out_specs=VMEM, ou...  5.02 us
  transfers between devices with their start and end apart: 27, of which 7 were waited for; matrix products, arithmetic and copies ran while one was open for 2% of the time, Pallas kernels for 33%

profile of v4, /device:TPU:0, one launch (start us, length us, event | category | flops | bytes accessed | tf_op | source)
XLA Modules:
  0.0 173.5 jit_solution(2423133455729514937)
XLA Ops:
  0.6 2.1 %fusion.2 = (f32[1,2,3,128,128]{4,3,2,1,0:T(8,128)}, f32[1,2,3,128,128]{4,3,2,1,0:T(8,128)S(1)}) fusion(f32[8,2,3,128,128]{4,3,2,1,0:T(8,128)} %param.13), kind=kLoop, calls=%fused_computation.19 | loop fusion | bytes 1572864 | tf_op jit(solution)/shard_map/slice | solution.py:327
  2.8 1.0 fusion.4
  3.9 5.1 %collective-permute-start = (f32[1032,128]{1,0:T(8,128)S(1)}, f32[1032,128]{1,0:T(8,128)S(1)}, u32[]{:S(2)}, u32[]{:S(2)}) collective-permute-start(f32[1032,128]{1,0:T(8,128)S(1)} %select_maximum_fusion.refs_3_.refs_0_), channel_id=1, source_target_pairs={{0,1},{7,6},{8,9},{15,14},{16,17},{23,22},{24,25},{31,30}} | collective-permute-start | bytes 1585160 | tf_op jit(solution)/shard_map/ppermute | solution.py:311
  9.0 1.5 collective-permute-start.1
  10.4 1.5 collective-permute-start.2
  11.9 1.1 fusion.3
  13.9 2.3 %collective-permute-start.3 = (f32[2048,128]{1,0:T(8,128)S(1)}, f32[2048,128]{1,0:T(8,128)}, u32[]{:S(2)}, u32[]{:S(2)}) collective-permute-start(f32[2048,128]{1,0:T(8,128)S(1)} %bitcast.27), channel_id=1, source_target_pairs={{0,1},{7,6},{8,9},{15,14},{16,17},{23,22},{24,25},{31,30}} | collective-permute-start | bytes 3145736 | tf_op jit(solution)/shard_map/ppermute | solution.py:311
  16.2 1.6 collective-permute-start.4
  19.7 8.2 %compose.5 = (bf16[1024,1152]{1,0:T(8,128)(2,1)S(1)}, bf16[1024,1152]{1,0:T(8,128)(2,1)S(1)}) custom-call(s32[4]{0:T(128)S(1)} %broadcast_select_fusion.refs_0_, s32[8,24]{1,0:T(8,128)S(1)} %copy.27.refs_1_, s32[8,128]{1,0:T(8,128)S(1)} %copy-done, f32[1032,128]{1,0:T(8,128)} %copy-done.6, f32[1032,128]{1,0:T(8,128)} %copy-done.18, ...), custom_call_target="tpu_custom_call" | custom-call | flops 3623878656 | bytes 2097152 | tf_op jit(solution)/shard_map/compose/pallas_call | solution.py:135
  27.9 9.8 %collective-permute-start.6 = (f32[2048,128]{1,0:T(8,128)S(1)}, f32[2048,128]{1,0:T(8,128)S(1)}, u32[]{:S(2)}, u32[]{:S(2)}) collective-permute-start(f32[2048,128]{1,0:T(8,128)S(1)} %bitcast.32), channel_id=1, source_target_pairs={{0,1},{7,6},{8,9},{15,14},{16,17},{23,22},{24,25},{31,30}} | collective-permute-start | bytes 3145736 | tf_op jit(solution)/shard_map/ppermute | solution.py:311
  38.7 2.6 %collective-permute-done.3.refs_4_.refs_5_ = f32[2048,128]{1,0:T(8,128)} collective-permute-done((f32[2048,128]{1,0:T(8,128)S(1)}, f32[2048,128]{1,0:T(8,128)}, u32[]{:S(2)}, u32[]{:S(2)}) %collective-permute-start.3) | collective-permute-done | bytes 1048608 | tf_op jit(solution)/shard_map/ppermute | solution.py:311
  42.2 1.0 copy-done.9
  43.2 14.4 %compose.6 = (bf16[1024,1152]{1,0:T(8,128)(2,1)S(1)}, bf16[1024,1152]{1,0:T(8,128)(2,1)S(1)}) custom-call(s32[4]{0:T(128)S(1)} %broadcast_select_fusion.refs_0_, s32[8,24]{1,0:T(8,128)S(1)} %copy.27.refs_1_, s32[8,128]{1,0:T(8,128)S(1)} %copy-done, f32[2048,128]{1,0:T(8,128)} %bitcast.30, ...), custom_call_target="tpu_custom_call", output_to_operand_aliasing={{0}: (8, {}), {1}: (9, {})} | custom-call | flops 7247757312 | bytes 4194304 | tf_op jit(solution)/shard_map/compose/pallas_call | solution.py:135
  59.0 4.7 %collective-permute-done.6.refs_4_.refs_9_ = f32[2048,128]{1,0:T(8,128)S(1)} collective-permute-done((f32[2048,128]{1,0:T(8,128)S(1)}, f32[2048,128]{1,0:T(8,128)S(1)}, u32[]{:S(2)}, u32[]{:S(2)}) %collective-permute-start.6) | collective-permute-done | bytes 1048608 | tf_op jit(solution)/shard_map/ppermute | solution.py:311
  63.7 6.4 %collective-permute-start.9 = (f32[2048,128]{1,0:T(8,128)S(1)}, f32[2048,128]{1,0:T(8,128)S(1)}, u32[]{:S(2)}, u32[]{:S(2)}) collective-permute-start(f32[2048,128]{1,0:T(8,128)S(1)} %bitcast.39), channel_id=1, source_target_pairs={{0,1},{7,6},{8,9},{15,14},{16,17},{23,22},{24,25},{31,30}} | collective-permute-start | bytes 3145736 | tf_op jit(solution)/shard_map/ppermute | solution.py:311
  71.6 1.0 copy-done.11
  72.7 1.0 copy-done.12
  73.6 14.4 %compose.7 = (bf16[1024,1152]{1,0:T(8,128)(2,1)S(1)}, bf16[1024,1152]{1,0:T(8,128)(2,1)S(1)}) custom-call(s32[4]{0:T(128)S(1)} %broadcast_select_fusion.refs_0_, s32[8,24]{1,0:T(8,128)S(1)} %copy.27.refs_1_, s32[8,128]{1,0:T(8,128)S(1)} %copy-done, f32[2048,128]{1,0:T(8,128)} %bitcast.35, ...), custom_call_target="tpu_custom_call", output_to_operand_aliasing={{0}: (8, {}), {1}: (9, {})} | custom-call | flops 7247757312 | bytes 4194304 | tf_op jit(solution)/shard_map/compose/pallas_call | solution.py:135
  88.0 1.3 collective-permute-start.12
  90.1 0.9 collective-permute-start.14
  91.0 1.0 copy-done.14
  92.0 1.0 copy-done.15
  93.0 14.4 %compose.8 = (bf16[1024,1152]{1,0:T(8,128)(2,1)S(1)}, bf16[1024,1152]{1,0:T(8,128)(2,1)S(1)}) custom-call(s32[4]{0:T(128)S(1)} %broadcast_select_fusion.refs_0_, s32[8,24]{1,0:T(8,128)S(1)} %copy.27.refs_1_, s32[8,128]{1,0:T(8,128)S(1)} %copy-done, f32[2048,128]{1,0:T(8,128)} %bitcast.40, ...), custom_call_target="tpu_custom_call", output_to_operand_aliasing={{0}: (8, {}), {1}: (9, {})} | custom-call | flops 7247757312 | bytes 4194304 | tf_op jit(solution)/shard_map/compose/pallas_call | solution.py:135
  108.6 8.5 %compose.9 = (bf16[1024,1152]{1,0:T(8,128)(2,1)S(1)}, bf16[1024,1152]{1,0:T(8,128)(2,1)S(1)}, f32[1024,1152]{1,0:T(8,128)S(1)}) custom-call(s32[4]{0:T(128)S(1)} %broadcast_select_fusion.refs_0_, s32[8,24]{1,0:T(8,128)S(1)} %copy.27.refs_1_, s32[8,128]{1,0:T(8,128)S(1)} %copy-done, ...), custom_call_target="tpu_custom_call", output_to_operand_aliasing={{0}: (8, {}), {1}: (9, {})} | custom-call | flops 3623878656 | bytes 2097152 | tf_op jit(solution)/shard_map/compose/pallas_call | solution.py:135
  124.4 6.1 %stage.1.refs_3_ = f32[4,8,1024,128]{3,2,1,0:T(8,128)S(1)} custom-call(f32[1032,128]{1,0:T(8,128)} %copy-done.6, f32[1032,128]{1,0:T(8,128)} %copy-done.18, f32[1032,128]{1,0:T(8,128)} %collective-permute-done.1.refs_5_.refs_2_, f32[1032,128]{1,0:T(8,128)} %collective-permute-done.2.refs_6_.refs_3_, f32[2048,128]{1,0:T(8,128)} %bitcast.31, ...), custom_call_target="tpu_custom_call" | custom-call | bytes 33554432 | tf_op jit(solution)/shard_map/stage/pallas_call | solution.py:207
  130.5 5.0 %segment.1 = f32[4,17,128]{2,1,0:T(8,128)S(1)} custom-call(s32[4]{0:T(128)S(1)} %broadcast_select_fusion.refs_0_, s32[8,24]{1,0:T(8,128)S(1)} %copy.27.refs_1_, s32[1]{0:T(128)S(6)} %convert_element_type.5.refs_2_, f32[4,8,1024,128]{3,2,1,0:T(8,128)S(1)} %stage.1.refs_3_, f32[8,128]{1,0:T(8,128)S(1)} %get-tuple-element.49.refs_7_.refs_4_, ...), custom_call_target="tpu_custom_call" | custom-call | tf_op jit(solution)/shard_map/segment/pallas_call | solution.py:266
  136.3 1.3 collective-permute-start.23
  137.6 10.3 %collective-permute-done.23 = f32[1,17,128]{2,1,0:T(8,128)S(1)} collective-permute-done((f32[1,17,128]{2,1,0:T(8,128)S(1)}, f32[1,17,128]{2,1,0:T(8,128)S(1)}, u32[]{:S(2)}, u32[]{:S(2)}) %collective-permute-start.23) | collective-permute-done | bytes 8736 | tf_op jit(solution)/shard_map/ppermute | solution.py:392
  147.9 2.0 %collective-permute-start.24 = (f32[1,128]{1,0:T(1,128)S(1)}, f32[1,128]{1,0:T(1,128)S(1)}, u32[]{:S(2)}, u32[]{:S(2)}) collective-permute-start(f32[1,128]{1,0:T(1,128)S(1)} %fusion.1), channel_id=1, source_target_pairs={{0,4},{4,0},{8,12},{12,8},{16,20},{20,16},{24,28},{28,24},{1,5},{5... | collective-permute-start | bytes 1544 | tf_op jit(solution)/shard_map/ppermute | solution.py:402
  150.7 7.0 %collective-permute-start.25 = (f32[1,128]{1,0:T(1,128)S(1)}, f32[1,128]{1,0:T(1,128)S(1)}, u32[]{:S(2)}, u32[]{:S(2)}) collective-permute-start(f32[1,128]{1,0:T(1,128)S(1)} %add.61), channel_id=1, source_target_pairs={{0,8},{4,12},{8,0},{12,4},{16,24},{20,28},{24,16},{28,20},{1,9},{5... | collective-permute-start | bytes 1544 | tf_op jit(solution)/shard_map/ppermute | solution.py:402
  157.7 1.5 collective-permute-done.25
  159.2 10.4 %collective-permute-start.26 = (f32[1,128]{1,0:T(1,128)S(1)}, f32[1,128]{1,0:T(1,128)S(1)}, u32[]{:S(2)}, u32[]{:S(2)}) collective-permute-start(f32[1,128]{1,0:T(1,128)S(1)} %add.62), channel_id=1, source_target_pairs={{0,16},{4,20},{8,24},{12,28},{16,0},{20,4},{24,8},{28,12},{1,17},{... | collective-permute-start | bytes 1544 | tf_op jit(solution)/shard_map/ppermute | solution.py:402
  (123 shorter events, 19.5 us)
Async XLA Ops:
  3.9 14.9 %collective-permute-start = (f32[1032,128]{1,0:T(8,128)S(1)}, f32[1032,128]{1,0:T(8,128)S(1)}, u32[]{:S(2)}, u32[]{:S(2)}) collective-permute-start(f32[1032,128]{1,0:T(8,128)S(1)} %select_maximum_fusion.refs_3_.refs_0_), channel_id=1, source_target_pairs={{0,1},{7,6},{8,9},{15,14},{16,17},{23,22},{24,25},{31,30}} | collective-permute-start | bytes 1585160 | tf_op jit(solution)/shard_map/ppermute | solution.py:311
  9.0 10.7 %collective-permute-start.1 = (f32[1032,128]{1,0:T(8,128)S(1)}, f32[1032,128]{1,0:T(8,128)}, u32[]{:S(2)}, u32[]{:S(2)}) collective-permute-start(f32[1032,128]{1,0:T(8,128)S(1)} %select_maximum_fusion.refs_3_.refs_0_), channel_id=1, source_target_pairs={{2,1},{5,6},{10,9},{13,14},{18,17},{21,22},{26,25},{29,30}} | collective-permute-start | bytes 1585160 | tf_op jit(solution)/shard_map/ppermute | solution.py:311
  10.4 9.2 %collective-permute-start.2 = (f32[1032,128]{1,0:T(8,128)S(1)}, f32[1032,128]{1,0:T(8,128)}, u32[]{:S(2)}, u32[]{:S(2)}) collective-permute-start(f32[1032,128]{1,0:T(8,128)S(1)} %select_maximum_fusion.refs_3_.refs_0_), channel_id=1, source_target_pairs={{3,1},{4,6},{11,9},{12,14},{19,17},{20,22},{27,25},{28,30}} | collective-permute-start | bytes 1585160 | tf_op jit(solution)/shard_map/ppermute | solution.py:311
  13.9 27.4 %collective-permute-start.3 = (f32[2048,128]{1,0:T(8,128)S(1)}, f32[2048,128]{1,0:T(8,128)}, u32[]{:S(2)}, u32[]{:S(2)}) collective-permute-start(f32[2048,128]{1,0:T(8,128)S(1)} %bitcast.27), channel_id=1, source_target_pairs={{0,1},{7,6},{8,9},{15,14},{16,17},{23,22},{24,25},{31,30}} | collective-permute-start | bytes 3145736 | tf_op jit(solution)/shard_map/ppermute | solution.py:311
  16.2 26.0 %collective-permute-start.4 = (f32[2048,128]{1,0:T(8,128)S(1)}, f32[2048,128]{1,0:T(8,128)}, u32[]{:S(2)}, u32[]{:S(2)}) collective-permute-start(f32[2048,128]{1,0:T(8,128)S(1)} %bitcast.28), channel_id=1, source_target_pairs={{2,1},{5,6},{10,9},{13,14},{18,17},{21,22},{26,25},{29,30}} | collective-permute-start | bytes 3145736 | tf_op jit(solution)/shard_map/ppermute | solution.py:311
  18.8 23.4 %collective-permute-start.5 = (f32[2048,128]{1,0:T(8,128)S(1)}, f32[2048,128]{1,0:T(8,128)S(1)}, u32[]{:S(2)}, u32[]{:S(2)}) collective-permute-start(f32[2048,128]{1,0:T(8,128)S(1)} %bitcast.29), channel_id=1, source_target_pairs={{3,1},{4,6},{11,9},{12,14},{19,17},{20,22},{27,25},{28,30}} | collective-permute-start | bytes 3145736 | tf_op jit(solution)/shard_map/ppermute | solution.py:311
  19.6 21.7 %copy-start.2 = (f32[2,1024,128]{2,1,0:T(8,128)}, f32[2,1024,128]{2,1,0:T(8,128)S(1)}, u32[]{:S(2)}) copy-start(f32[2,1024,128]{2,1,0:T(8,128)S(1)} %pad_maximum_fusion.1) | copy-start | bytes 3145732
  27.9 35.8 %collective-permute-start.6 = (f32[2048,128]{1,0:T(8,128)S(1)}, f32[2048,128]{1,0:T(8,128)S(1)}, u32[]{:S(2)}, u32[]{:S(2)}) collective-permute-start(f32[2048,128]{1,0:T(8,128)S(1)} %bitcast.32), channel_id=1, source_target_pairs={{0,1},{7,6},{8,9},{15,14},{16,17},{23,22},{24,25},{31,30}} | collective-permute-start | bytes 3145736 | tf_op jit(solution)/shard_map/ppermute | solution.py:311
  37.8 25.9 %copy-start.3 = (f32[2,1024,128]{2,1,0:T(8,128)}, f32[2,1024,128]{2,1,0:T(8,128)S(1)}, u32[]{:S(2)}) copy-start(f32[2,1024,128]{2,1,0:T(8,128)S(1)} %pad_maximum_fusion.2) | copy-start | bytes 3145732
  37.8 32.4 %copy-start.8 = (f32[1,2,3,128,128]{4,3,2,1,0:T(8,128)S(1)}, f32[1,2,3,128,128]{4,3,2,1,0:T(8,128)}, u32[]{:S(2)}) copy-start(f32[1,2,3,128,128]{4,3,2,1,0:T(8,128)} %get-tuple-element.38) | copy-start | bytes 1179652
  37.8 33.8 %slice-start = ((f32[1032,128]{1,0:T(8,128)}), f32[2,128]{1,0:T(2,128)S(1)}, s32[]{:S(2)}) async-start(f32[1032,128]{1,0:T(8,128)} %copy-done.18), calls=%async_computation | async-start | bytes 2048 | tf_op jit(solution)/shard_map/slice | solution.py:358
  37.8 33.8 %collective-permute-start.7 = (f32[2048,128]{1,0:T(8,128)S(1)}, f32[2048,128]{1,0:T(8,128)S(1)}, u32[]{:S(2)}, u32[]{:S(2)}) collective-permute-start(f32[2048,128]{1,0:T(8,128)S(1)} %bitcast.33), channel_id=1, source_target_pairs={{2,1},{5,6},{10,9},{13,14},{18,17},{21,22},{26,25},{29,30}} | collective-permute-start | bytes 3145736 | tf_op jit(solution)/shard_map/ppermute | solution.py:311
  41.2 30.4 %collective-permute-start.8 = (f32[2048,128]{1,0:T(8,128)S(1)}, f32[2048,128]{1,0:T(8,128)S(1)}, u32[]{:S(2)}, u32[]{:S(2)}) collective-permute-start(f32[2048,128]{1,0:T(8,128)S(1)} %bitcast.34), channel_id=1, source_target_pairs={{3,1},{4,6},{11,9},{12,14},{19,17},{20,22},{27,25},{28,30}} | collective-permute-start | bytes 3145736 | tf_op jit(solution)/shard_map/ppermute | solution.py:311
  57.6 32.5 %collective-permute-start.10 = (f32[2048,128]{1,0:T(8,128)S(1)}, f32[2048,128]{1,0:T(8,128)S(1)}, u32[]{:S(2)}, u32[]{:S(2)}) collective-permute-start(f32[2048,128]{1,0:T(8,128)S(1)} %bitcast.37), channel_id=1, source_target_pairs={{2,1},{5,6},{10,9},{13,14},{18,17},{21,22},{26,25},{29,30}} | collective-permute-start | bytes 3145736 | tf_op jit(solution)/shard_map/ppermute | solution.py:311
  58.3 32.7 %collective-permute-start.11 = (f32[2048,128]{1,0:T(8,128)S(1)}, f32[2048,128]{1,0:T(8,128)S(1)}, u32[]{:S(2)}, u32[]{:S(2)}) collective-permute-start(f32[2048,128]{1,0:T(8,128)S(1)} %bitcast.38), channel_id=1, source_target_pairs={{3,1},{4,6},{11,9},{12,14},{19,17},{20,22},{27,25},{28,30}} | collective-permute-start | bytes 3145736 | tf_op jit(solution)/shard_map/ppermute | solution.py:311
  63.7 27.3 %collective-permute-start.9 = (f32[2048,128]{1,0:T(8,128)S(1)}, f32[2048,128]{1,0:T(8,128)S(1)}, u32[]{:S(2)}, u32[]{:S(2)}) collective-permute-start(f32[2048,128]{1,0:T(8,128)S(1)} %bitcast.39), channel_id=1, source_target_pairs={{0,1},{7,6},{8,9},{15,14},{16,17},{23,22},{24,25},{31,30}} | collective-permute-start | bytes 3145736 | tf_op jit(solution)/shard_map/ppermute | solution.py:311
  70.2 19.9 %copy-start.7 = (f32[1024,128]{1,0:T(8,128)}, f32[1024,128]{1,0:T(8,128)S(1)}, u32[]{:S(2)}) copy-start(f32[1024,128]{1,0:T(8,128)S(1)} %maximum_bitcast_fusion.1.refs_3_.refs_16_) | copy-start | bytes 1572868
  88.0 19.4 %collective-permute-start.12 = (f32[1024,128]{1,0:T(8,128)S(1)}, f32[1024,128]{1,0:T(8,128)S(1)}, u32[]{:S(2)}, u32[]{:S(2)}) collective-permute-start(f32[1024,128]{1,0:T(8,128)S(1)} %maximum_bitcast_fusion.1.refs_3_.refs_16_), channel_id=1, source_target_pairs={{0,1},{7,6},{8,9},{15,14},{16,17},{23,22},{24,25},{31,30}} | collective-permute-start | bytes 1572872 | tf_op jit(solution)/shard_map/ppermute | solution.py:311
  89.3 18.1 %collective-permute-start.13 = (f32[1024,128]{1,0:T(8,128)S(1)}, f32[1024,128]{1,0:T(8,128)S(1)}, u32[]{:S(2)}, u32[]{:S(2)}) collective-permute-start(f32[1024,128]{1,0:T(8,128)S(1)} %maximum_bitcast_fusion.1.refs_3_.refs_16_), channel_id=1, source_target_pairs={{2,1},{5,6},{10,9},{13,14},{18,17},{21,22},{26,25},{29,30}} | collective-permute-start | bytes 1572872 | tf_op jit(solution)/shard_map/ppermute | solution.py:311
  90.1 17.4 %collective-permute-start.14 = (f32[1024,128]{1,0:T(8,128)S(1)}, f32[1024,128]{1,0:T(8,128)S(1)}, u32[]{:S(2)}, u32[]{:S(2)}) collective-permute-start(f32[1024,128]{1,0:T(8,128)S(1)} %maximum_bitcast_fusion.1.refs_3_.refs_16_), channel_id=1, source_target_pairs={{3,1},{4,6},{11,9},{12,14},{19,17},{20,22},{27,25},{28,30}} | collective-permute-start | bytes 1572872 | tf_op jit(solution)/shard_map/ppermute | solution.py:311
  117.4 0.7 collective-permute-start.15
  118.5 0.7 collective-permute-start.16
  119.5 0.7 collective-permute-start.17
  120.6 0.7 collective-permute-start.18
  121.6 0.7 collective-permute-start.19
  122.7 0.7 collective-permute-start.20
  123.7 6.8 %collective-permute-start.21 = (f32[8,128]{1,0:T(8,128)S(1)}, f32[8,128]{1,0:T(8,128)S(1)}, u32[]{:S(2)}, u32[]{:S(2)}) collective-permute-start(f32[8,128]{1,0:T(8,128)S(1)} %hop.13), channel_id=1, source_target_pairs={{25,30}} | collective-permute-start | bytes 12296 | tf_op jit(solution)/shard_map/ppermute | solution.py:367
  135.6 0.7 collective-permute-start.22
  136.3 11.6 %collective-permute-start.23 = (f32[1,17,128]{2,1,0:T(8,128)S(1)}, f32[1,17,128]{2,1,0:T(8,128)S(1)}, u32[]{:S(2)}, u32[]{:S(2)}) collective-permute-start(f32[1,17,128]{2,1,0:T(8,128)S(1)} %slice.93), channel_id=1, source_target_pairs={{1,0},{2,3},{6,7},{5,4},{9,8},{10,11},{14,15},{13,12},{17,16},{18,... | collective-permute-start | bytes 26120 | tf_op jit(solution)/shard_map/ppermute | solution.py:392
  147.9 2.8 %collective-permute-start.24 = (f32[1,128]{1,0:T(1,128)S(1)}, f32[1,128]{1,0:T(1,128)S(1)}, u32[]{:S(2)}, u32[]{:S(2)}) collective-permute-start(f32[1,128]{1,0:T(1,128)S(1)} %fusion.1), channel_id=1, source_target_pairs={{0,4},{4,0},{8,12},{12,8},{16,20},{20,16},{24,28},{28,24},{1,5},{5... | collective-permute-start | bytes 1544 | tf_op jit(solution)/shard_map/ppermute | solution.py:402
  150.7 8.5 %collective-permute-start.25 = (f32[1,128]{1,0:T(1,128)S(1)}, f32[1,128]{1,0:T(1,128)S(1)}, u32[]{:S(2)}, u32[]{:S(2)}) collective-permute-start(f32[1,128]{1,0:T(1,128)S(1)} %add.61), channel_id=1, source_target_pairs={{0,8},{4,12},{8,0},{12,4},{16,24},{20,28},{24,16},{28,20},{1,9},{5... | collective-permute-start | bytes 1544 | tf_op jit(solution)/shard_map/ppermute | solution.py:402
  159.2 11.9 %collective-permute-start.26 = (f32[1,128]{1,0:T(1,128)S(1)}, f32[1,128]{1,0:T(1,128)S(1)}, u32[]{:S(2)}, u32[]{:S(2)}) collective-permute-start(f32[1,128]{1,0:T(1,128)S(1)} %add.62), channel_id=1, source_target_pairs={{0,16},{4,20},{8,24},{12,28},{16,0},{20,4},{24,8},{28,12},{1,17},{... | collective-permute-start | bytes 1544 | tf_op jit(solution)/shard_map/ppermute | solution.py:402
  (24 other events, 134.6 us)

commit v5 on v4

--- a/solution.py
+++ b/solution.py
@@ -10,8 +10,8 @@
 ORDER = 4
 LANES = 128
 CHUNKS = (1, 2, 2, 2, 1)
+STAGED = 2
 VMEM = pl.BlockSpec(memory_space=pltpu.VMEM)
-UNROLL = 8
 HBM = pl.BlockSpec(memory_space=pltpu.HBM)
 SMEM = pl.BlockSpec(memory_space=pltpu.SMEM)
 
@@ -45,33 +45,40 @@
     high, low, refs = refs[0], refs[1], refs[2:]
     if last:
         whole, refs = refs[0], refs[1:]
-    through, seen, store, sems = refs
+    through, seen, refs = refs[0], refs[1], refs[2:]
+    if not last:
+        store, sems = refs
     width, columns = high.shape
-    pack_rows = store.shape[2]
+    pack_rows = held * (nonzero + 1) * LANES
     gain_row = held * nonzero * LANES
 
     def fetch(s, t):
         rows = pl.ds(t * pack_rows, pack_rows)
         return pltpu.make_async_copy(packs[s].at[rows, :], store.at[s, t], sems.at[s, t])
 
-    for t in range(steps):
-        for s in range(slots):
-            fetch(s, t).start()
-    if first:
-        rows = lax.broadcasted_iota(jnp.int32, (width, columns), 0)
-        cols = lax.broadcasted_iota(jnp.int32, (width, columns), 1)
-        high[...] = (rows == cols).astype(jnp.float32).astype(jnp.bfloat16)
-        low[...] = jnp.zeros_like(low)
-
+    def load(s, t, at):
+        if last:
+            return packs[s][pl.ds(t * pack_rows + at.start, at.size), :]
+        return store[s, t, at, :]
+
+    if not last:
+        for t in range(steps):
+            for s in range(slots):
+                fetch(s, t).start()
     def step(t, carry):
-        for s in range(slots):
-            fetch(s, t).wait()
-
-        def block_row(i, carry):
-            s, h = i // held, i % held
+        if not last:
+            for s in range(slots):
+                fetch(s, t).wait()
+
+        def block_row(s, h):
             row = held * places[s] + h
             picks = [aligned(pattern[base + t, row * nonzero + j]) for j in range(nonzero)]
-            parts = [split(store[s, t, aligned(h * nonzero + j), :]) for j in range(nonzero)]
+            if first:
+                for j in range(nonzero):
+                    block = load(s, t, aligned(h * nonzero + j))
+                    through[aligned(row), picks[j]] = through[aligned(row), picks[j]] + block
+                return
+            parts = [split(load(s, t, aligned(h * nonzero + j))) for j in range(nonzero)]
             up = [p[0] for p in parts]
             down = [p[1] for p in parts]
             tops = [high[pick, :] for pick in picks]
@@ -80,9 +87,12 @@
                 jnp.concatenate(up + down + up, axis=1),
                 jnp.concatenate(tops + tops + bottoms),
             )
-            return carry
-
-        lax.fori_loop(0, slots * held, block_row, 0, unroll=UNROLL)
+
+        if first:
+            through[...] = jnp.zeros_like(through)
+        for s in range(slots):
+            for h in range(held):
+                block_row(s, h)
 
         def pick_rows(i, carry):
             for u in range(32):
@@ -96,7 +106,7 @@
         offset = pl.ds(width, LANES)
         seen[:, offset] = seen[:, offset] - jnp.where(lane == 0, target, 0.0)
         top, bottom = split(seen[...])
-        halves = [split(store[s, t, pl.ds(gain_row, held * LANES), :]) for s in range(slots)]
+        halves = [split(load(s, t, pl.ds(gain_row, held * LANES))) for s in range(slots)]
         left = jnp.concatenate([jnp.concatenate([a, b, a], axis=1) for a, b in halves])
         moved = matmul(left, jnp.concatenate([top, top, bottom]))
         for s in range(slots):
@@ -134,15 +144,18 @@
 
     done = pl.pallas_call(
         body,
-        in_specs=[SMEM] * 3 + [HBM] * slots + [VMEM] * (1 + len(state)),
+        in_specs=[SMEM] * 3 + [VMEM if last else HBM] * slots + [VMEM] * (1 + len(state)),
         out_specs=[VMEM] * len(out_shape),
         out_shape=out_shape,
         scratch_shapes=[
             pltpu.VMEM((width, columns), jnp.float32),
             pltpu.VMEM((LANES, columns), jnp.float32),
+        ]
+        + [
             pltpu.VMEM((slots, steps, pack_rows, LANES), jnp.float32),
             pltpu.SemaphoreType.DMA((slots, steps)),
-        ],
+        ]
+        * (not last),
         cost_estimate=pl.CostEstimate(
             flops=steps * 2 * width * columns * 3 * (nonzero + 1) * LANES,
             transcendentals=0,
@@ -151,7 +164,7 @@
         input_output_aliases={} if first else {slots + 4: 0, slots + 5: 1},
         compiler_params=pltpu.CompilerParams(vmem_limit_bytes=36 << 20),
         name="compose",
-    )(places, pattern, sites, *[in_hbm(p) for p in packs], targets, *state)
+    )(places, pattern, sites, *[p if last else in_hbm(p) for p in packs], targets, *state)
     return done[2] if last else done
 
 
@@ -171,37 +184,38 @@
         in_specs=[VMEM, VMEM],
         out_specs=VMEM,
         out_shape=jax.ShapeDtypeStruct(start.shape, jnp.float32),
-        compiler_params=pltpu.CompilerParams(vmem_limit_bytes=8 << 20),
+        compiler_params=pltpu.CompilerParams(vmem_limit_bytes=2 << 20),
         name="hop",
     )(whole, start)
 
 
-def stage_kernel(slots, sizes, *refs):
-    packs, store, sems = refs[: slots * len(sizes)], refs[-2], refs[-1]
-    rows = store.shape[2]
-    copies, t = [], 0
+def fetches(packs, sizes, slots, store, sems):
+    rows, steps = store.shape[2], []
     for c, size in enumerate(sizes):
         for i in range(size):
-            for s in range(slots):
-                copies.append(
+            t = len(steps)
+            steps.append(
+                [
                     pltpu.make_async_copy(
                         packs[c * slots + s].at[pl.ds(i * rows, rows), :],
                         store.at[s, t],
                         sems.at[s, t],
                     )
-                )
-            t += 1
-    for copy in copies:
-        copy.start()
-    for copy in copies:
-        copy.wait()
+                    for s in range(slots)
+                ]
+            )
+    return [copy for step in steps for copy in step]
 
 
 def stage(sizes, pack_rows, packs, after):
     slots, steps = len(packs[0]), sum(sizes)
 
     def body(*refs):
-        stage_kernel(slots, sizes, *refs)
+        copies = fetches(refs, sizes, slots, refs[-2], refs[-1])
+        for copy in copies:
+            copy.start()
+        for copy in copies:
+            copy.wait()
 
     shape = (slots, steps, pack_rows, LANES)
     return pl.pallas_call(
@@ -218,63 +232,101 @@
     )(*[in_hbm(p) for pack in packs for p in pack], after)
 
 
-def segment_kernel(held, nonzero, places, pattern, owner, store, *refs):
-    targets, sites, weights, start, parcels, mean, predicted = refs
-    slots, steps = store.shape[:2]
-    blocks = start.shape[0]
-    gain_row = held * nonzero * LANES
+def segment_kernel(held, nonzero, sizes, slots, places, pattern, owner, store, *refs):
+    packs, refs = refs[: slots * len(sizes)], refs[slots * len(sizes) :]
+    targets, sites, weights, start, parcels, mean, predicted, rest, sems = refs
+    near, far = store.shape[1], rest.shape[1]
+    for copy in fetches(packs, sizes, slots, rest, sems):
+        copy.start()
     mean[...] = start[...]
     mine = owner[0] == 1
 
-    def step(t, misfit):
+    def step(t, misfit, load):
+        innovation = filter_step(
+            t, held, nonzero, places, pattern, load, targets, sites, mean, predicted
+        )
         for s in range(slots):
             for h in range(held):
-                row = held * places[s] + h
-                total = None
-                for j in range(nonzero):
-                    column = pattern[t, row * nonzero + j]
-                    block = store[s, t, pl.ds((h * nonzero + j) * LANES, LANES), :]
-                    part = block * mean[pl.ds(column, 1), :]
-                    total = part if total is None else total + part
-                predicted[pl.ds(row, 1), :] = lane_sums(total)
-        flat = ORDER * sites[pl.ds(t, 1), :]
-        lane = jnp.broadcast_to(flat % LANES, (blocks, LANES))
-        picked = jnp.take_along_axis(predicted[...], lane, axis=1)
-        block = lax.broadcasted_iota(jnp.int32, (blocks, LANES), 0)
-        picked = jnp.where(block == flat // LANES, picked, 0.0)
-        innovation = targets[pl.ds(t, 1), :] - jnp.sum(picked, axis=0, keepdims=True)
+                row = mean[pl.ds(held * places[s] + h, 1), :]
+                parcels[s, pl.ds(t * held + h, 1), :] = jnp.where(mine, row, 0.0)
+        return misfit + innovation * innovation * weights[pl.ds(t, 1), :]
+
+    def near_step(t, misfit):
+        return step(t, misfit, lambda s, at: store[s, t, at, :])
+
+    def far_step(t, misfit):
         for s in range(slots):
-            for h in range(held):
-                row = held * places[s] + h
-                moved = store[s, t, pl.ds(gain_row + h * LANES, LANES), :] * innovation
-                updated = predicted[pl.ds(row, 1), :] + lane_sums(moved)
-                mean[pl.ds(row, 1), :] = updated
-                parcels[s, pl.ds(t * held + h, 1), :] = jnp.where(mine, updated, 0.0)
-        return misfit + innovation * innovation * weights[pl.ds(t, 1), :]
-
-    misfit = lax.fori_loop(0, steps, step, jnp.zeros((1, LANES), jnp.float32))
+            rows = pl.ds(0, rest.shape[2])
+            pltpu.make_async_copy(packs[s].at[rows, :], rest.at[s, t], sems.at[s, t]).wait()
+        return step(near + t, misfit, lambda s, at: rest[s, t, at, :])
+
+    misfit = lax.fori_loop(0, near, near_step, jnp.zeros((1, LANES), jnp.float32))
+    misfit = lax.fori_loop(0, far, far_step, misfit)
     for s in range(slots):
-        parcels[s, pl.ds(steps * held, 1), :] = jnp.where(mine, misfit, 0.0)
-
-
-def run_segment(held, nonzero, places, pattern, owner, store, targets, sites, weights, start):
-    slots, steps = store.shape[:2]
+        parcels[s, pl.ds((near + far) * held, 1), :] = jnp.where(mine, misfit, 0.0)
+
+
+def run_segment(
+    held, nonzero, sizes, places, pattern, owner, store, packs, targets, sites, weights, start
+):
+    slots, near, rows = store.shape[:3]
+    far = sum(sizes)
 
     def body(*refs):
-        segment_kernel(held, nonzero, *refs)
+        segment_kernel(held, nonzero, sizes, slots, *refs)
 
     return pl.pallas_call(
         body,
-        in_specs=[SMEM] * 3 + [VMEM] * 5,
+        in_specs=[SMEM] * 3 + [VMEM] + [HBM] * (slots * len(sizes)) + [VMEM] * 4,
         out_specs=VMEM,
-        out_shape=jax.ShapeDtypeStruct((slots, steps * held + 1, LANES), jnp.float32),
+        out_shape=jax.ShapeDtypeStruct((slots, (near + far) * held + 1, LANES), jnp.float32),
         scratch_shapes=[
             pltpu.VMEM(start.shape, jnp.float32),
             pltpu.VMEM(start.shape, jnp.float32),
+            pltpu.VMEM((slots, far, rows, LANES), jnp.float32),
+            pltpu.SemaphoreType.DMA((slots, far)),
         ],
-        compiler_params=pltpu.CompilerParams(vmem_limit_bytes=24 << 20),
+        compiler_params=pltpu.CompilerParams(vmem_limit_bytes=32 << 20),
         name="segment",
-    )(places, pattern, owner, store, targets, sites, weights, start)
+    )(
+        places,
+        pattern,
+        owner,
+        store,
+        *[in_hbm(p) for pack in packs for p in pack],
+        targets,
+        sites,
+        weights,
+        start,
+    )
+
+
+def filter_step(t, held, nonzero, places, pattern, load, targets, sites, mean, predicted):
+    blocks = mean.shape[0]
+    slots = blocks // held
+    for s in range(slots):
+        for h in range(held):
+            row = held * places[s] + h
+            total = None
+            for j in range(nonzero):
+                column = pattern[t, row * nonzero + j]
+                block = load(s, pl.ds((h * nonzero + j) * LANES, LANES))
+                part = block * mean[pl.ds(column, 1), :]
+                total = part if total is None else total + part
+            predicted[pl.ds(row, 1), :] = lane_sums(total)
+    flat = ORDER * sites[pl.ds(t, 1), :]
+    lane = jnp.broadcast_to(flat % LANES, (blocks, LANES))
+    picked = jnp.take_along_axis(predicted[...], lane, axis=1)
+    block = lax.broadcasted_iota(jnp.int32, (blocks, LANES), 0)
+    picked = jnp.where(block == flat // LANES, picked, 0.0)
+    innovation = targets[pl.ds(t, 1), :] - jnp.sum(picked, axis=0, keepdims=True)
+    for s in range(slots):
+        for h in range(held):
+            row = held * places[s] + h
+            gain = load(s, pl.ds((held * nonzero + h) * LANES, LANES))
+            updated = predicted[pl.ds(row, 1), :] + lane_sums(gain * innovation)
+            mean[pl.ds(row, 1), :] = updated
+    return innovation
 
 
 def on_device(
@@ -351,9 +403,10 @@
             state,
         )
         base += size
-        if i + 2 < len(sizes):
-            packs[i + 2], *state = lax.optimization_barrier((packs[i + 2], *state))
-            packs[i + 2] = meet(packs[i + 2])
+        for k in (i + 2, i + 3):
+            if k == i + 2 < len(sizes) - 1 or k == i + 3 == len(sizes) - 1:
+                packs[k], *state = lax.optimization_barrier((packs[k], *state))
+                packs[k] = meet(packs[k])
 
     starts = [p[sizes[0] * pack_rows :][:held] for p in packs[0]]
     by_even = [starts[order_even.index(z)] for z in range(rows)]
@@ -366,16 +419,17 @@
         ended = hop(state, mean)
         mean = lax.ppermute(ended, both, pair)
         begin = begin + mean
-        if t == min(2, segments - 2):
-            store = stage(sizes, pack_rows, packs, ended)
+    store = stage(sizes[:STAGED], pack_rows, packs[:STAGED], ended)
     owner = (row == places[:1]).astype(jnp.int32)
     local = run_segment(
         held,
         nonzero,
+        sizes[STAGED:],
         places,
         flat_pattern,
         owner,
         store,
+        packs[STAGED:],
         targets,
         sites,
         1.0 / variances,

time: 174 us -> 169 us (0.971)
  Pallas kernels: 73.4 us -> 65.8 us
  waiting for transfers between devices: 21 us -> 26.2 us
  local copies, waits for them, and re-layouts: 13.3 us -> 9.74 us
    pallas_call x6, Pallas kernels: 64.8 us -> 60.3 us  [the longest x5 55 us: compose(): pl.pallas_call(body, in_specs=[SMEM] * 3 + [VMEM if last else HBM] * slot...]
    ppermute x15, waiting for transfers between devices: 7.39 us -> 11.9 us  [meet(): moved.append(lax.ppermute(shard, both, pairs))]
    unnamed x57 -> x53, local copies, waits for them, and re-layouts: 6.27 us -> 2.32 us
    pallas_call x1, Pallas kernels: 6.06 us -> 2.88 us  [stage(): pl.pallas_call(body, in_specs=[HBM] * (slots * len(sizes)) + [VMEM], out_...]
  transfers between devices with their start and end apart: 27 -> 27, of which waited for: 7 -> 8; matrix products, arithmetic and copies ran while one was open for 2% -> 3% of each run, Pallas kernels for 33% -> 30%
where the time goes in v5:
time: 169 us; the launch traced here: 168 us
  Pallas kernels  65.8 us (39%)
  starting transfers between devices  60.6 us (36%)
  waiting for transfers between devices  26.2 us (16%)
  local copies, waits for them, and re-layouts  9.74 us (6%)
  between operations  3.87 us (2%)
  other arithmetic  1.96 us (1%)
    pallas_call x5, Pallas kernels, compose(): pl.pallas_call(body, in_specs=[SMEM] * 3 + [VMEM if last else HBM] * slot...  55 us
    ppermute x15, starting transfers between devices, meet(): moved.append(lax.ppermute(shard, both, pairs))  34.7 us
    ppermute x3, starting transfers between devices, on_device(): lax.ppermute(term, 'tm', [(t, t ^ reach) for t in range(segments)])  19.2 us
    ppermute x15, waiting for transfers between devices, meet(): moved.append(lax.ppermute(shard, both, pairs))  11.9 us
    ppermute x2, waiting for transfers between devices, on_device(): local = local[:half] + lax.ppermute(local[half:], both, pairs)  11.1 us
    pallas_call x1, Pallas kernels, run_segment(): pl.pallas_call(body, in_specs=[SMEM] * 3 + [VMEM] + [HBM] * (slots * len(...  5.35 us
    ppermute x7, starting transfers between devices, on_device(): mean = lax.ppermute(ended, both, pair)  4.85 us
  transfers between devices with their start and end apart: 27, of which 8 were waited for; matrix products, arithmetic and copies ran while one was open for 3% of the time, Pallas kernels for 30%

profile of v5, /device:TPU:0, one launch (start us, length us, event | category | flops | bytes accessed | tf_op | source)
XLA Modules:
  0.0 168.2 jit_solution(12526164015034221076)
XLA Ops:
  0.6 2.1 %fusion.3 = (f32[1,2,3,128,128]{4,3,2,1,0:T(8,128)}, f32[1,2,3,128,128]{4,3,2,1,0:T(8,128)S(1)}) fusion(f32[8,2,3,128,128]{4,3,2,1,0:T(8,128)} %param.13), kind=kLoop, calls=%fused_computation.20 | loop fusion | bytes 1572864 | tf_op jit(solution)/shard_map/slice | solution.py:379
  2.8 1.6 fusion.5
  4.5 5.9 %collective-permute-start = (f32[1032,128]{1,0:T(8,128)S(1)}, f32[1032,128]{1,0:T(8,128)}, u32[]{:S(2)}, u32[]{:S(2)}) collective-permute-start(f32[1032,128]{1,0:T(8,128)S(1)} %select_maximum_fusion.refs_3_.refs_0_), channel_id=1, source_target_pairs={{0,1},{7,6},{8,9},{15,14},{16,17},{23,22},{24,25},{31,30}} | collective-permute-start | bytes 1585160 | tf_op jit(solution)/shard_map/ppermute | solution.py:363
  10.4 1.5 collective-permute-start.1
  11.9 1.5 collective-permute-start.2
  14.4 2.3 %collective-permute-start.3 = (f32[2048,128]{1,0:T(8,128)S(1)}, f32[2048,128]{1,0:T(8,128)}, u32[]{:S(2)}, u32[]{:S(2)}) collective-permute-start(f32[2048,128]{1,0:T(8,128)S(1)} %bitcast.27), channel_id=1, source_target_pairs={{0,1},{7,6},{8,9},{15,14},{16,17},{23,22},{24,25},{31,30}} | collective-permute-start | bytes 3145736 | tf_op jit(solution)/shard_map/ppermute | solution.py:363
  16.7 1.6 collective-permute-start.4
  20.2 1.0 pad_maximum_fusion.2
  21.3 5.0 %compose.5 = (bf16[1024,1152]{1,0:T(8,128)(2,1)S(1)}, bf16[1024,1152]{1,0:T(8,128)(2,1)S(1)}) custom-call(s32[4]{0:T(128)S(1)} %broadcast_select_fusion.refs_0_, s32[8,24]{1,0:T(8,128)S(1)} %copy.27.refs_1_, s32[8,128]{1,0:T(8,128)S(1)} %copy-done.4, f32[1032,128]{1,0:T(8,128)} %copy-done.9, f32[1032,128]{1,0:T(8,128)} %collective-permute-done.refs_4_.refs_1_, ...), custom_call_target="tpu_custom_call" | custom-call | flops 3623878656 | bytes 2097152 | tf_op jit(solution)/shard_map/compose/pallas_call | solution.py:145
  26.3 8.8 %collective-permute-start.12 = (f32[2048,128]{1,0:T(8,128)S(1)}, f32[2048,128]{1,0:T(8,128)S(1)}, u32[]{:S(2)}, u32[]{:S(2)}) collective-permute-start(f32[2048,128]{1,0:T(8,128)S(1)} %bitcast.32), channel_id=1, source_target_pairs={{0,1},{7,6},{8,9},{15,14},{16,17},{23,22},{24,25},{31,30}} | collective-permute-start | bytes 3145736 | tf_op jit(solution)/shard_map/ppermute | solution.py:363
  35.2 0.9 collective-permute-start.13
  36.1 5.8 %collective-permute-done.3.refs_4_.refs_5_ = f32[2048,128]{1,0:T(8,128)} collective-permute-done((f32[2048,128]{1,0:T(8,128)S(1)}, f32[2048,128]{1,0:T(8,128)}, u32[]{:S(2)}, u32[]{:S(2)}) %collective-permute-start.3) | collective-permute-done | bytes 1048608 | tf_op jit(solution)/shard_map/ppermute | solution.py:363
  42.7 1.0 copy-done.11
  43.6 14.4 %compose.6 = (bf16[1024,1152]{1,0:T(8,128)(2,1)S(1)}, bf16[1024,1152]{1,0:T(8,128)(2,1)S(1)}) custom-call(s32[4]{0:T(128)S(1)} %broadcast_select_fusion.refs_0_, s32[8,24]{1,0:T(8,128)S(1)} %copy.27.refs_1_, s32[8,128]{1,0:T(8,128)S(1)} %copy-done.4, f32[2048,128]{1,0:T(8,128)} %bitcast.30, ...), custom_call_target="tpu_custom_call", output_to_operand_aliasing={{0}: (8, {}), {1}: (9, {})} | custom-call | flops 7247757312 | bytes 4194304 | tf_op jit(solution)/shard_map/compose/pallas_call | solution.py:145
  59.5 4.9 %collective-permute-done.12.refs_4_.refs_5_ = f32[2048,128]{1,0:T(8,128)S(1)} collective-permute-done((f32[2048,128]{1,0:T(8,128)S(1)}, f32[2048,128]{1,0:T(8,128)S(1)}, u32[]{:S(2)}, u32[]{:S(2)}) %collective-permute-start.12) | collective-permute-done | bytes 1048608 | tf_op jit(solution)/shard_map/ppermute | solution.py:363
  64.4 6.5 %collective-permute-start.9 = (f32[2048,128]{1,0:T(8,128)S(1)}, f32[2048,128]{1,0:T(8,128)S(1)}, u32[]{:S(2)}, u32[]{:S(2)}) collective-permute-start(f32[2048,128]{1,0:T(8,128)S(1)} %bitcast.39), channel_id=1, source_target_pairs={{0,1},{7,6},{8,9},{15,14},{16,17},{23,22},{24,25},{31,30}} | collective-permute-start | bytes 3145736 | tf_op jit(solution)/shard_map/ppermute | solution.py:363
  73.0 1.3 collective-permute-start.6
  74.4 0.9 collective-permute-start.7
  75.4 14.4 %compose.7 = (bf16[1024,1152]{1,0:T(8,128)(2,1)S(1)}, bf16[1024,1152]{1,0:T(8,128)(2,1)S(1)}) custom-call(s32[4]{0:T(128)S(1)} %broadcast_select_fusion.refs_0_, s32[8,24]{1,0:T(8,128)S(1)} %copy.27.refs_1_, s32[8,128]{1,0:T(8,128)S(1)} %copy-done.4, f32[2048,128]{1,0:T(8,128)} %bitcast.35, ...), custom_call_target="tpu_custom_call", output_to_operand_aliasing={{0}: (8, {}), {1}: (9, {})} | custom-call | flops 7247757312 | bytes 4194304 | tf_op jit(solution)/shard_map/compose/pallas_call | solution.py:145
  91.5 0.9 copy-done.17
  92.4 14.4 %compose.8 = (bf16[1024,1152]{1,0:T(8,128)(2,1)S(1)}, bf16[1024,1152]{1,0:T(8,128)(2,1)S(1)}) custom-call(s32[4]{0:T(128)S(1)} %broadcast_select_fusion.refs_0_, s32[8,24]{1,0:T(8,128)S(1)} %copy.27.refs_1_, s32[8,128]{1,0:T(8,128)S(1)} %copy-done.4, f32[2048,128]{1,0:T(8,128)} %bitcast.40, ...), custom_call_target="tpu_custom_call", output_to_operand_aliasing={{0}: (8, {}), {1}: (9, {})} | custom-call | flops 7247757312 | bytes 4194304 | tf_op jit(solution)/shard_map/compose/pallas_call | solution.py:145
  106.9 6.9 %compose.9 = (bf16[1024,1152]{1,0:T(8,128)(2,1)S(1)}, bf16[1024,1152]{1,0:T(8,128)(2,1)S(1)}, f32[1024,1152]{1,0:T(8,128)S(1)}) custom-call(s32[4]{0:T(128)S(1)} %broadcast_select_fusion.refs_0_, s32[8,24]{1,0:T(8,128)S(1)} %copy.27.refs_1_, s32[8,128]{1,0:T(8,128)S(1)} %copy-done.4, ...), custom_call_target="tpu_custom_call", output_to_operand_aliasing={{0}: (8, {}), {1}: (9, {})} | custom-call | flops 3623878656 | bytes 2097152 | tf_op jit(solution)/shard_map/compose/pallas_call | solution.py:145
  117.3 0.9 collective-permute-start.18
  121.4 2.9 %stage.1.refs_3_ = f32[4,3,1024,128]{3,2,1,0:T(8,128)S(1)} custom-call(f32[1032,128]{1,0:T(8,128)} %copy-done.9, f32[1032,128]{1,0:T(8,128)} %collective-permute-done.refs_4_.refs_1_, f32[1032,128]{1,0:T(8,128)} %collective-permute-done.1.refs_5_.refs_2_, f32[1032,128]{1,0:T(8,128)} %collective-permute-done.2.refs_6_.refs_3_, f32[2048,128]{1,0:T(8,128)} %bitcast.31, ...), custom_call_target="tpu_custom_call" | custom-call | bytes 12582912 | tf_op jit(solution)/shard_map/stage/pallas_call | solution.py:221
  124.3 5.4 %segment.1 = f32[4,17,128]{2,1,0:T(8,128)S(1)} custom-call(s32[4]{0:T(128)S(1)} %broadcast_select_fusion.refs_0_, s32[8,24]{1,0:T(8,128)S(1)} %copy.27.refs_1_, s32[1]{0:T(128)S(6)} %convert_element_type.5.refs_2_, f32[4,3,1024,128]{3,2,1,0:T(8,128)S(1)} %stage.1.refs_3_, f32[2048,128]{1,0:T(8,128)} %bitcast.36, f32[2048,128]{1,0:T(8,128)} %copy-done.12, ...), custom_call_target="tpu_custom_call" | custom-call | tf_op jit(solution)/shard_map/segment/pallas_call | solution.py:278
  130.4 1.3 collective-permute-start.23
  131.7 11.1 %collective-permute-done.23 = f32[1,17,128]{2,1,0:T(8,128)S(1)} collective-permute-done((f32[1,17,128]{2,1,0:T(8,128)S(1)}, f32[1,17,128]{2,1,0:T(8,128)S(1)}, u32[]{:S(2)}, u32[]{:S(2)}) %collective-permute-start.23) | collective-permute-done | bytes 8736 | tf_op jit(solution)/shard_map/ppermute | solution.py:446
  142.8 2.0 %collective-permute-start.24 = (f32[1,128]{1,0:T(1,128)S(1)}, f32[1,128]{1,0:T(1,128)S(1)}, u32[]{:S(2)}, u32[]{:S(2)}) collective-permute-start(f32[1,128]{1,0:T(1,128)S(1)} %fusion.1), channel_id=1, source_target_pairs={{0,4},{4,0},{8,12},{12,8},{16,20},{20,16},{24,28},{28,24},{1,5},{5... | collective-permute-start | bytes 1544 | tf_op jit(solution)/shard_map/ppermute | solution.py:456
  145.6 6.8 %collective-permute-start.25 = (f32[1,128]{1,0:T(1,128)S(1)}, f32[1,128]{1,0:T(1,128)S(1)}, u32[]{:S(2)}, u32[]{:S(2)}) collective-permute-start(f32[1,128]{1,0:T(1,128)S(1)} %add.61), channel_id=1, source_target_pairs={{0,8},{4,12},{8,0},{12,4},{16,24},{20,28},{24,16},{28,20},{1,9},{5... | collective-permute-start | bytes 1544 | tf_op jit(solution)/shard_map/ppermute | solution.py:456
  152.4 1.5 collective-permute-done.25
  153.9 10.4 %collective-permute-start.26 = (f32[1,128]{1,0:T(1,128)S(1)}, f32[1,128]{1,0:T(1,128)S(1)}, u32[]{:S(2)}, u32[]{:S(2)}) collective-permute-start(f32[1,128]{1,0:T(1,128)S(1)} %add.62), channel_id=1, source_target_pairs={{0,16},{4,20},{8,24},{12,28},{16,0},{20,4},{24,8},{28,12},{1,17},{... | collective-permute-start | bytes 1544 | tf_op jit(solution)/shard_map/ppermute | solution.py:456
  164.9 0.9 collective-permute-done.26
  (118 shorter events, 17.8 us)
Async XLA Ops:
  4.5 14.9 %collective-permute-start = (f32[1032,128]{1,0:T(8,128)S(1)}, f32[1032,128]{1,0:T(8,128)}, u32[]{:S(2)}, u32[]{:S(2)}) collective-permute-start(f32[1032,128]{1,0:T(8,128)S(1)} %select_maximum_fusion.refs_3_.refs_0_), channel_id=1, source_target_pairs={{0,1},{7,6},{8,9},{15,14},{16,17},{23,22},{24,25},{31,30}} | collective-permute-start | bytes 1585160 | tf_op jit(solution)/shard_map/ppermute | solution.py:363
  10.4 10.9 %collective-permute-start.1 = (f32[1032,128]{1,0:T(8,128)S(1)}, f32[1032,128]{1,0:T(8,128)}, u32[]{:S(2)}, u32[]{:S(2)}) collective-permute-start(f32[1032,128]{1,0:T(8,128)S(1)} %select_maximum_fusion.refs_3_.refs_0_), channel_id=1, source_target_pairs={{2,1},{5,6},{10,9},{13,14},{18,17},{21,22},{26,25},{29,30}} | collective-permute-start | bytes 1585160 | tf_op jit(solution)/shard_map/ppermute | solution.py:363
  11.9 9.4 %collective-permute-start.2 = (f32[1032,128]{1,0:T(8,128)S(1)}, f32[1032,128]{1,0:T(8,128)}, u32[]{:S(2)}, u32[]{:S(2)}) collective-permute-start(f32[1032,128]{1,0:T(8,128)S(1)} %select_maximum_fusion.refs_3_.refs_0_), channel_id=1, source_target_pairs={{3,1},{4,6},{11,9},{12,14},{19,17},{20,22},{27,25},{28,30}} | collective-permute-start | bytes 1585160 | tf_op jit(solution)/shard_map/ppermute | solution.py:363
  14.4 27.5 %collective-permute-start.3 = (f32[2048,128]{1,0:T(8,128)S(1)}, f32[2048,128]{1,0:T(8,128)}, u32[]{:S(2)}, u32[]{:S(2)}) collective-permute-start(f32[2048,128]{1,0:T(8,128)S(1)} %bitcast.27), channel_id=1, source_target_pairs={{0,1},{7,6},{8,9},{15,14},{16,17},{23,22},{24,25},{31,30}} | collective-permute-start | bytes 3145736 | tf_op jit(solution)/shard_map/ppermute | solution.py:363
  16.7 26.0 %collective-permute-start.4 = (f32[2048,128]{1,0:T(8,128)S(1)}, f32[2048,128]{1,0:T(8,128)}, u32[]{:S(2)}, u32[]{:S(2)}) collective-permute-start(f32[2048,128]{1,0:T(8,128)S(1)} %bitcast.28), channel_id=1, source_target_pairs={{2,1},{5,6},{10,9},{13,14},{18,17},{21,22},{26,25},{29,30}} | collective-permute-start | bytes 3145736 | tf_op jit(solution)/shard_map/ppermute | solution.py:363
  19.4 23.2 %collective-permute-start.5 = (f32[2048,128]{1,0:T(8,128)S(1)}, f32[2048,128]{1,0:T(8,128)S(1)}, u32[]{:S(2)}, u32[]{:S(2)}) collective-permute-start(f32[2048,128]{1,0:T(8,128)S(1)} %bitcast.29), channel_id=1, source_target_pairs={{3,1},{4,6},{11,9},{12,14},{19,17},{20,22},{27,25},{28,30}} | collective-permute-start | bytes 3145736 | tf_op jit(solution)/shard_map/ppermute | solution.py:363
  21.2 20.7 %copy-start.6 = (f32[2,1024,128]{2,1,0:T(8,128)}, f32[2,1024,128]{2,1,0:T(8,128)S(1)}, u32[]{:S(2)}) copy-start(f32[2,1024,128]{2,1,0:T(8,128)S(1)} %pad_maximum_fusion.2) | copy-start | bytes 3145732
  26.3 38.1 %collective-permute-start.12 = (f32[2048,128]{1,0:T(8,128)S(1)}, f32[2048,128]{1,0:T(8,128)S(1)}, u32[]{:S(2)}, u32[]{:S(2)}) collective-permute-start(f32[2048,128]{1,0:T(8,128)S(1)} %bitcast.32), channel_id=1, source_target_pairs={{0,1},{7,6},{8,9},{15,14},{16,17},{23,22},{24,25},{31,30}} | collective-permute-start | bytes 3145736 | tf_op jit(solution)/shard_map/ppermute | solution.py:363
  35.2 29.2 %copy-start.7 = (f32[2,1024,128]{2,1,0:T(8,128)}, f32[2,1024,128]{2,1,0:T(8,128)S(1)}, u32[]{:S(2)}) copy-start(f32[2,1024,128]{2,1,0:T(8,128)S(1)} %pad_maximum_fusion.1) | copy-start | bytes 3145732
  35.2 35.7 %copy-start.10 = (f32[1,2,3,128,128]{4,3,2,1,0:T(8,128)S(1)}, f32[1,2,3,128,128]{4,3,2,1,0:T(8,128)}, u32[]{:S(2)}) copy-start(f32[1,2,3,128,128]{4,3,2,1,0:T(8,128)} %get-tuple-element.41) | copy-start | bytes 1179652
  35.2 35.7 %copy-start.19 = (f32[1,256,128]{2,1,0:T(8,128)S(1)}, f32[1,256,128]{2,1,0:T(8,128)}, u32[]{:S(2)}) copy-start(f32[1,256,128]{2,1,0:T(8,128)} %get-tuple-element.46) | copy-start | bytes 393220
  35.2 37.8 %collective-permute-start.13 = (f32[2048,128]{1,0:T(8,128)S(1)}, f32[2048,128]{1,0:T(8,128)S(1)}, u32[]{:S(2)}, u32[]{:S(2)}) collective-permute-start(f32[2048,128]{1,0:T(8,128)S(1)} %bitcast.33), channel_id=1, source_target_pairs={{2,1},{5,6},{10,9},{13,14},{18,17},{21,22},{26,25},{29,30}} | collective-permute-start | bytes 3145736 | tf_op jit(solution)/shard_map/ppermute | solution.py:363
  41.9 32.4 %collective-permute-start.14 = (f32[2048,128]{1,0:T(8,128)S(1)}, f32[2048,128]{1,0:T(8,128)S(1)}, u32[]{:S(2)}, u32[]{:S(2)}) collective-permute-start(f32[2048,128]{1,0:T(8,128)S(1)} %bitcast.34), channel_id=1, source_target_pairs={{3,1},{4,6},{11,9},{12,14},{19,17},{20,22},{27,25},{28,30}} | collective-permute-start | bytes 3145736 | tf_op jit(solution)/shard_map/ppermute | solution.py:363
  58.0 31.8 %collective-permute-start.10 = (f32[2048,128]{1,0:T(8,128)S(1)}, f32[2048,128]{1,0:T(8,128)S(1)}, u32[]{:S(2)}, u32[]{:S(2)}) collective-permute-start(f32[2048,128]{1,0:T(8,128)S(1)} %bitcast.37), channel_id=1, source_target_pairs={{2,1},{5,6},{10,9},{13,14},{18,17},{21,22},{26,25},{29,30}} | collective-permute-start | bytes 3145736 | tf_op jit(solution)/shard_map/ppermute | solution.py:363
  58.7 31.8 %collective-permute-start.11 = (f32[2048,128]{1,0:T(8,128)S(1)}, f32[2048,128]{1,0:T(8,128)S(1)}, u32[]{:S(2)}, u32[]{:S(2)}) collective-permute-start(f32[2048,128]{1,0:T(8,128)S(1)} %bitcast.38), channel_id=1, source_target_pairs={{3,1},{4,6},{11,9},{12,14},{19,17},{20,22},{27,25},{28,30}} | collective-permute-start | bytes 3145736 | tf_op jit(solution)/shard_map/ppermute | solution.py:363
  64.4 27.0 %collective-permute-start.9 = (f32[2048,128]{1,0:T(8,128)S(1)}, f32[2048,128]{1,0:T(8,128)S(1)}, u32[]{:S(2)}, u32[]{:S(2)}) collective-permute-start(f32[2048,128]{1,0:T(8,128)S(1)} %bitcast.39), channel_id=1, source_target_pairs={{0,1},{7,6},{8,9},{15,14},{16,17},{23,22},{24,25},{31,30}} | collective-permute-start | bytes 3145736 | tf_op jit(solution)/shard_map/ppermute | solution.py:363
  70.9 35.9 %copy-start = (f32[1024,128]{1,0:T(8,128)}, f32[1024,128]{1,0:T(8,128)S(1)}, u32[]{:S(2)}) copy-start(f32[1024,128]{1,0:T(8,128)S(1)} %maximum_bitcast_fusion.1.refs_3_.refs_12_) | copy-start | bytes 1572868
  73.0 33.8 %collective-permute-start.6 = (f32[1024,128]{1,0:T(8,128)S(1)}, f32[1024,128]{1,0:T(8,128)S(1)}, u32[]{:S(2)}, u32[]{:S(2)}) collective-permute-start(f32[1024,128]{1,0:T(8,128)S(1)} %maximum_bitcast_fusion.1.refs_3_.refs_12_), channel_id=1, source_target_pairs={{0,1},{7,6},{8,9},{15,14},{16,17},{23,22},{24,25},{31,30}} | collective-permute-start | bytes 1572872 | tf_op jit(solution)/shard_map/ppermute | solution.py:363
  74.4 32.5 %collective-permute-start.7 = (f32[1024,128]{1,0:T(8,128)S(1)}, f32[1024,128]{1,0:T(8,128)S(1)}, u32[]{:S(2)}, u32[]{:S(2)}) collective-permute-start(f32[1024,128]{1,0:T(8,128)S(1)} %maximum_bitcast_fusion.1.refs_3_.refs_12_), channel_id=1, source_target_pairs={{2,1},{5,6},{10,9},{13,14},{18,17},{21,22},{26,25},{29,30}} | collective-permute-start | bytes 1572872 | tf_op jit(solution)/shard_map/ppermute | solution.py:363
  89.8 17.1 %collective-permute-start.8 = (f32[1024,128]{1,0:T(8,128)S(1)}, f32[1024,128]{1,0:T(8,128)S(1)}, u32[]{:S(2)}, u32[]{:S(2)}) collective-permute-start(f32[1024,128]{1,0:T(8,128)S(1)} %maximum_bitcast_fusion.1.refs_3_.refs_12_), channel_id=1, source_target_pairs={{3,1},{4,6},{11,9},{12,14},{19,17},{20,22},{27,25},{28,30}} | collective-permute-start | bytes 1572872 | tf_op jit(solution)/shard_map/ppermute | solution.py:363
  114.2 0.7 collective-permute-start.15
  115.2 0.7 collective-permute-start.16
  116.3 0.7 collective-permute-start.17
  117.3 0.9 collective-permute-start.18
  118.6 0.7 collective-permute-start.19
  119.6 0.7 collective-permute-start.20
  120.7 3.6 %collective-permute-start.21 = (f32[8,128]{1,0:T(8,128)S(1)}, f32[8,128]{1,0:T(8,128)S(1)}, u32[]{:S(2)}, u32[]{:S(2)}) collective-permute-start(f32[8,128]{1,0:T(8,128)S(1)} %hop.13.refs_8_), channel_id=1, source_target_pairs={{25,30}} | collective-permute-start | bytes 12296 | tf_op jit(solution)/shard_map/ppermute | solution.py:420
  129.7 0.7 collective-permute-start.22
  130.4 12.4 %collective-permute-start.23 = (f32[1,17,128]{2,1,0:T(8,128)S(1)}, f32[1,17,128]{2,1,0:T(8,128)S(1)}, u32[]{:S(2)}, u32[]{:S(2)}) collective-permute-start(f32[1,17,128]{2,1,0:T(8,128)S(1)} %slice.93), channel_id=1, source_target_pairs={{1,0},{2,3},{6,7},{5,4},{9,8},{10,11},{14,15},{13,12},{17,16},{18,... | collective-permute-start | bytes 26120 | tf_op jit(solution)/shard_map/ppermute | solution.py:446
  142.8 2.8 %collective-permute-start.24 = (f32[1,128]{1,0:T(1,128)S(1)}, f32[1,128]{1,0:T(1,128)S(1)}, u32[]{:S(2)}, u32[]{:S(2)}) collective-permute-start(f32[1,128]{1,0:T(1,128)S(1)} %fusion.1), channel_id=1, source_target_pairs={{0,4},{4,0},{8,12},{12,8},{16,20},{20,16},{24,28},{28,24},{1,5},{5... | collective-permute-start | bytes 1544 | tf_op jit(solution)/shard_map/ppermute | solution.py:456
  145.6 8.3 %collective-permute-start.25 = (f32[1,128]{1,0:T(1,128)S(1)}, f32[1,128]{1,0:T(1,128)S(1)}, u32[]{:S(2)}, u32[]{:S(2)}) collective-permute-start(f32[1,128]{1,0:T(1,128)S(1)} %add.61), channel_id=1, source_target_pairs={{0,8},{4,12},{8,0},{12,4},{16,24},{20,28},{24,16},{28,20},{1,9},{5... | collective-permute-start | bytes 1544 | tf_op jit(solution)/shard_map/ppermute | solution.py:456
  153.9 11.9 %collective-permute-start.26 = (f32[1,128]{1,0:T(1,128)S(1)}, f32[1,128]{1,0:T(1,128)S(1)}, u32[]{:S(2)}, u32[]{:S(2)}) collective-permute-start(f32[1,128]{1,0:T(1,128)S(1)} %add.62), channel_id=1, source_target_pairs={{0,16},{4,20},{8,24},{12,28},{16,0},{20,4},{24,8},{28,12},{1,17},{... | collective-permute-start | bytes 1544 | tf_op jit(solution)/shard_map/ppermute | solution.py:456
  (21 other events, 123.3 us)

commit v6 on v5

--- a/solution.py
+++ b/solution.py
@@ -45,31 +45,16 @@
     high, low, refs = refs[0], refs[1], refs[2:]
     if last:
         whole, refs = refs[0], refs[1:]
-    through, seen, refs = refs[0], refs[1], refs[2:]
-    if not last:
-        store, sems = refs
+    through, seen = refs
     width, columns = high.shape
     pack_rows = held * (nonzero + 1) * LANES
     gain_row = held * nonzero * LANES
 
-    def fetch(s, t):
-        rows = pl.ds(t * pack_rows, pack_rows)
-        return pltpu.make_async_copy(packs[s].at[rows, :], store.at[s, t], sems.at[s, t])
-
     def load(s, t, at):
-        if last:
-            return packs[s][pl.ds(t * pack_rows + at.start, at.size), :]
-        return store[s, t, at, :]
-
-    if not last:
-        for t in range(steps):
-            for s in range(slots):
-                fetch(s, t).start()
+        start = pl.multiple_of(t * pack_rows + at.start, LANES)
+        return packs[s][pl.ds(start, at.size), :]
+
     def step(t, carry):
-        if not last:
-            for s in range(slots):
-                fetch(s, t).wait()
-
         def block_row(s, h):
             row = held * places[s] + h
             picks = [aligned(pattern[base + t, row * nonzero + j]) for j in range(nonzero)]
@@ -144,18 +129,13 @@
 
     done = pl.pallas_call(
         body,
-        in_specs=[SMEM] * 3 + [VMEM if last else HBM] * slots + [VMEM] * (1 + len(state)),
+        in_specs=[SMEM] * 3 + [VMEM] * (slots + 1 + len(state)),
         out_specs=[VMEM] * len(out_shape),
         out_shape=out_shape,
         scratch_shapes=[
             pltpu.VMEM((width, columns), jnp.float32),
             pltpu.VMEM((LANES, columns), jnp.float32),
-        ]
-        + [
-            pltpu.VMEM((slots, steps, pack_rows, LANES), jnp.float32),
-            pltpu.SemaphoreType.DMA((slots, steps)),
-        ]
-        * (not last),
+        ],
         cost_estimate=pl.CostEstimate(
             flops=steps * 2 * width * columns * 3 * (nonzero + 1) * LANES,
             transcendentals=0,
@@ -164,7 +144,7 @@
         input_output_aliases={} if first else {slots + 4: 0, slots + 5: 1},
         compiler_params=pltpu.CompilerParams(vmem_limit_bytes=36 << 20),
         name="compose",
-    )(places, pattern, sites, *[p if last else in_hbm(p) for p in packs], targets, *state)
+    )(places, pattern, sites, *packs, targets, *state)
     return done[2] if last else done
 
 

time: 169 us -> 165 us (0.976)
  Pallas kernels: 65.8 us -> 60.8 us
  waiting for transfers between devices: 26.2 us -> 30.8 us
  local copies, waits for them, and re-layouts: 9.74 us -> 6.74 us
    ppermute x15, waiting for transfers between devices: 11.9 us -> 16.9 us  [meet(): moved.append(lax.ppermute(shard, both, pairs))]
    pallas_call x5, Pallas kernels: 55 us -> 50 us  [compose(): pl.pallas_call(body, in_specs=[SMEM] * 3 + [VMEM] * (slots + 1 + len(stat...]
    unnamed x53 -> x61, local copies, waits for them, and re-layouts: 2.32 us -> 0.2 us
    slice x3, local copies, waits for them, and re-layouts: 2.04 us -> 0.01 us  [on_device(): starts = [p[sizes[0] * pack_rows:][:held] for p in packs[0]]]
  transfers between devices with their start and end apart: 27 -> 27, of which waited for: 8 -> 8; matrix products, arithmetic and copies ran while one was open for 3% -> 3% of each run, Pallas kernels for 30% -> 28%
where the time goes in v6:
time: 165 us; the launch traced here: 164 us
  Pallas kernels  60.8 us (37%)
  starting transfers between devices  59.3 us (36%)
  waiting for transfers between devices  30.8 us (19%)
  local copies, waits for them, and re-layouts  6.74 us (4%)
  between operations  4 us (2%)
  other arithmetic  2.22 us (1%)
    pallas_call x5, Pallas kernels, compose(): pl.pallas_call(body, in_specs=[SMEM] * 3 + [VMEM] * (slots + 1 + len(stat...  50 us
    ppermute x15, starting transfers between devices, meet(): moved.append(lax.ppermute(shard, both, pairs))  33.4 us
    ppermute x3, starting transfers between devices, on_device(): lax.ppermute(term, 'tm', [(t, t ^ reach) for t in range(segments)])  19.2 us
    ppermute x15, waiting for transfers between devices, meet(): moved.append(lax.ppermute(shard, both, pairs))  16.9 us
    ppermute x2, waiting for transfers between devices, on_device(): local = local[:half] + lax.ppermute(local[half:], both, pairs)  10.6 us
    pallas_call x1, Pallas kernels, run_segment(): pl.pallas_call(body, in_specs=[SMEM] * 3 + [VMEM] + [HBM] * (slots * len(...  5.35 us
    ppermute x7, starting transfers between devices, on_device(): mean = lax.ppermute(ended, both, pair)  4.85 us
    slice x2, local copies, waits for them, and re-layouts, on_device(): blocks = block_values[base:base + size].reshape(size, -1, LANES)  3.45 us
  transfers between devices with their start and end apart: 27, of which 8 were waited for; matrix products, arithmetic and copies ran while one was open for 3% of the time, Pallas kernels for 28%

profile of v6, /device:TPU:0, one launch (start us, length us, event | category | flops | bytes accessed | tf_op | source)
XLA Modules:
  0.0 163.9 jit_solution(11129500345101568540)
XLA Ops:
  0.6 2.1 %fusion.3 = (f32[1,2,3,128,128]{4,3,2,1,0:T(8,128)}, f32[1,2,3,128,128]{4,3,2,1,0:T(8,128)S(1)}) fusion(f32[8,2,3,128,128]{4,3,2,1,0:T(8,128)} %param.13), kind=kLoop, calls=%fused_computation.20 | loop fusion | bytes 1572864 | tf_op jit(solution)/shard_map/slice | solution.py:359
  2.8 1.6 fusion.5
  4.5 5.1 %collective-permute-start = (f32[1032,128]{1,0:T(8,128)S(1)}, f32[1032,128]{1,0:T(8,128)S(1)}, u32[]{:S(2)}, u32[]{:S(2)}) collective-permute-start(f32[1032,128]{1,0:T(8,128)S(1)} %select_maximum_fusion.refs_3_.refs_0_), channel_id=1, source_target_pairs={{0,1},{7,6},{8,9},{15,14},{16,17},{23,22},{24,25},{31,30}} | collective-permute-start | bytes 1585160 | tf_op jit(solution)/shard_map/ppermute | solution.py:343
  11.0 1.3 fusion.2
  12.4 0.8 fusion.4
  13.2 3.4 %collective-permute-start.3 = (f32[2048,128]{1,0:T(8,128)S(1)}, f32[2048,128]{1,0:T(8,128)}, u32[]{:S(2)}, u32[]{:S(2)}) collective-permute-start(f32[2048,128]{1,0:T(8,128)S(1)} %bitcast.26), channel_id=1, source_target_pairs={{0,1},{7,6},{8,9},{15,14},{16,17},{23,22},{24,25},{31,30}} | collective-permute-start | bytes 3145736 | tf_op jit(solution)/shard_map/ppermute | solution.py:343
  16.7 1.6 collective-permute-start.4
  20.1 1.3 pad_maximum_fusion.2
  21.6 3.4 %compose.5 = (bf16[1024,1152]{1,0:T(8,128)(2,1)S(1)}, bf16[1024,1152]{1,0:T(8,128)(2,1)S(1)}) custom-call(s32[4]{0:T(128)S(1)} %broadcast_select_fusion.refs_0_, s32[8,24]{1,0:T(8,128)S(1)} %copy.27.refs_1_, s32[8,128]{1,0:T(8,128)S(1)} %copy-done.18, f32[1032,128]{1,0:T(8,128)S(1)} %select_maximum_fusion.refs_3_.refs_0_, ...), custom_call_target="tpu_custom_call" | custom-call | flops 3623878656 | bytes 2097152 | tf_op jit(solution)/shard_map/compose/pallas_call | solution.py:130
  25.0 8.4 %collective-permute-start.12 = (f32[2048,128]{1,0:T(8,128)S(1)}, f32[2048,128]{1,0:T(8,128)S(1)}, u32[]{:S(2)}, u32[]{:S(2)}) collective-permute-start(f32[2048,128]{1,0:T(8,128)S(1)} %bitcast.31), channel_id=1, source_target_pairs={{0,1},{7,6},{8,9},{15,14},{16,17},{23,22},{24,25},{31,30}} | collective-permute-start | bytes 3145736 | tf_op jit(solution)/shard_map/ppermute | solution.py:343
  33.6 0.9 collective-permute-start.13
  34.4 7.5 %collective-permute-done.3.refs_4_.refs_5_ = f32[2048,128]{1,0:T(8,128)} collective-permute-done((f32[2048,128]{1,0:T(8,128)S(1)}, f32[2048,128]{1,0:T(8,128)}, u32[]{:S(2)}, u32[]{:S(2)}) %collective-permute-start.3) | collective-permute-done | bytes 1048608 | tf_op jit(solution)/shard_map/ppermute | solution.py:343
  42.6 14.1 %compose.6 = (bf16[1024,1152]{1,0:T(8,128)(2,1)S(1)}, bf16[1024,1152]{1,0:T(8,128)(2,1)S(1)}) custom-call(s32[4]{0:T(128)S(1)} %broadcast_select_fusion.refs_0_, s32[8,24]{1,0:T(8,128)S(1)} %copy.27.refs_1_, s32[8,128]{1,0:T(8,128)S(1)} %copy-done.18, f32[2048,128]{1,0:T(8,128)S(1)} %bitcast.29, ...), custom_call_target="tpu_custom_call", output_to_operand_aliasing={{0}: (8, {}), {1}: (9, {})} | custom-call | flops 7247757312 | bytes 4194304 | tf_op jit(solution)/shard_map/compose/pallas_call | solution.py:130
  58.2 6.1 %collective-permute-done.12.refs_4_.refs_5_ = f32[2048,128]{1,0:T(8,128)S(1)} collective-permute-done((f32[2048,128]{1,0:T(8,128)S(1)}, f32[2048,128]{1,0:T(8,128)S(1)}, u32[]{:S(2)}, u32[]{:S(2)}) %collective-permute-start.12) | collective-permute-done | bytes 1048608 | tf_op jit(solution)/shard_map/ppermute | solution.py:343
  64.4 5.1 %collective-permute-start.9 = (f32[2048,128]{1,0:T(8,128)S(1)}, f32[2048,128]{1,0:T(8,128)S(1)}, u32[]{:S(2)}, u32[]{:S(2)}) collective-permute-start(f32[2048,128]{1,0:T(8,128)S(1)} %bitcast.38), channel_id=1, source_target_pairs={{0,1},{7,6},{8,9},{15,14},{16,17},{23,22},{24,25},{31,30}} | collective-permute-start | bytes 3145736 | tf_op jit(solution)/shard_map/ppermute | solution.py:343
  69.7 2.9 %collective-permute-start.6 = (f32[1024,128]{1,0:T(8,128)S(1)}, f32[1024,128]{1,0:T(8,128)S(1)}, u32[]{:S(2)}, u32[]{:S(2)}) collective-permute-start(f32[1024,128]{1,0:T(8,128)S(1)} %maximum_bitcast_fusion.1.refs_3_.refs_12_), channel_id=1, source_target_pairs={{0,1},{7,6},{8,9},{15,14},{16,17},{23,22},{24,25},{31,30}} | collective-permute-start | bytes 1572872 | tf_op jit(solution)/shard_map/ppermute | solution.py:343
  72.6 0.9 collective-permute-start.7
  73.5 12.8 %compose.7 = (bf16[1024,1152]{1,0:T(8,128)(2,1)S(1)}, bf16[1024,1152]{1,0:T(8,128)(2,1)S(1)}) custom-call(s32[4]{0:T(128)S(1)} %broadcast_select_fusion.refs_0_, s32[8,24]{1,0:T(8,128)S(1)} %copy.27.refs_1_, s32[8,128]{1,0:T(8,128)S(1)} %copy-done.18, f32[2048,128]{1,0:T(8,128)S(1)} %bitcast.34, ...), custom_call_target="tpu_custom_call", output_to_operand_aliasing={{0}: (8, {}), {1}: (9, {})} | custom-call | flops 7247757312 | bytes 4194304 | tf_op jit(solution)/shard_map/compose/pallas_call | solution.py:130
  87.1 3.0 %collective-permute-done.9.refs_4_.refs_9_ = f32[2048,128]{1,0:T(8,128)S(1)} collective-permute-done((f32[2048,128]{1,0:T(8,128)S(1)}, f32[2048,128]{1,0:T(8,128)S(1)}, u32[]{:S(2)}, u32[]{:S(2)}) %collective-permute-start.9) | collective-permute-done | bytes 1048608 | tf_op jit(solution)/shard_map/ppermute | solution.py:343
  90.1 12.8 %compose.8 = (bf16[1024,1152]{1,0:T(8,128)(2,1)S(1)}, bf16[1024,1152]{1,0:T(8,128)(2,1)S(1)}) custom-call(s32[4]{0:T(128)S(1)} %broadcast_select_fusion.refs_0_, s32[8,24]{1,0:T(8,128)S(1)} %copy.27.refs_1_, s32[8,128]{1,0:T(8,128)S(1)} %copy-done.18, f32[2048,128]{1,0:T(8,128)S(1)} %bitcast.39, ...), custom_call_target="tpu_custom_call", output_to_operand_aliasing={{0}: (8, {}), {1}: (9, {})} | custom-call | flops 7247757312 | bytes 4194304 | tf_op jit(solution)/shard_map/compose/pallas_call | solution.py:130
  103.0 6.9 %compose.9 = (bf16[1024,1152]{1,0:T(8,128)(2,1)S(1)}, bf16[1024,1152]{1,0:T(8,128)(2,1)S(1)}, f32[1024,1152]{1,0:T(8,128)S(1)}) custom-call(s32[4]{0:T(128)S(1)} %broadcast_select_fusion.refs_0_, s32[8,24]{1,0:T(8,128)S(1)} %copy.27.refs_1_, s32[8,128]{1,0:T(8,128)S(1)} %copy-done.18, ...), custom_call_target="tpu_custom_call", output_to_operand_aliasing={{0}: (8, {}), {1}: (9, {})} | custom-call | flops 3623878656 | bytes 2097152 | tf_op jit(solution)/shard_map/compose/pallas_call | solution.py:130
  113.5 0.9 collective-permute-start.18
  117.5 2.9 %stage.1.refs_3_ = f32[4,3,1024,128]{3,2,1,0:T(8,128)S(1)} custom-call(f32[1032,128]{1,0:T(8,128)} %copy-done.3, f32[1032,128]{1,0:T(8,128)} %copy-done.12, f32[1032,128]{1,0:T(8,128)} %copy-done.13, f32[1032,128]{1,0:T(8,128)} %copy-done.14, f32[2048,128]{1,0:T(8,128)} %bitcast.30, f32[2048,128]{1,0:T(8,128)} %collective-permute-done.3.refs_4_.refs_5_, ...), custom_call_target="tpu_custom_call" | custom-call | bytes 12582912 | tf_op jit(solution)/shard_map/stage/pallas_call | solution.py:201
  120.5 5.4 %segment.1 = f32[4,17,128]{2,1,0:T(8,128)S(1)} custom-call(s32[4]{0:T(128)S(1)} %broadcast_select_fusion.refs_0_, s32[8,24]{1,0:T(8,128)S(1)} %copy.27.refs_1_, s32[1]{0:T(128)S(6)} %convert_element_type.5.refs_2_, f32[4,3,1024,128]{3,2,1,0:T(8,128)S(1)} %stage.1.refs_3_, f32[2048,128]{1,0:T(8,128)} %bitcast.35, f32[2048,128]{1,0:T(8,128)} %copy-done.6, ...), custom_call_target="tpu_custom_call" | custom-call | tf_op jit(solution)/shard_map/segment/pallas_call | solution.py:258
  126.5 1.3 collective-permute-start.23
  127.8 10.6 %collective-permute-done.23 = f32[1,17,128]{2,1,0:T(8,128)S(1)} collective-permute-done((f32[1,17,128]{2,1,0:T(8,128)S(1)}, f32[1,17,128]{2,1,0:T(8,128)S(1)}, u32[]{:S(2)}, u32[]{:S(2)}) %collective-permute-start.23) | collective-permute-done | bytes 8736 | tf_op jit(solution)/shard_map/ppermute | solution.py:426
  138.5 2.0 %collective-permute-start.24 = (f32[1,128]{1,0:T(1,128)S(1)}, f32[1,128]{1,0:T(1,128)S(1)}, u32[]{:S(2)}, u32[]{:S(2)}) collective-permute-start(f32[1,128]{1,0:T(1,128)S(1)} %fusion.1), channel_id=1, source_target_pairs={{0,4},{4,0},{8,12},{12,8},{16,20},{20,16},{24,28},{28,24},{1,5},{5... | collective-permute-start | bytes 1544 | tf_op jit(solution)/shard_map/ppermute | solution.py:436
  140.5 0.8 collective-permute-done.24
  141.3 6.8 %collective-permute-start.25 = (f32[1,128]{1,0:T(1,128)S(1)}, f32[1,128]{1,0:T(1,128)S(1)}, u32[]{:S(2)}, u32[]{:S(2)}) collective-permute-start(f32[1,128]{1,0:T(1,128)S(1)} %add.61), channel_id=1, source_target_pairs={{0,8},{4,12},{8,0},{12,4},{16,24},{20,28},{24,16},{28,20},{1,9},{5... | collective-permute-start | bytes 1544 | tf_op jit(solution)/shard_map/ppermute | solution.py:436
  148.1 1.5 collective-permute-done.25
  149.6 10.4 %collective-permute-start.26 = (f32[1,128]{1,0:T(1,128)S(1)}, f32[1,128]{1,0:T(1,128)S(1)}, u32[]{:S(2)}, u32[]{:S(2)}) collective-permute-start(f32[1,128]{1,0:T(1,128)S(1)} %add.62), channel_id=1, source_target_pairs={{0,16},{4,20},{8,24},{12,28},{16,0},{20,4},{24,8},{28,12},{1,17},{... | collective-permute-start | bytes 1544 | tf_op jit(solution)/shard_map/ppermute | solution.py:436
  160.6 0.9 collective-permute-done.26
  (126 shorter events, 14.3 us)
Async XLA Ops:
  4.5 14.9 %collective-permute-start = (f32[1032,128]{1,0:T(8,128)S(1)}, f32[1032,128]{1,0:T(8,128)S(1)}, u32[]{:S(2)}, u32[]{:S(2)}) collective-permute-start(f32[1032,128]{1,0:T(8,128)S(1)} %select_maximum_fusion.refs_3_.refs_0_), channel_id=1, source_target_pairs={{0,1},{7,6},{8,9},{15,14},{16,17},{23,22},{24,25},{31,30}} | collective-permute-start | bytes 1585160 | tf_op jit(solution)/shard_map/ppermute | solution.py:343
  9.6 11.9 %collective-permute-start.1 = (f32[1032,128]{1,0:T(8,128)S(1)}, f32[1032,128]{1,0:T(8,128)S(1)}, u32[]{:S(2)}, u32[]{:S(2)}) collective-permute-start(f32[1032,128]{1,0:T(8,128)S(1)} %select_maximum_fusion.refs_3_.refs_0_), channel_id=1, source_target_pairs={{2,1},{5,6},{10,9},{13,14},{18,17},{21,22},{26,25},{29,30}} | collective-permute-start | bytes 1585160 | tf_op jit(solution)/shard_map/ppermute | solution.py:343
  10.3 11.2 %collective-permute-start.2 = (f32[1032,128]{1,0:T(8,128)S(1)}, f32[1032,128]{1,0:T(8,128)S(1)}, u32[]{:S(2)}, u32[]{:S(2)}) collective-permute-start(f32[1032,128]{1,0:T(8,128)S(1)} %select_maximum_fusion.refs_3_.refs_0_), channel_id=1, source_target_pairs={{3,1},{4,6},{11,9},{12,14},{19,17},{20,22},{27,25},{28,30}} | collective-permute-start | bytes 1585160 | tf_op jit(solution)/shard_map/ppermute | solution.py:343
  13.2 28.7 %collective-permute-start.3 = (f32[2048,128]{1,0:T(8,128)S(1)}, f32[2048,128]{1,0:T(8,128)}, u32[]{:S(2)}, u32[]{:S(2)}) collective-permute-start(f32[2048,128]{1,0:T(8,128)S(1)} %bitcast.26), channel_id=1, source_target_pairs={{0,1},{7,6},{8,9},{15,14},{16,17},{23,22},{24,25},{31,30}} | collective-permute-start | bytes 3145736 | tf_op jit(solution)/shard_map/ppermute | solution.py:343
  16.7 25.9 %collective-permute-start.4 = (f32[2048,128]{1,0:T(8,128)S(1)}, f32[2048,128]{1,0:T(8,128)}, u32[]{:S(2)}, u32[]{:S(2)}) collective-permute-start(f32[2048,128]{1,0:T(8,128)S(1)} %bitcast.27), channel_id=1, source_target_pairs={{2,1},{5,6},{10,9},{13,14},{18,17},{21,22},{26,25},{29,30}} | collective-permute-start | bytes 3145736 | tf_op jit(solution)/shard_map/ppermute | solution.py:343
  19.4 50.1 %copy-start.12 = (f32[1032,128]{1,0:T(8,128)}, f32[1032,128]{1,0:T(8,128)S(1)}, u32[]{:S(2)}) copy-start(f32[1032,128]{1,0:T(8,128)S(1)} %collective-permute-done.refs_4_.refs_1_) | copy-start | bytes 1585156
  19.4 23.2 %collective-permute-start.5 = (f32[2048,128]{1,0:T(8,128)S(1)}, f32[2048,128]{1,0:T(8,128)S(1)}, u32[]{:S(2)}, u32[]{:S(2)}) collective-permute-start(f32[2048,128]{1,0:T(8,128)S(1)} %bitcast.28), channel_id=1, source_target_pairs={{3,1},{4,6},{11,9},{12,14},{19,17},{20,22},{27,25},{28,30}} | collective-permute-start | bytes 3145736 | tf_op jit(solution)/shard_map/ppermute | solution.py:343
  21.4 52.1 %copy-start.1 = (f32[2,1024,128]{2,1,0:T(8,128)}, f32[2,1024,128]{2,1,0:T(8,128)S(1)}, u32[]{:S(2)}) copy-start(f32[2,1024,128]{2,1,0:T(8,128)S(1)} %pad_maximum_fusion.2) | copy-start | bytes 3145732
  21.5 48.1 %copy-start.13 = (f32[1032,128]{1,0:T(8,128)}, f32[1032,128]{1,0:T(8,128)S(1)}, u32[]{:S(2)}) copy-start(f32[1032,128]{1,0:T(8,128)S(1)} %collective-permute-done.1.refs_5_.refs_2_) | copy-start | bytes 1585156
  21.5 48.1 %copy-start.14 = (f32[1032,128]{1,0:T(8,128)}, f32[1032,128]{1,0:T(8,128)S(1)}, u32[]{:S(2)}) copy-start(f32[1032,128]{1,0:T(8,128)S(1)} %collective-permute-done.2.refs_6_.refs_3_) | copy-start | bytes 1585156
  25.0 39.3 %collective-permute-start.12 = (f32[2048,128]{1,0:T(8,128)S(1)}, f32[2048,128]{1,0:T(8,128)S(1)}, u32[]{:S(2)}, u32[]{:S(2)}) collective-permute-start(f32[2048,128]{1,0:T(8,128)S(1)} %bitcast.31), channel_id=1, source_target_pairs={{0,1},{7,6},{8,9},{15,14},{16,17},{23,22},{24,25},{31,30}} | collective-permute-start | bytes 3145736 | tf_op jit(solution)/shard_map/ppermute | solution.py:343
  33.5 56.6 %copy-start.2 = (f32[2,1024,128]{2,1,0:T(8,128)}, f32[2,1024,128]{2,1,0:T(8,128)S(1)}, u32[]{:S(2)}) copy-start(f32[2,1024,128]{2,1,0:T(8,128)S(1)} %pad_maximum_fusion.1) | copy-start | bytes 3145732
  33.6 36.1 %collective-permute-start.13 = (f32[2048,128]{1,0:T(8,128)S(1)}, f32[2048,128]{1,0:T(8,128)S(1)}, u32[]{:S(2)}, u32[]{:S(2)}) collective-permute-start(f32[2048,128]{1,0:T(8,128)S(1)} %bitcast.32), channel_id=1, source_target_pairs={{2,1},{5,6},{10,9},{13,14},{18,17},{21,22},{26,25},{29,30}} | collective-permute-start | bytes 3145736 | tf_op jit(solution)/shard_map/ppermute | solution.py:343
  41.9 30.7 %collective-permute-start.14 = (f32[2048,128]{1,0:T(8,128)S(1)}, f32[2048,128]{1,0:T(8,128)S(1)}, u32[]{:S(2)}, u32[]{:S(2)}) collective-permute-start(f32[2048,128]{1,0:T(8,128)S(1)} %bitcast.33), channel_id=1, source_target_pairs={{3,1},{4,6},{11,9},{12,14},{19,17},{20,22},{27,25},{28,30}} | collective-permute-start | bytes 3145736 | tf_op jit(solution)/shard_map/ppermute | solution.py:343
  56.8 29.6 %collective-permute-start.10 = (f32[2048,128]{1,0:T(8,128)S(1)}, f32[2048,128]{1,0:T(8,128)S(1)}, u32[]{:S(2)}, u32[]{:S(2)}) collective-permute-start(f32[2048,128]{1,0:T(8,128)S(1)} %bitcast.36), channel_id=1, source_target_pairs={{2,1},{5,6},{10,9},{13,14},{18,17},{21,22},{26,25},{29,30}} | collective-permute-start | bytes 3145736 | tf_op jit(solution)/shard_map/ppermute | solution.py:343
  57.5 29.6 %collective-permute-start.11 = (f32[2048,128]{1,0:T(8,128)S(1)}, f32[2048,128]{1,0:T(8,128)S(1)}, u32[]{:S(2)}, u32[]{:S(2)}) collective-permute-start(f32[2048,128]{1,0:T(8,128)S(1)} %bitcast.37), channel_id=1, source_target_pairs={{3,1},{4,6},{11,9},{12,14},{19,17},{20,22},{27,25},{28,30}} | collective-permute-start | bytes 3145736 | tf_op jit(solution)/shard_map/ppermute | solution.py:343
  64.4 25.8 %collective-permute-start.9 = (f32[2048,128]{1,0:T(8,128)S(1)}, f32[2048,128]{1,0:T(8,128)S(1)}, u32[]{:S(2)}, u32[]{:S(2)}) collective-permute-start(f32[2048,128]{1,0:T(8,128)S(1)} %bitcast.38), channel_id=1, source_target_pairs={{0,1},{7,6},{8,9},{15,14},{16,17},{23,22},{24,25},{31,30}} | collective-permute-start | bytes 3145736 | tf_op jit(solution)/shard_map/ppermute | solution.py:343
  69.7 33.3 %collective-permute-start.6 = (f32[1024,128]{1,0:T(8,128)S(1)}, f32[1024,128]{1,0:T(8,128)S(1)}, u32[]{:S(2)}, u32[]{:S(2)}) collective-permute-start(f32[1024,128]{1,0:T(8,128)S(1)} %maximum_bitcast_fusion.1.refs_3_.refs_12_), channel_id=1, source_target_pairs={{0,1},{7,6},{8,9},{15,14},{16,17},{23,22},{24,25},{31,30}} | collective-permute-start | bytes 1572872 | tf_op jit(solution)/shard_map/ppermute | solution.py:343
  72.6 30.3 %collective-permute-start.7 = (f32[1024,128]{1,0:T(8,128)S(1)}, f32[1024,128]{1,0:T(8,128)S(1)}, u32[]{:S(2)}, u32[]{:S(2)}) collective-permute-start(f32[1024,128]{1,0:T(8,128)S(1)} %maximum_bitcast_fusion.1.refs_3_.refs_12_), channel_id=1, source_target_pairs={{2,1},{5,6},{10,9},{13,14},{18,17},{21,22},{26,25},{29,30}} | collective-permute-start | bytes 1572872 | tf_op jit(solution)/shard_map/ppermute | solution.py:343
  86.4 16.6 %collective-permute-start.8 = (f32[1024,128]{1,0:T(8,128)S(1)}, f32[1024,128]{1,0:T(8,128)S(1)}, u32[]{:S(2)}, u32[]{:S(2)}) collective-permute-start(f32[1024,128]{1,0:T(8,128)S(1)} %maximum_bitcast_fusion.1.refs_3_.refs_12_), channel_id=1, source_target_pairs={{3,1},{4,6},{11,9},{12,14},{19,17},{20,22},{27,25},{28,30}} | collective-permute-start | bytes 1572872 | tf_op jit(solution)/shard_map/ppermute | solution.py:343
  110.3 0.7 collective-permute-start.15
  111.4 0.7 collective-permute-start.16
  112.4 0.7 collective-permute-start.17
  113.5 0.9 collective-permute-start.18
  114.7 0.7 collective-permute-start.19
  115.8 0.7 collective-permute-start.20
  116.8 3.6 %collective-permute-start.21 = (f32[8,128]{1,0:T(8,128)S(1)}, f32[8,128]{1,0:T(8,128)S(1)}, u32[]{:S(2)}, u32[]{:S(2)}) collective-permute-start(f32[8,128]{1,0:T(8,128)S(1)} %hop.13.refs_8_), channel_id=1, source_target_pairs={{25,30}} | collective-permute-start | bytes 12296 | tf_op jit(solution)/shard_map/ppermute | solution.py:400
  125.8 0.7 collective-permute-start.22
  126.5 11.9 %collective-permute-start.23 = (f32[1,17,128]{2,1,0:T(8,128)S(1)}, f32[1,17,128]{2,1,0:T(8,128)S(1)}, u32[]{:S(2)}, u32[]{:S(2)}) collective-permute-start(f32[1,17,128]{2,1,0:T(8,128)S(1)} %slice.93), channel_id=1, source_target_pairs={{1,0},{2,3},{6,7},{5,4},{9,8},{10,11},{14,15},{13,12},{17,16},{18,... | collective-permute-start | bytes 26120 | tf_op jit(solution)/shard_map/ppermute | solution.py:426
  138.5 2.8 %collective-permute-start.24 = (f32[1,128]{1,0:T(1,128)S(1)}, f32[1,128]{1,0:T(1,128)S(1)}, u32[]{:S(2)}, u32[]{:S(2)}) collective-permute-start(f32[1,128]{1,0:T(1,128)S(1)} %fusion.1), channel_id=1, source_target_pairs={{0,4},{4,0},{8,12},{12,8},{16,20},{20,16},{24,28},{28,24},{1,5},{5... | collective-permute-start | bytes 1544 | tf_op jit(solution)/shard_map/ppermute | solution.py:436
  141.3 8.3 %collective-permute-start.25 = (f32[1,128]{1,0:T(1,128)S(1)}, f32[1,128]{1,0:T(1,128)S(1)}, u32[]{:S(2)}, u32[]{:S(2)}) collective-permute-start(f32[1,128]{1,0:T(1,128)S(1)} %add.61), channel_id=1, source_target_pairs={{0,8},{4,12},{8,0},{12,4},{16,24},{20,28},{24,16},{28,20},{1,9},{5... | collective-permute-start | bytes 1544 | tf_op jit(solution)/shard_map/ppermute | solution.py:436
  149.6 11.9 %collective-permute-start.26 = (f32[1,128]{1,0:T(1,128)S(1)}, f32[1,128]{1,0:T(1,128)S(1)}, u32[]{:S(2)}, u32[]{:S(2)}) collective-permute-start(f32[1,128]{1,0:T(1,128)S(1)} %add.62), channel_id=1, source_target_pairs={{0,16},{4,20},{8,24},{12,28},{16,0},{20,4},{24,8},{28,12},{1,17},{... | collective-permute-start | bytes 1544 | tf_op jit(solution)/shard_map/ppermute | solution.py:436
  (25 other events, 363.4 us)

commit v7 on v6

--- a/solution.py
+++ b/solution.py
@@ -362,6 +362,7 @@
         if i == 0:
             first = initial_mean.reshape(held, LANES)
             pack = jnp.concatenate([pack, jnp.pad(first, ((0, -held % 8), (0, 0)))])
+            pack, block_values, gains = lax.optimization_barrier((pack, block_values, gains))
         packs.append(pack)
         base += size
 

time: 165 us -> 164 us (level)
    slice x2 -> x4, local copies, waits for them, and re-layouts: 3.45 us -> 2.52 us  [on_device(): blocks = block_values[base:base + size].reshape(size, -1, LANES)]
where the time goes in v7:
time: 164 us; the launch traced here: 163 us
  Pallas kernels  60.8 us (37%)
  starting transfers between devices  58.7 us (36%)
  waiting for transfers between devices  30.7 us (19%)
  local copies, waits for them, and re-layouts  5.78 us (4%)
  between operations  3.97 us (2%)
  other arithmetic  2.9 us (2%)
    pallas_call x5, Pallas kernels, compose(): pl.pallas_call(body, in_specs=[SMEM] * 3 + [VMEM] * (slots + 1 + len(stat...  50 us
    ppermute x15, starting transfers between devices, meet(): moved.append(lax.ppermute(shard, both, pairs))  32.7 us
    ppermute x3, starting transfers between devices, on_device(): lax.ppermute(term, 'tm', [(t, t ^ reach) for t in range(segments)])  19.2 us
    ppermute x15, waiting for transfers between devices, meet(): moved.append(lax.ppermute(shard, both, pairs))  16.8 us
    ppermute x2, waiting for transfers between devices, on_device(): local = local[:half] + lax.ppermute(local[half:], both, pairs)  10.6 us
    pallas_call x1, Pallas kernels, run_segment(): pl.pallas_call(body, in_specs=[SMEM] * 3 + [VMEM] + [HBM] * (slots * len(...  5.35 us
    ppermute x7, starting transfers between devices, on_device(): mean = lax.ppermute(ended, both, pair)  4.85 us
  transfers between devices with their start and end apart: 27, of which 8 were waited for; matrix products, arithmetic and copies ran while one was open for 3% of the time, Pallas kernels for 28%

profile of v7, /device:TPU:0, one launch (start us, length us, event | category | flops | bytes accessed | tf_op | source)
XLA Modules:
  0.0 162.9 jit_solution(6447664127470947929)
XLA Ops:
  0.6 1.2 slice.72
  1.8 0.9 slice.73
  3.5 5.1 %collective-permute-start = (f32[1032,128]{1,0:T(8,128)S(1)}, f32[1032,128]{1,0:T(8,128)S(1)}, u32[]{:S(2)}, u32[]{:S(2)}) collective-permute-start(f32[1032,128]{1,0:T(8,128)S(1)} %select_maximum_fusion.refs_3_.refs_0_), channel_id=1, source_target_pairs={{0,1},{7,6},{8,9},{15,14},{16,17},{23,22},{24,25},{31,30}} | collective-permute-start | bytes 1585160 | tf_op jit(solution)/shard_map/ppermute | solution.py:343
  10.0 1.3 fusion.2
  11.4 0.8 fusion.3
  12.2 3.4 %collective-permute-start.3 = (f32[2048,128]{1,0:T(8,128)S(1)}, f32[2048,128]{1,0:T(8,128)}, u32[]{:S(2)}, u32[]{:S(2)}) collective-permute-start(f32[2048,128]{1,0:T(8,128)S(1)} %bitcast.26), channel_id=1, source_target_pairs={{0,1},{7,6},{8,9},{15,14},{16,17},{23,22},{24,25},{31,30}} | collective-permute-start | bytes 3145736 | tf_op jit(solution)/shard_map/ppermute | solution.py:343
  15.7 1.6 %collective-permute-start.4 = (f32[2048,128]{1,0:T(8,128)S(1)}, f32[2048,128]{1,0:T(8,128)}, u32[]{:S(2)}, u32[]{:S(2)}) collective-permute-start(f32[2048,128]{1,0:T(8,128)S(1)} %bitcast.27), channel_id=1, source_target_pairs={{2,1},{5,6},{10,9},{13,14},{18,17},{21,22},{26,25},{29,30}} | collective-permute-start | bytes 3145736 | tf_op jit(solution)/shard_map/ppermute | solution.py:343
  19.2 1.3 pad_maximum_fusion.2
  20.6 3.4 %compose.5 = (bf16[1024,1152]{1,0:T(8,128)(2,1)S(1)}, bf16[1024,1152]{1,0:T(8,128)(2,1)S(1)}) custom-call(s32[4]{0:T(128)S(1)} %broadcast_select_fusion.refs_0_, s32[8,24]{1,0:T(8,128)S(1)} %copy.27.refs_1_, s32[8,128]{1,0:T(8,128)S(1)} %copy-done.18, f32[1032,128]{1,0:T(8,128)S(1)} %select_maximum_fusion.refs_3_.refs_0_, ...), custom_call_target="tpu_custom_call" | custom-call | flops 3623878656 | bytes 2097152 | tf_op jit(solution)/shard_map/compose/pallas_call | solution.py:130
  24.0 8.4 %collective-permute-start.12 = (f32[2048,128]{1,0:T(8,128)S(1)}, f32[2048,128]{1,0:T(8,128)S(1)}, u32[]{:S(2)}, u32[]{:S(2)}) collective-permute-start(f32[2048,128]{1,0:T(8,128)S(1)} %bitcast.31), channel_id=1, source_target_pairs={{0,1},{7,6},{8,9},{15,14},{16,17},{23,22},{24,25},{31,30}} | collective-permute-start | bytes 3145736 | tf_op jit(solution)/shard_map/ppermute | solution.py:343
  32.6 0.9 collective-permute-start.13
  33.5 7.4 %collective-permute-done.3.refs_4_.refs_5_ = f32[2048,128]{1,0:T(8,128)} collective-permute-done((f32[2048,128]{1,0:T(8,128)S(1)}, f32[2048,128]{1,0:T(8,128)}, u32[]{:S(2)}, u32[]{:S(2)}) %collective-permute-start.3) | collective-permute-done | bytes 1048608 | tf_op jit(solution)/shard_map/ppermute | solution.py:343
  41.7 14.1 %compose.6 = (bf16[1024,1152]{1,0:T(8,128)(2,1)S(1)}, bf16[1024,1152]{1,0:T(8,128)(2,1)S(1)}) custom-call(s32[4]{0:T(128)S(1)} %broadcast_select_fusion.refs_0_, s32[8,24]{1,0:T(8,128)S(1)} %copy.27.refs_1_, s32[8,128]{1,0:T(8,128)S(1)} %copy-done.18, f32[2048,128]{1,0:T(8,128)S(1)} %bitcast.29, ...), custom_call_target="tpu_custom_call", output_to_operand_aliasing={{0}: (8, {}), {1}: (9, {})} | custom-call | flops 7247757312 | bytes 4194304 | tf_op jit(solution)/shard_map/compose/pallas_call | solution.py:130
  57.3 6.1 %collective-permute-done.12.refs_4_.refs_5_ = f32[2048,128]{1,0:T(8,128)S(1)} collective-permute-done((f32[2048,128]{1,0:T(8,128)S(1)}, f32[2048,128]{1,0:T(8,128)S(1)}, u32[]{:S(2)}, u32[]{:S(2)}) %collective-permute-start.12) | collective-permute-done | bytes 1048608 | tf_op jit(solution)/shard_map/ppermute | solution.py:343
  63.4 5.1 %collective-permute-start.9 = (f32[2048,128]{1,0:T(8,128)S(1)}, f32[2048,128]{1,0:T(8,128)S(1)}, u32[]{:S(2)}, u32[]{:S(2)}) collective-permute-start(f32[2048,128]{1,0:T(8,128)S(1)} %bitcast.38), channel_id=1, source_target_pairs={{0,1},{7,6},{8,9},{15,14},{16,17},{23,22},{24,25},{31,30}} | collective-permute-start | bytes 3145736 | tf_op jit(solution)/shard_map/ppermute | solution.py:343
  69.3 2.3 %collective-permute-start.6 = (f32[1024,128]{1,0:T(8,128)S(1)}, f32[1024,128]{1,0:T(8,128)S(1)}, u32[]{:S(2)}, u32[]{:S(2)}) collective-permute-start(f32[1024,128]{1,0:T(8,128)S(1)} %maximum_bitcast_fusion.1.refs_3_.refs_12_), channel_id=1, source_target_pairs={{0,1},{7,6},{8,9},{15,14},{16,17},{23,22},{24,25},{31,30}} | collective-permute-start | bytes 1572872 | tf_op jit(solution)/shard_map/ppermute | solution.py:343
  71.7 0.9 collective-permute-start.7
  72.5 12.8 %compose.7 = (bf16[1024,1152]{1,0:T(8,128)(2,1)S(1)}, bf16[1024,1152]{1,0:T(8,128)(2,1)S(1)}) custom-call(s32[4]{0:T(128)S(1)} %broadcast_select_fusion.refs_0_, s32[8,24]{1,0:T(8,128)S(1)} %copy.27.refs_1_, s32[8,128]{1,0:T(8,128)S(1)} %copy-done.18, f32[2048,128]{1,0:T(8,128)S(1)} %bitcast.34, ...), custom_call_target="tpu_custom_call", output_to_operand_aliasing={{0}: (8, {}), {1}: (9, {})} | custom-call | flops 7247757312 | bytes 4194304 | tf_op jit(solution)/shard_map/compose/pallas_call | solution.py:130
  86.1 3.0 %collective-permute-done.9.refs_4_.refs_9_ = f32[2048,128]{1,0:T(8,128)S(1)} collective-permute-done((f32[2048,128]{1,0:T(8,128)S(1)}, f32[2048,128]{1,0:T(8,128)S(1)}, u32[]{:S(2)}, u32[]{:S(2)}) %collective-permute-start.9) | collective-permute-done | bytes 1048608 | tf_op jit(solution)/shard_map/ppermute | solution.py:343
  89.1 12.8 %compose.8 = (bf16[1024,1152]{1,0:T(8,128)(2,1)S(1)}, bf16[1024,1152]{1,0:T(8,128)(2,1)S(1)}) custom-call(s32[4]{0:T(128)S(1)} %broadcast_select_fusion.refs_0_, s32[8,24]{1,0:T(8,128)S(1)} %copy.27.refs_1_, s32[8,128]{1,0:T(8,128)S(1)} %copy-done.18, f32[2048,128]{1,0:T(8,128)S(1)} %bitcast.39, ...), custom_call_target="tpu_custom_call", output_to_operand_aliasing={{0}: (8, {}), {1}: (9, {})} | custom-call | flops 7247757312 | bytes 4194304 | tf_op jit(solution)/shard_map/compose/pallas_call | solution.py:130
  102.0 6.9 %compose.9 = (bf16[1024,1152]{1,0:T(8,128)(2,1)S(1)}, bf16[1024,1152]{1,0:T(8,128)(2,1)S(1)}, f32[1024,1152]{1,0:T(8,128)S(1)}) custom-call(s32[4]{0:T(128)S(1)} %broadcast_select_fusion.refs_0_, s32[8,24]{1,0:T(8,128)S(1)} %copy.27.refs_1_, s32[8,128]{1,0:T(8,128)S(1)} %copy-done.18, ...), custom_call_target="tpu_custom_call", output_to_operand_aliasing={{0}: (8, {}), {1}: (9, {})} | custom-call | flops 3623878656 | bytes 2097152 | tf_op jit(solution)/shard_map/compose/pallas_call | solution.py:130
  112.5 0.9 collective-permute-start.18
  116.6 2.9 %stage.1.refs_3_ = f32[4,3,1024,128]{3,2,1,0:T(8,128)S(1)} custom-call(f32[1032,128]{1,0:T(8,128)} %copy-done.3, f32[1032,128]{1,0:T(8,128)} %copy-done.12, f32[1032,128]{1,0:T(8,128)} %copy-done.13, f32[1032,128]{1,0:T(8,128)} %copy-done.14, f32[2048,128]{1,0:T(8,128)} %bitcast.30, f32[2048,128]{1,0:T(8,128)} %collective-permute-done.3.refs_4_.refs_5_, ...), custom_call_target="tpu_custom_call" | custom-call | bytes 12582912 | tf_op jit(solution)/shard_map/stage/pallas_call | solution.py:201
  119.5 5.4 %segment.1 = f32[4,17,128]{2,1,0:T(8,128)S(1)} custom-call(s32[4]{0:T(128)S(1)} %broadcast_select_fusion.refs_0_, s32[8,24]{1,0:T(8,128)S(1)} %copy.27.refs_1_, s32[1]{0:T(128)S(6)} %convert_element_type.5.refs_2_, f32[4,3,1024,128]{3,2,1,0:T(8,128)S(1)} %stage.1.refs_3_, f32[2048,128]{1,0:T(8,128)} %bitcast.35, f32[2048,128]{1,0:T(8,128)} %copy-done.6, ...), custom_call_target="tpu_custom_call" | custom-call | tf_op jit(solution)/shard_map/segment/pallas_call | solution.py:258
  125.6 1.3 collective-permute-start.23
  126.9 10.6 %collective-permute-done.23 = f32[1,17,128]{2,1,0:T(8,128)S(1)} collective-permute-done((f32[1,17,128]{2,1,0:T(8,128)S(1)}, f32[1,17,128]{2,1,0:T(8,128)S(1)}, u32[]{:S(2)}, u32[]{:S(2)}) %collective-permute-start.23) | collective-permute-done | bytes 8736 | tf_op jit(solution)/shard_map/ppermute | solution.py:427
  137.5 2.0 %collective-permute-start.24 = (f32[1,128]{1,0:T(1,128)S(1)}, f32[1,128]{1,0:T(1,128)S(1)}, u32[]{:S(2)}, u32[]{:S(2)}) collective-permute-start(f32[1,128]{1,0:T(1,128)S(1)} %fusion.1), channel_id=1, source_target_pairs={{0,4},{4,0},{8,12},{12,8},{16,20},{20,16},{24,28},{28,24},{1,5},{5... | collective-permute-start | bytes 1544 | tf_op jit(solution)/shard_map/ppermute | solution.py:437
  139.5 0.8 collective-permute-done.24
  140.3 6.8 %collective-permute-start.25 = (f32[1,128]{1,0:T(1,128)S(1)}, f32[1,128]{1,0:T(1,128)S(1)}, u32[]{:S(2)}, u32[]{:S(2)}) collective-permute-start(f32[1,128]{1,0:T(1,128)S(1)} %add.61), channel_id=1, source_target_pairs={{0,8},{4,12},{8,0},{12,4},{16,24},{20,28},{24,16},{28,20},{1,9},{5... | collective-permute-start | bytes 1544 | tf_op jit(solution)/shard_map/ppermute | solution.py:437
  147.1 1.5 collective-permute-done.25
  148.6 10.4 %collective-permute-start.26 = (f32[1,128]{1,0:T(1,128)S(1)}, f32[1,128]{1,0:T(1,128)S(1)}, u32[]{:S(2)}, u32[]{:S(2)}) collective-permute-start(f32[1,128]{1,0:T(1,128)S(1)} %add.62), channel_id=1, source_target_pairs={{0,16},{4,20},{8,24},{12,28},{16,0},{20,4},{24,8},{28,12},{1,17},{... | collective-permute-start | bytes 1544 | tf_op jit(solution)/shard_map/ppermute | solution.py:437
  159.6 0.9 collective-permute-done.26
  (125 shorter events, 15.7 us)
Async XLA Ops:
  3.5 14.9 %collective-permute-start = (f32[1032,128]{1,0:T(8,128)S(1)}, f32[1032,128]{1,0:T(8,128)S(1)}, u32[]{:S(2)}, u32[]{:S(2)}) collective-permute-start(f32[1032,128]{1,0:T(8,128)S(1)} %select_maximum_fusion.refs_3_.refs_0_), channel_id=1, source_target_pairs={{0,1},{7,6},{8,9},{15,14},{16,17},{23,22},{24,25},{31,30}} | collective-permute-start | bytes 1585160 | tf_op jit(solution)/shard_map/ppermute | solution.py:343
  8.6 11.9 %collective-permute-start.1 = (f32[1032,128]{1,0:T(8,128)S(1)}, f32[1032,128]{1,0:T(8,128)S(1)}, u32[]{:S(2)}, u32[]{:S(2)}) collective-permute-start(f32[1032,128]{1,0:T(8,128)S(1)} %select_maximum_fusion.refs_3_.refs_0_), channel_id=1, source_target_pairs={{2,1},{5,6},{10,9},{13,14},{18,17},{21,22},{26,25},{29,30}} | collective-permute-start | bytes 1585160 | tf_op jit(solution)/shard_map/ppermute | solution.py:343
  9.3 11.2 %collective-permute-start.2 = (f32[1032,128]{1,0:T(8,128)S(1)}, f32[1032,128]{1,0:T(8,128)S(1)}, u32[]{:S(2)}, u32[]{:S(2)}) collective-permute-start(f32[1032,128]{1,0:T(8,128)S(1)} %select_maximum_fusion.refs_3_.refs_0_), channel_id=1, source_target_pairs={{3,1},{4,6},{11,9},{12,14},{19,17},{20,22},{27,25},{28,30}} | collective-permute-start | bytes 1585160 | tf_op jit(solution)/shard_map/ppermute | solution.py:343
  12.2 28.7 %collective-permute-start.3 = (f32[2048,128]{1,0:T(8,128)S(1)}, f32[2048,128]{1,0:T(8,128)}, u32[]{:S(2)}, u32[]{:S(2)}) collective-permute-start(f32[2048,128]{1,0:T(8,128)S(1)} %bitcast.26), channel_id=1, source_target_pairs={{0,1},{7,6},{8,9},{15,14},{16,17},{23,22},{24,25},{31,30}} | collective-permute-start | bytes 3145736 | tf_op jit(solution)/shard_map/ppermute | solution.py:343
  15.7 25.9 %collective-permute-start.4 = (f32[2048,128]{1,0:T(8,128)S(1)}, f32[2048,128]{1,0:T(8,128)}, u32[]{:S(2)}, u32[]{:S(2)}) collective-permute-start(f32[2048,128]{1,0:T(8,128)S(1)} %bitcast.27), channel_id=1, source_target_pairs={{2,1},{5,6},{10,9},{13,14},{18,17},{21,22},{26,25},{29,30}} | collective-permute-start | bytes 3145736 | tf_op jit(solution)/shard_map/ppermute | solution.py:343
  18.4 50.8 %copy-start.12 = (f32[1032,128]{1,0:T(8,128)}, f32[1032,128]{1,0:T(8,128)S(1)}, u32[]{:S(2)}) copy-start(f32[1032,128]{1,0:T(8,128)S(1)} %collective-permute-done.refs_4_.refs_1_) | copy-start | bytes 1585156
  18.4 23.2 %collective-permute-start.5 = (f32[2048,128]{1,0:T(8,128)S(1)}, f32[2048,128]{1,0:T(8,128)S(1)}, u32[]{:S(2)}, u32[]{:S(2)}) collective-permute-start(f32[2048,128]{1,0:T(8,128)S(1)} %bitcast.28), channel_id=1, source_target_pairs={{3,1},{4,6},{11,9},{12,14},{19,17},{20,22},{27,25},{28,30}} | collective-permute-start | bytes 3145736 | tf_op jit(solution)/shard_map/ppermute | solution.py:343
  20.5 52.1 %copy-start.1 = (f32[2,1024,128]{2,1,0:T(8,128)}, f32[2,1024,128]{2,1,0:T(8,128)S(1)}, u32[]{:S(2)}) copy-start(f32[2,1024,128]{2,1,0:T(8,128)S(1)} %pad_maximum_fusion.2) | copy-start | bytes 3145732
  20.5 48.7 %copy-start.13 = (f32[1032,128]{1,0:T(8,128)}, f32[1032,128]{1,0:T(8,128)S(1)}, u32[]{:S(2)}) copy-start(f32[1032,128]{1,0:T(8,128)S(1)} %collective-permute-done.1.refs_5_.refs_2_) | copy-start | bytes 1585156
  20.5 48.7 %copy-start.14 = (f32[1032,128]{1,0:T(8,128)}, f32[1032,128]{1,0:T(8,128)S(1)}, u32[]{:S(2)}) copy-start(f32[1032,128]{1,0:T(8,128)S(1)} %collective-permute-done.2.refs_6_.refs_3_) | copy-start | bytes 1585156
  24.0 39.3 %collective-permute-start.12 = (f32[2048,128]{1,0:T(8,128)S(1)}, f32[2048,128]{1,0:T(8,128)S(1)}, u32[]{:S(2)}, u32[]{:S(2)}) collective-permute-start(f32[2048,128]{1,0:T(8,128)S(1)} %bitcast.31), channel_id=1, source_target_pairs={{0,1},{7,6},{8,9},{15,14},{16,17},{23,22},{24,25},{31,30}} | collective-permute-start | bytes 3145736 | tf_op jit(solution)/shard_map/ppermute | solution.py:343
  32.6 56.6 %copy-start.2 = (f32[2,1024,128]{2,1,0:T(8,128)}, f32[2,1024,128]{2,1,0:T(8,128)S(1)}, u32[]{:S(2)}) copy-start(f32[2,1024,128]{2,1,0:T(8,128)S(1)} %pad_maximum_fusion.1) | copy-start | bytes 3145732
  32.6 36.7 %collective-permute-start.13 = (f32[2048,128]{1,0:T(8,128)S(1)}, f32[2048,128]{1,0:T(8,128)S(1)}, u32[]{:S(2)}, u32[]{:S(2)}) collective-permute-start(f32[2048,128]{1,0:T(8,128)S(1)} %bitcast.32), channel_id=1, source_target_pairs={{2,1},{5,6},{10,9},{13,14},{18,17},{21,22},{26,25},{29,30}} | collective-permute-start | bytes 3145736 | tf_op jit(solution)/shard_map/ppermute | solution.py:343
  40.9 30.7 %collective-permute-start.14 = (f32[2048,128]{1,0:T(8,128)S(1)}, f32[2048,128]{1,0:T(8,128)S(1)}, u32[]{:S(2)}, u32[]{:S(2)}) collective-permute-start(f32[2048,128]{1,0:T(8,128)S(1)} %bitcast.33), channel_id=1, source_target_pairs={{3,1},{4,6},{11,9},{12,14},{19,17},{20,22},{27,25},{28,30}} | collective-permute-start | bytes 3145736 | tf_op jit(solution)/shard_map/ppermute | solution.py:343
  55.8 29.6 %collective-permute-start.10 = (f32[2048,128]{1,0:T(8,128)S(1)}, f32[2048,128]{1,0:T(8,128)S(1)}, u32[]{:S(2)}, u32[]{:S(2)}) collective-permute-start(f32[2048,128]{1,0:T(8,128)S(1)} %bitcast.36), channel_id=1, source_target_pairs={{2,1},{5,6},{10,9},{13,14},{18,17},{21,22},{26,25},{29,30}} | collective-permute-start | bytes 3145736 | tf_op jit(solution)/shard_map/ppermute | solution.py:343
  56.5 29.6 %collective-permute-start.11 = (f32[2048,128]{1,0:T(8,128)S(1)}, f32[2048,128]{1,0:T(8,128)S(1)}, u32[]{:S(2)}, u32[]{:S(2)}) collective-permute-start(f32[2048,128]{1,0:T(8,128)S(1)} %bitcast.37), channel_id=1, source_target_pairs={{3,1},{4,6},{11,9},{12,14},{19,17},{20,22},{27,25},{28,30}} | collective-permute-start | bytes 3145736 | tf_op jit(solution)/shard_map/ppermute | solution.py:343
  63.4 25.7 %collective-permute-start.9 = (f32[2048,128]{1,0:T(8,128)S(1)}, f32[2048,128]{1,0:T(8,128)S(1)}, u32[]{:S(2)}, u32[]{:S(2)}) collective-permute-start(f32[2048,128]{1,0:T(8,128)S(1)} %bitcast.38), channel_id=1, source_target_pairs={{0,1},{7,6},{8,9},{15,14},{16,17},{23,22},{24,25},{31,30}} | collective-permute-start | bytes 3145736 | tf_op jit(solution)/shard_map/ppermute | solution.py:343
  69.3 32.6 %collective-permute-start.6 = (f32[1024,128]{1,0:T(8,128)S(1)}, f32[1024,128]{1,0:T(8,128)S(1)}, u32[]{:S(2)}, u32[]{:S(2)}) collective-permute-start(f32[1024,128]{1,0:T(8,128)S(1)} %maximum_bitcast_fusion.1.refs_3_.refs_12_), channel_id=1, source_target_pairs={{0,1},{7,6},{8,9},{15,14},{16,17},{23,22},{24,25},{31,30}} | collective-permute-start | bytes 1572872 | tf_op jit(solution)/shard_map/ppermute | solution.py:343
  71.7 30.3 %collective-permute-start.7 = (f32[1024,128]{1,0:T(8,128)S(1)}, f32[1024,128]{1,0:T(8,128)S(1)}, u32[]{:S(2)}, u32[]{:S(2)}) collective-permute-start(f32[1024,128]{1,0:T(8,128)S(1)} %maximum_bitcast_fusion.1.refs_3_.refs_12_), channel_id=1, source_target_pairs={{2,1},{5,6},{10,9},{13,14},{18,17},{21,22},{26,25},{29,30}} | collective-permute-start | bytes 1572872 | tf_op jit(solution)/shard_map/ppermute | solution.py:343
  85.4 16.6 %collective-permute-start.8 = (f32[1024,128]{1,0:T(8,128)S(1)}, f32[1024,128]{1,0:T(8,128)S(1)}, u32[]{:S(2)}, u32[]{:S(2)}) collective-permute-start(f32[1024,128]{1,0:T(8,128)S(1)} %maximum_bitcast_fusion.1.refs_3_.refs_12_), channel_id=1, source_target_pairs={{3,1},{4,6},{11,9},{12,14},{19,17},{20,22},{27,25},{28,30}} | collective-permute-start | bytes 1572872 | tf_op jit(solution)/shard_map/ppermute | solution.py:343
  109.3 0.7 collective-permute-start.15
  110.4 0.7 collective-permute-start.16
  111.4 0.7 collective-permute-start.17
  112.5 0.9 collective-permute-start.18
  113.7 0.7 collective-permute-start.19
  114.8 0.7 collective-permute-start.20
  115.8 3.6 %collective-permute-start.21 = (f32[8,128]{1,0:T(8,128)S(1)}, f32[8,128]{1,0:T(8,128)S(1)}, u32[]{:S(2)}, u32[]{:S(2)}) collective-permute-start(f32[8,128]{1,0:T(8,128)S(1)} %hop.13.refs_8_), channel_id=1, source_target_pairs={{25,30}} | collective-permute-start | bytes 12296 | tf_op jit(solution)/shard_map/ppermute | solution.py:401
  124.8 0.7 collective-permute-start.22
  125.6 11.9 %collective-permute-start.23 = (f32[1,17,128]{2,1,0:T(8,128)S(1)}, f32[1,17,128]{2,1,0:T(8,128)S(1)}, u32[]{:S(2)}, u32[]{:S(2)}) collective-permute-start(f32[1,17,128]{2,1,0:T(8,128)S(1)} %slice.98), channel_id=1, source_target_pairs={{1,0},{2,3},{6,7},{5,4},{9,8},{10,11},{14,15},{13,12},{17,16},{18,... | collective-permute-start | bytes 26120 | tf_op jit(solution)/shard_map/ppermute | solution.py:427
  137.5 2.8 %collective-permute-start.24 = (f32[1,128]{1,0:T(1,128)S(1)}, f32[1,128]{1,0:T(1,128)S(1)}, u32[]{:S(2)}, u32[]{:S(2)}) collective-permute-start(f32[1,128]{1,0:T(1,128)S(1)} %fusion.1), channel_id=1, source_target_pairs={{0,4},{4,0},{8,12},{12,8},{16,20},{20,16},{24,28},{28,24},{1,5},{5... | collective-permute-start | bytes 1544 | tf_op jit(solution)/shard_map/ppermute | solution.py:437
  140.3 8.3 %collective-permute-start.25 = (f32[1,128]{1,0:T(1,128)S(1)}, f32[1,128]{1,0:T(1,128)S(1)}, u32[]{:S(2)}, u32[]{:S(2)}) collective-permute-start(f32[1,128]{1,0:T(1,128)S(1)} %add.61), channel_id=1, source_target_pairs={{0,8},{4,12},{8,0},{12,4},{16,24},{20,28},{24,16},{28,20},{1,9},{5... | collective-permute-start | bytes 1544 | tf_op jit(solution)/shard_map/ppermute | solution.py:437
  148.6 11.9 %collective-permute-start.26 = (f32[1,128]{1,0:T(1,128)S(1)}, f32[1,128]{1,0:T(1,128)S(1)}, u32[]{:S(2)}, u32[]{:S(2)}) collective-permute-start(f32[1,128]{1,0:T(1,128)S(1)} %add.62), channel_id=1, source_target_pairs={{0,16},{4,20},{8,24},{12,28},{16,0},{20,4},{24,8},{28,12},{1,17},{... | collective-permute-start | bytes 1544 | tf_op jit(solution)/shard_map/ppermute | solution.py:437
  (24 other events, 358.7 us)

commit v8 on v7

--- a/solution.py
+++ b/solution.py
@@ -434,8 +434,15 @@
     else:
         reach = 1
         while reach < segments:
-            term = term + lax.ppermute(term, "tm", [(t, t ^ reach) for t in range(segments)])
-            reach *= 2
+            span = 4 if 4 * reach <= segments else 2
+            near = [
+                lax.ppermute(term, "tm", [(t, t ^ (k * reach)) for t in range(segments)])
+                for k in range(1, span)
+            ]
+            term = term + near[0]
+            if span == 4:
+                term = term + (near[1] + near[2])
+            reach *= span
     count = observations.size * segments
     evidence = jnp.sum(term) / count - 0.5 * math.log(2.0 * math.pi)
     return own_filtered, evidence.reshape(1)

time: 164 us -> 164 us (level)
    ppermute x3 -> x4, waiting for transfers between devices: 3.25 us -> 3.87 us  [on_device(): lax.ppermute(term, 'tm', [(t, t ^ k * reach) for t in range(segments)])]
    ppermute x3 -> x4, starting transfers between devices: 19.2 us -> 18.9 us  [on_device(): lax.ppermute(term, 'tm', [(t, t ^ k * reach) for t in range(segments)])]
  transfers between devices with their start and end apart: 27 -> 28, of which waited for: 8 -> 8; matrix products, arithmetic and copies ran while one was open for 3% -> 3% of each run, Pallas kernels for 28% -> 28%
where the time goes in v8:
time: 164 us; the launch traced here: 163 us
  Pallas kernels  60.8 us (37%)
  starting transfers between devices  58.4 us (36%)
  waiting for transfers between devices  31.4 us (19%)
  local copies, waits for them, and re-layouts  5.78 us (4%)
  between operations  3.97 us (2%)
  other arithmetic  2.9 us (2%)
    pallas_call x5, Pallas kernels, compose(): pl.pallas_call(body, in_specs=[SMEM] * 3 + [VMEM] * (slots + 1 + len(stat...  50 us
    ppermute x15, starting transfers between devices, meet(): moved.append(lax.ppermute(shard, both, pairs))  32.7 us
    ppermute x4, starting transfers between devices, on_device(): lax.ppermute(term, 'tm', [(t, t ^ k * reach) for t in range(segments)])  18.9 us
    ppermute x15, waiting for transfers between devices, meet(): moved.append(lax.ppermute(shard, both, pairs))  16.9 us
    ppermute x2, waiting for transfers between devices, on_device(): local = local[:half] + lax.ppermute(local[half:], both, pairs)  10.6 us
    pallas_call x1, Pallas kernels, run_segment(): pl.pallas_call(body, in_specs=[SMEM] * 3 + [VMEM] + [HBM] * (slots * len(...  5.35 us
    ppermute x7, starting transfers between devices, on_device(): mean = lax.ppermute(ended, both, pair)  4.85 us
    ppermute x4, waiting for transfers between devices, on_device(): lax.ppermute(term, 'tm', [(t, t ^ k * reach) for t in range(segments)])  3.87 us
  transfers between devices with their start and end apart: 28, of which 8 were waited for; matrix products, arithmetic and copies ran while one was open for 3% of the time, Pallas kernels for 28%

profile of v8, /device:TPU:0, one launch (start us, length us, event | category | flops | bytes accessed | tf_op | source)
XLA Modules:
  0.0 163.3 jit_solution(3584622499220505346)
XLA Ops:
  0.6 1.2 slice.72
  1.8 0.9 slice.73
  3.5 5.1 %collective-permute-start = (f32[1032,128]{1,0:T(8,128)S(1)}, f32[1032,128]{1,0:T(8,128)S(1)}, u32[]{:S(2)}, u32[]{:S(2)}) collective-permute-start(f32[1032,128]{1,0:T(8,128)S(1)} %select_maximum_fusion.refs_3_.refs_0_), channel_id=1, source_target_pairs={{0,1},{7,6},{8,9},{15,14},{16,17},{23,22},{24,25},{31,30}} | collective-permute-start | bytes 1585160 | tf_op jit(solution)/shard_map/ppermute | solution.py:343
  10.0 1.3 fusion.2
  11.4 0.8 fusion.3
  12.2 3.4 %collective-permute-start.3 = (f32[2048,128]{1,0:T(8,128)S(1)}, f32[2048,128]{1,0:T(8,128)}, u32[]{:S(2)}, u32[]{:S(2)}) collective-permute-start(f32[2048,128]{1,0:T(8,128)S(1)} %bitcast.26), channel_id=1, source_target_pairs={{0,1},{7,6},{8,9},{15,14},{16,17},{23,22},{24,25},{31,30}} | collective-permute-start | bytes 3145736 | tf_op jit(solution)/shard_map/ppermute | solution.py:343
  15.7 1.6 collective-permute-start.4
  19.2 1.3 pad_maximum_fusion.2
  20.6 3.4 %compose.5 = (bf16[1024,1152]{1,0:T(8,128)(2,1)S(1)}, bf16[1024,1152]{1,0:T(8,128)(2,1)S(1)}) custom-call(s32[4]{0:T(128)S(1)} %broadcast_select_fusion.refs_0_, s32[8,24]{1,0:T(8,128)S(1)} %copy.27.refs_1_, s32[8,128]{1,0:T(8,128)S(1)} %copy-done.18, f32[1032,128]{1,0:T(8,128)S(1)} %select_maximum_fusion.refs_3_.refs_0_, ...), custom_call_target="tpu_custom_call" | custom-call | flops 3623878656 | bytes 2097152 | tf_op jit(solution)/shard_map/compose/pallas_call | solution.py:130
  24.0 8.4 %collective-permute-start.12 = (f32[2048,128]{1,0:T(8,128)S(1)}, f32[2048,128]{1,0:T(8,128)S(1)}, u32[]{:S(2)}, u32[]{:S(2)}) collective-permute-start(f32[2048,128]{1,0:T(8,128)S(1)} %bitcast.31), channel_id=1, source_target_pairs={{0,1},{7,6},{8,9},{15,14},{16,17},{23,22},{24,25},{31,30}} | collective-permute-start | bytes 3145736 | tf_op jit(solution)/shard_map/ppermute | solution.py:343
  32.6 0.9 collective-permute-start.13
  33.5 7.4 %collective-permute-done.3.refs_4_.refs_5_ = f32[2048,128]{1,0:T(8,128)} collective-permute-done((f32[2048,128]{1,0:T(8,128)S(1)}, f32[2048,128]{1,0:T(8,128)}, u32[]{:S(2)}, u32[]{:S(2)}) %collective-permute-start.3) | collective-permute-done | bytes 1048608 | tf_op jit(solution)/shard_map/ppermute | solution.py:343
  41.7 14.1 %compose.6 = (bf16[1024,1152]{1,0:T(8,128)(2,1)S(1)}, bf16[1024,1152]{1,0:T(8,128)(2,1)S(1)}) custom-call(s32[4]{0:T(128)S(1)} %broadcast_select_fusion.refs_0_, s32[8,24]{1,0:T(8,128)S(1)} %copy.27.refs_1_, s32[8,128]{1,0:T(8,128)S(1)} %copy-done.18, f32[2048,128]{1,0:T(8,128)S(1)} %bitcast.29, ...), custom_call_target="tpu_custom_call", output_to_operand_aliasing={{0}: (8, {}), {1}: (9, {})} | custom-call | flops 7247757312 | bytes 4194304 | tf_op jit(solution)/shard_map/compose/pallas_call | solution.py:130
  57.3 6.1 %collective-permute-done.12.refs_4_.refs_5_ = f32[2048,128]{1,0:T(8,128)S(1)} collective-permute-done((f32[2048,128]{1,0:T(8,128)S(1)}, f32[2048,128]{1,0:T(8,128)S(1)}, u32[]{:S(2)}, u32[]{:S(2)}) %collective-permute-start.12) | collective-permute-done | bytes 1048608 | tf_op jit(solution)/shard_map/ppermute | solution.py:343
  63.4 5.1 %collective-permute-start.9 = (f32[2048,128]{1,0:T(8,128)S(1)}, f32[2048,128]{1,0:T(8,128)S(1)}, u32[]{:S(2)}, u32[]{:S(2)}) collective-permute-start(f32[2048,128]{1,0:T(8,128)S(1)} %bitcast.38), channel_id=1, source_target_pairs={{0,1},{7,6},{8,9},{15,14},{16,17},{23,22},{24,25},{31,30}} | collective-permute-start | bytes 3145736 | tf_op jit(solution)/shard_map/ppermute | solution.py:343
  69.3 2.3 %collective-permute-start.6 = (f32[1024,128]{1,0:T(8,128)S(1)}, f32[1024,128]{1,0:T(8,128)S(1)}, u32[]{:S(2)}, u32[]{:S(2)}) collective-permute-start(f32[1024,128]{1,0:T(8,128)S(1)} %maximum_bitcast_fusion.1.refs_3_.refs_12_), channel_id=1, source_target_pairs={{0,1},{7,6},{8,9},{15,14},{16,17},{23,22},{24,25},{31,30}} | collective-permute-start | bytes 1572872 | tf_op jit(solution)/shard_map/ppermute | solution.py:343
  71.7 0.9 collective-permute-start.7
  72.5 12.8 %compose.7 = (bf16[1024,1152]{1,0:T(8,128)(2,1)S(1)}, bf16[1024,1152]{1,0:T(8,128)(2,1)S(1)}) custom-call(s32[4]{0:T(128)S(1)} %broadcast_select_fusion.refs_0_, s32[8,24]{1,0:T(8,128)S(1)} %copy.27.refs_1_, s32[8,128]{1,0:T(8,128)S(1)} %copy-done.18, f32[2048,128]{1,0:T(8,128)S(1)} %bitcast.34, ...), custom_call_target="tpu_custom_call", output_to_operand_aliasing={{0}: (8, {}), {1}: (9, {})} | custom-call | flops 7247757312 | bytes 4194304 | tf_op jit(solution)/shard_map/compose/pallas_call | solution.py:130
  86.1 3.0 %collective-permute-done.9.refs_4_.refs_9_ = f32[2048,128]{1,0:T(8,128)S(1)} collective-permute-done((f32[2048,128]{1,0:T(8,128)S(1)}, f32[2048,128]{1,0:T(8,128)S(1)}, u32[]{:S(2)}, u32[]{:S(2)}) %collective-permute-start.9) | collective-permute-done | bytes 1048608 | tf_op jit(solution)/shard_map/ppermute | solution.py:343
  89.1 12.8 %compose.8 = (bf16[1024,1152]{1,0:T(8,128)(2,1)S(1)}, bf16[1024,1152]{1,0:T(8,128)(2,1)S(1)}) custom-call(s32[4]{0:T(128)S(1)} %broadcast_select_fusion.refs_0_, s32[8,24]{1,0:T(8,128)S(1)} %copy.27.refs_1_, s32[8,128]{1,0:T(8,128)S(1)} %copy-done.18, f32[2048,128]{1,0:T(8,128)S(1)} %bitcast.39, ...), custom_call_target="tpu_custom_call", output_to_operand_aliasing={{0}: (8, {}), {1}: (9, {})} | custom-call | flops 7247757312 | bytes 4194304 | tf_op jit(solution)/shard_map/compose/pallas_call | solution.py:130
  102.0 6.9 %compose.9 = (bf16[1024,1152]{1,0:T(8,128)(2,1)S(1)}, bf16[1024,1152]{1,0:T(8,128)(2,1)S(1)}, f32[1024,1152]{1,0:T(8,128)S(1)}) custom-call(s32[4]{0:T(128)S(1)} %broadcast_select_fusion.refs_0_, s32[8,24]{1,0:T(8,128)S(1)} %copy.27.refs_1_, s32[8,128]{1,0:T(8,128)S(1)} %copy-done.18, ...), custom_call_target="tpu_custom_call", output_to_operand_aliasing={{0}: (8, {}), {1}: (9, {})} | custom-call | flops 3623878656 | bytes 2097152 | tf_op jit(solution)/shard_map/compose/pallas_call | solution.py:130
  112.5 0.9 collective-permute-start.18
  116.6 2.9 %stage.1.refs_3_ = f32[4,3,1024,128]{3,2,1,0:T(8,128)S(1)} custom-call(f32[1032,128]{1,0:T(8,128)} %copy-done.3, f32[1032,128]{1,0:T(8,128)} %copy-done.12, f32[1032,128]{1,0:T(8,128)} %copy-done.13, f32[1032,128]{1,0:T(8,128)} %copy-done.14, f32[2048,128]{1,0:T(8,128)} %bitcast.30, f32[2048,128]{1,0:T(8,128)} %collective-permute-done.3.refs_4_.refs_5_, ...), custom_call_target="tpu_custom_call" | custom-call | bytes 12582912 | tf_op jit(solution)/shard_map/stage/pallas_call | solution.py:201
  119.5 5.4 %segment.1 = f32[4,17,128]{2,1,0:T(8,128)S(1)} custom-call(s32[4]{0:T(128)S(1)} %broadcast_select_fusion.refs_0_, s32[8,24]{1,0:T(8,128)S(1)} %copy.27.refs_1_, s32[1]{0:T(128)S(6)} %convert_element_type.5.refs_2_, f32[4,3,1024,128]{3,2,1,0:T(8,128)S(1)} %stage.1.refs_3_, f32[2048,128]{1,0:T(8,128)} %bitcast.35, f32[2048,128]{1,0:T(8,128)} %copy-done.6, ...), custom_call_target="tpu_custom_call" | custom-call | tf_op jit(solution)/shard_map/segment/pallas_call | solution.py:258
  125.6 1.3 collective-permute-start.23
  126.9 10.6 %collective-permute-done.23 = f32[1,17,128]{2,1,0:T(8,128)S(1)} collective-permute-done((f32[1,17,128]{2,1,0:T(8,128)S(1)}, f32[1,17,128]{2,1,0:T(8,128)S(1)}, u32[]{:S(2)}, u32[]{:S(2)}) %collective-permute-start.23) | collective-permute-done | bytes 8736 | tf_op jit(solution)/shard_map/ppermute | solution.py:427
  137.5 2.0 %collective-permute-start.24 = (f32[1,128]{1,0:T(1,128)S(1)}, f32[1,128]{1,0:T(1,128)S(1)}, u32[]{:S(2)}, u32[]{:S(2)}) collective-permute-start(f32[1,128]{1,0:T(1,128)S(1)} %fusion.1), channel_id=1, source_target_pairs={{0,4},{4,0},{8,12},{12,8},{16,20},{20,16},{24,28},{28,24},{1,5},{5... | collective-permute-start | bytes 1544 | tf_op jit(solution)/shard_map/ppermute | solution.py:439
  139.5 6.8 %collective-permute-start.25 = (f32[1,128]{1,0:T(1,128)S(1)}, f32[1,128]{1,0:T(1,128)S(1)}, u32[]{:S(2)}, u32[]{:S(2)}) collective-permute-start(f32[1,128]{1,0:T(1,128)S(1)} %fusion.1), channel_id=1, source_target_pairs={{0,8},{4,12},{8,0},{12,4},{16,24},{20,28},{24,16},{28,20},{1,9},{5... | collective-permute-start | bytes 1544 | tf_op jit(solution)/shard_map/ppermute | solution.py:439
  146.3 1.5 collective-permute-done.25
  147.8 1.4 collective-permute-done.26
  149.2 10.2 %collective-permute-start.27 = (f32[1,128]{1,0:T(1,128)S(1)}, f32[1,128]{1,0:T(1,128)S(1)}, u32[]{:S(2)}, u32[]{:S(2)}) collective-permute-start(f32[1,128]{1,0:T(1,128)S(1)} %add_add_fusion.1), channel_id=1, source_target_pairs={{0,16},{4,20},{8,24},{12,28},{16,0},{20,4},{24,8},{28,12},{1,17},{... | collective-permute-start | bytes 1544 | tf_op jit(solution)/shard_map/ppermute | solution.py:439
  160.0 0.9 collective-permute-done.27
  (126 shorter events, 15.7 us)
Async XLA Ops:
  3.5 14.9 %collective-permute-start = (f32[1032,128]{1,0:T(8,128)S(1)}, f32[1032,128]{1,0:T(8,128)S(1)}, u32[]{:S(2)}, u32[]{:S(2)}) collective-permute-start(f32[1032,128]{1,0:T(8,128)S(1)} %select_maximum_fusion.refs_3_.refs_0_), channel_id=1, source_target_pairs={{0,1},{7,6},{8,9},{15,14},{16,17},{23,22},{24,25},{31,30}} | collective-permute-start | bytes 1585160 | tf_op jit(solution)/shard_map/ppermute | solution.py:343
  8.6 11.9 %collective-permute-start.1 = (f32[1032,128]{1,0:T(8,128)S(1)}, f32[1032,128]{1,0:T(8,128)S(1)}, u32[]{:S(2)}, u32[]{:S(2)}) collective-permute-start(f32[1032,128]{1,0:T(8,128)S(1)} %select_maximum_fusion.refs_3_.refs_0_), channel_id=1, source_target_pairs={{2,1},{5,6},{10,9},{13,14},{18,17},{21,22},{26,25},{29,30}} | collective-permute-start | bytes 1585160 | tf_op jit(solution)/shard_map/ppermute | solution.py:343
  9.3 11.2 %collective-permute-start.2 = (f32[1032,128]{1,0:T(8,128)S(1)}, f32[1032,128]{1,0:T(8,128)S(1)}, u32[]{:S(2)}, u32[]{:S(2)}) collective-permute-start(f32[1032,128]{1,0:T(8,128)S(1)} %select_maximum_fusion.refs_3_.refs_0_), channel_id=1, source_target_pairs={{3,1},{4,6},{11,9},{12,14},{19,17},{20,22},{27,25},{28,30}} | collective-permute-start | bytes 1585160 | tf_op jit(solution)/shard_map/ppermute | solution.py:343
  12.2 28.7 %collective-permute-start.3 = (f32[2048,128]{1,0:T(8,128)S(1)}, f32[2048,128]{1,0:T(8,128)}, u32[]{:S(2)}, u32[]{:S(2)}) collective-permute-start(f32[2048,128]{1,0:T(8,128)S(1)} %bitcast.26), channel_id=1, source_target_pairs={{0,1},{7,6},{8,9},{15,14},{16,17},{23,22},{24,25},{31,30}} | collective-permute-start | bytes 3145736 | tf_op jit(solution)/shard_map/ppermute | solution.py:343
  15.7 25.9 %collective-permute-start.4 = (f32[2048,128]{1,0:T(8,128)S(1)}, f32[2048,128]{1,0:T(8,128)}, u32[]{:S(2)}, u32[]{:S(2)}) collective-permute-start(f32[2048,128]{1,0:T(8,128)S(1)} %bitcast.27), channel_id=1, source_target_pairs={{2,1},{5,6},{10,9},{13,14},{18,17},{21,22},{26,25},{29,30}} | collective-permute-start | bytes 3145736 | tf_op jit(solution)/shard_map/ppermute | solution.py:343
  18.4 50.8 %copy-start.12 = (f32[1032,128]{1,0:T(8,128)}, f32[1032,128]{1,0:T(8,128)S(1)}, u32[]{:S(2)}) copy-start(f32[1032,128]{1,0:T(8,128)S(1)} %collective-permute-done.refs_4_.refs_1_) | copy-start | bytes 1585156
  18.4 23.2 %collective-permute-start.5 = (f32[2048,128]{1,0:T(8,128)S(1)}, f32[2048,128]{1,0:T(8,128)S(1)}, u32[]{:S(2)}, u32[]{:S(2)}) collective-permute-start(f32[2048,128]{1,0:T(8,128)S(1)} %bitcast.28), channel_id=1, source_target_pairs={{3,1},{4,6},{11,9},{12,14},{19,17},{20,22},{27,25},{28,30}} | collective-permute-start | bytes 3145736 | tf_op jit(solution)/shard_map/ppermute | solution.py:343
  20.5 52.1 %copy-start.1 = (f32[2,1024,128]{2,1,0:T(8,128)}, f32[2,1024,128]{2,1,0:T(8,128)S(1)}, u32[]{:S(2)}) copy-start(f32[2,1024,128]{2,1,0:T(8,128)S(1)} %pad_maximum_fusion.2) | copy-start | bytes 3145732
  20.5 48.8 %copy-start.13 = (f32[1032,128]{1,0:T(8,128)}, f32[1032,128]{1,0:T(8,128)S(1)}, u32[]{:S(2)}) copy-start(f32[1032,128]{1,0:T(8,128)S(1)} %collective-permute-done.1.refs_5_.refs_2_) | copy-start | bytes 1585156
  24.0 39.3 %collective-permute-start.12 = (f32[2048,128]{1,0:T(8,128)S(1)}, f32[2048,128]{1,0:T(8,128)S(1)}, u32[]{:S(2)}, u32[]{:S(2)}) collective-permute-start(f32[2048,128]{1,0:T(8,128)S(1)} %bitcast.31), channel_id=1, source_target_pairs={{0,1},{7,6},{8,9},{15,14},{16,17},{23,22},{24,25},{31,30}} | collective-permute-start | bytes 3145736 | tf_op jit(solution)/shard_map/ppermute | solution.py:343
  32.6 56.6 %copy-start.2 = (f32[2,1024,128]{2,1,0:T(8,128)}, f32[2,1024,128]{2,1,0:T(8,128)S(1)}, u32[]{:S(2)}) copy-start(f32[2,1024,128]{2,1,0:T(8,128)S(1)} %pad_maximum_fusion.1) | copy-start | bytes 3145732
  32.6 36.7 %collective-permute-start.13 = (f32[2048,128]{1,0:T(8,128)S(1)}, f32[2048,128]{1,0:T(8,128)S(1)}, u32[]{:S(2)}, u32[]{:S(2)}) collective-permute-start(f32[2048,128]{1,0:T(8,128)S(1)} %bitcast.32), channel_id=1, source_target_pairs={{2,1},{5,6},{10,9},{13,14},{18,17},{21,22},{26,25},{29,30}} | collective-permute-start | bytes 3145736 | tf_op jit(solution)/shard_map/ppermute | solution.py:343
  40.9 30.7 %collective-permute-start.14 = (f32[2048,128]{1,0:T(8,128)S(1)}, f32[2048,128]{1,0:T(8,128)S(1)}, u32[]{:S(2)}, u32[]{:S(2)}) collective-permute-start(f32[2048,128]{1,0:T(8,128)S(1)} %bitcast.33), channel_id=1, source_target_pairs={{3,1},{4,6},{11,9},{12,14},{19,17},{20,22},{27,25},{28,30}} | collective-permute-start | bytes 3145736 | tf_op jit(solution)/shard_map/ppermute | solution.py:343
  55.8 29.6 %collective-permute-start.10 = (f32[2048,128]{1,0:T(8,128)S(1)}, f32[2048,128]{1,0:T(8,128)S(1)}, u32[]{:S(2)}, u32[]{:S(2)}) collective-permute-start(f32[2048,128]{1,0:T(8,128)S(1)} %bitcast.36), channel_id=1, source_target_pairs={{2,1},{5,6},{10,9},{13,14},{18,17},{21,22},{26,25},{29,30}} | collective-permute-start | bytes 3145736 | tf_op jit(solution)/shard_map/ppermute | solution.py:343
  56.5 29.6 %collective-permute-start.11 = (f32[2048,128]{1,0:T(8,128)S(1)}, f32[2048,128]{1,0:T(8,128)S(1)}, u32[]{:S(2)}, u32[]{:S(2)}) collective-permute-start(f32[2048,128]{1,0:T(8,128)S(1)} %bitcast.37), channel_id=1, source_target_pairs={{3,1},{4,6},{11,9},{12,14},{19,17},{20,22},{27,25},{28,30}} | collective-permute-start | bytes 3145736 | tf_op jit(solution)/shard_map/ppermute | solution.py:343
  63.4 25.7 %collective-permute-start.9 = (f32[2048,128]{1,0:T(8,128)S(1)}, f32[2048,128]{1,0:T(8,128)S(1)}, u32[]{:S(2)}, u32[]{:S(2)}) collective-permute-start(f32[2048,128]{1,0:T(8,128)S(1)} %bitcast.38), channel_id=1, source_target_pairs={{0,1},{7,6},{8,9},{15,14},{16,17},{23,22},{24,25},{31,30}} | collective-permute-start | bytes 3145736 | tf_op jit(solution)/shard_map/ppermute | solution.py:343
  69.3 32.6 %collective-permute-start.6 = (f32[1024,128]{1,0:T(8,128)S(1)}, f32[1024,128]{1,0:T(8,128)S(1)}, u32[]{:S(2)}, u32[]{:S(2)}) collective-permute-start(f32[1024,128]{1,0:T(8,128)S(1)} %maximum_bitcast_fusion.1.refs_3_.refs_12_), channel_id=1, source_target_pairs={{0,1},{7,6},{8,9},{15,14},{16,17},{23,22},{24,25},{31,30}} | collective-permute-start | bytes 1572872 | tf_op jit(solution)/shard_map/ppermute | solution.py:343
  71.7 30.3 %collective-permute-start.7 = (f32[1024,128]{1,0:T(8,128)S(1)}, f32[1024,128]{1,0:T(8,128)S(1)}, u32[]{:S(2)}, u32[]{:S(2)}) collective-permute-start(f32[1024,128]{1,0:T(8,128)S(1)} %maximum_bitcast_fusion.1.refs_3_.refs_12_), channel_id=1, source_target_pairs={{2,1},{5,6},{10,9},{13,14},{18,17},{21,22},{26,25},{29,30}} | collective-permute-start | bytes 1572872 | tf_op jit(solution)/shard_map/ppermute | solution.py:343
  85.4 16.6 %collective-permute-start.8 = (f32[1024,128]{1,0:T(8,128)S(1)}, f32[1024,128]{1,0:T(8,128)S(1)}, u32[]{:S(2)}, u32[]{:S(2)}) collective-permute-start(f32[1024,128]{1,0:T(8,128)S(1)} %maximum_bitcast_fusion.1.refs_3_.refs_12_), channel_id=1, source_target_pairs={{3,1},{4,6},{11,9},{12,14},{19,17},{20,22},{27,25},{28,30}} | collective-permute-start | bytes 1572872 | tf_op jit(solution)/shard_map/ppermute | solution.py:343
  109.3 0.7 collective-permute-start.15
  110.4 0.7 collective-permute-start.16
  111.4 0.7 collective-permute-start.17
  112.5 0.9 collective-permute-start.18
  113.7 0.7 collective-permute-start.19
  114.8 0.7 collective-permute-start.20
  115.8 3.6 %collective-permute-start.21 = (f32[8,128]{1,0:T(8,128)S(1)}, f32[8,128]{1,0:T(8,128)S(1)}, u32[]{:S(2)}, u32[]{:S(2)}) collective-permute-start(f32[8,128]{1,0:T(8,128)S(1)} %hop.13.refs_8_), channel_id=1, source_target_pairs={{25,30}} | collective-permute-start | bytes 12296 | tf_op jit(solution)/shard_map/ppermute | solution.py:401
  124.8 0.7 collective-permute-start.22
  125.6 11.9 %collective-permute-start.23 = (f32[1,17,128]{2,1,0:T(8,128)S(1)}, f32[1,17,128]{2,1,0:T(8,128)S(1)}, u32[]{:S(2)}, u32[]{:S(2)}) collective-permute-start(f32[1,17,128]{2,1,0:T(8,128)S(1)} %slice.98), channel_id=1, source_target_pairs={{1,0},{2,3},{6,7},{5,4},{9,8},{10,11},{14,15},{13,12},{17,16},{18,... | collective-permute-start | bytes 26120 | tf_op jit(solution)/shard_map/ppermute | solution.py:427
  137.5 8.8 %collective-permute-start.24 = (f32[1,128]{1,0:T(1,128)S(1)}, f32[1,128]{1,0:T(1,128)S(1)}, u32[]{:S(2)}, u32[]{:S(2)}) collective-permute-start(f32[1,128]{1,0:T(1,128)S(1)} %fusion.1), channel_id=1, source_target_pairs={{0,4},{4,0},{8,12},{12,8},{16,20},{20,16},{24,28},{28,24},{1,5},{5... | collective-permute-start | bytes 1544 | tf_op jit(solution)/shard_map/ppermute | solution.py:439
  139.5 8.3 %collective-permute-start.25 = (f32[1,128]{1,0:T(1,128)S(1)}, f32[1,128]{1,0:T(1,128)S(1)}, u32[]{:S(2)}, u32[]{:S(2)}) collective-permute-start(f32[1,128]{1,0:T(1,128)S(1)} %fusion.1), channel_id=1, source_target_pairs={{0,8},{4,12},{8,0},{12,4},{16,24},{20,28},{24,16},{28,20},{1,9},{5... | collective-permute-start | bytes 1544 | tf_op jit(solution)/shard_map/ppermute | solution.py:439
  146.3 3.0 %collective-permute-start.26 = (f32[1,128]{1,0:T(1,128)S(1)}, f32[1,128]{1,0:T(1,128)S(1)}, u32[]{:S(2)}, u32[]{:S(2)}) collective-permute-start(f32[1,128]{1,0:T(1,128)S(1)} %fusion.1), channel_id=1, source_target_pairs={{0,12},{4,8},{8,4},{12,0},{16,28},{20,24},{24,20},{28,16},{1,13},{... | collective-permute-start | bytes 1544 | tf_op jit(solution)/shard_map/ppermute | solution.py:439
  149.2 11.7 %collective-permute-start.27 = (f32[1,128]{1,0:T(1,128)S(1)}, f32[1,128]{1,0:T(1,128)S(1)}, u32[]{:S(2)}, u32[]{:S(2)}) collective-permute-start(f32[1,128]{1,0:T(1,128)S(1)} %add_add_fusion.1), channel_id=1, source_target_pairs={{0,16},{4,20},{8,24},{12,28},{16,0},{20,4},{24,8},{28,12},{1,17},{... | collective-permute-start | bytes 1544 | tf_op jit(solution)/shard_map/ppermute | solution.py:439
  (25 other events, 407.4 us)
